TPU v7x, 32 devices: a whole 2x2x4 slice. The times are simulated.
32 devices in a mesh: ka: 16 (over z, x, core), ga: 2 (over y).
Axes of the slice: x: 2, y: 2, z: 4, core: 2. Of those that a mesh axis runs over, the one named last changes fastest.
Arguments:
- pair_density: bfloat16 [256, 64, 4096], P('ka', None, 'ga'), may hold values from -0.1875 to 0.1875
- trial_vectors: bfloat16 [256, 64, 128], P('ka'), may hold values from -6 to 6
- energy: float32 [256, 64], P('ka'), may hold values from 0.5 to 2.5
- coulomb: float32 [4096], P('ga'), may hold values from 0.03 to 0.3
- screen: bfloat16 [32, 4096, 256], P(None, 'ga'), may hold values from -0.375 to 0.375
- neighbors: int32 [256, 16], P('ka'), may hold values from 0 to 255, as said below
- live_count: int32 [256], P('ka'), may hold values from 1 to 16, as said below
- q_index: int32 [256, 16], P('ka'), may hold values from 0 to 31
Outputs:
- applied: bfloat16 [256, 64, 128], P('ka', 'ga')
Inputs may be any that keep to these rules, and one draw needn't show every extreme that they name: `neighbors`: the 16 partners of k-point k are distinct k-points whose block k' // 16 is the block of k or one of its two neighbours on the closed cycle of 16 blocks. Only the first live_count[k] slots of row k of neighbors and q_index are used; some k-point uses all 16.
All inputs are finite; a program needn't handle non-finite values.
Results may differ from a plain program's by a relative error of at most 0.013.
Values may be sent and summed in bfloat16 or wider, within the bound.
No kernel may reach another device: no remote copies, remote signals or barrier semaphores. Data moves between devices by JAX's collectives and lax.ppermute only.
A program may use at most 192 MiB of HBM per device.

v0:
```python
import jax
import jax.numpy as jnp
from jax import lax
from jax.sharding import PartitionSpec as P


def passed_along(value, axis, steps):
    count = lax.axis_size(axis)
    pairs = [(source, (source + steps) % count) for source in range(count)]
    return lax.ppermute(value, axis, pairs)


def form_products(density, vectors):
    return jnp.einsum("kpg,kpt->kgt", density, vectors, preferred_element_type=jnp.float32).astype(
        jnp.bfloat16
    )


def on_device(pair_density, trial_vectors, energy, coulomb, screen, neighbors, live_count, q_index):
    local_k, pair_count, local_g = pair_density.shape
    trial_count = trial_vectors.shape[2]
    block_size = screen.shape[2]
    groups = local_g // block_size
    cycle_size = lax.axis_size("ka")
    position = lax.axis_index("ka")
    own_products = form_products(pair_density, trial_vectors)
    below_block = passed_along(own_products, "ka", 1)
    above_block = passed_along(own_products, "ka", -1)
    window = jnp.concatenate([below_block, own_products, above_block], axis=0)
    partial_value = jnp.sum(own_products, axis=0, dtype=jnp.float32)
    density_total = lax.psum(partial_value, "ka")
    screened = coulomb[:, None] * density_total
    offset = (neighbors // local_k - position + 1) % cycle_size
    local_index = offset * local_k + neighbors % local_k

    def add_slot(slot_index, summed):
        picked = jnp.take(window, local_index[:, slot_index], axis=0)
        blocks = jnp.take(screen, q_index[:, slot_index], axis=0)
        coupled = jnp.einsum(
            "kbgc,kbct->kbgt",
            blocks.reshape(local_k, groups, block_size, block_size),
            picked.reshape(local_k, groups, block_size, trial_count),
            preferred_element_type=jnp.float32,
        ).reshape(local_k, local_g, trial_count)
        is_live = (slot_index < live_count)[:, None, None]
        return summed + jnp.where(is_live, coupled, 0.0)

    last_slot = neighbors.shape[1]
    direct = lax.fori_loop(
        0, last_slot, add_slot, jnp.zeros((local_k, local_g, trial_count), jnp.float32)
    )
    kernel = (2.0 * screened[None] - direct).astype(jnp.bfloat16)
    pair_terms = jnp.einsum(
        "kpg,kgt->kpt", pair_density, kernel, preferred_element_type=jnp.float32
    )
    mine = lax.psum_scatter(pair_terms, "ga", scatter_dimension=1, tiled=True)
    row_count = mine.shape[1]
    first_row = lax.axis_index("ga") * row_count
    energy_rows = lax.dynamic_slice_in_dim(energy, first_row, row_count, 1)
    vector_rows = lax.dynamic_slice_in_dim(trial_vectors, first_row, row_count, 1)
    return (energy_rows[:, :, None] * vector_rows.astype(jnp.float32) + mine).astype(jnp.bfloat16)


def solution(mesh):
    in_specs = (
        P("ka", None, "ga"),
        P("ka", None, None),
        P("ka", None),
        P("ga"),
        P(None, "ga", None),
        P("ka", None),
        P("ka"),
        P("ka", None),
    )
    out_specs = P("ka", "ga", None)
    return jax.shard_map(
        on_device, mesh=mesh, in_specs=in_specs, out_specs=out_specs, check_vma=False
    )
```

profile of v0, /device:TPU:1, one launch (start us, length us, event | category | flops | bytes accessed | tf_op | source)
XLA Modules:
  0.0 1170.1 jit_solution(3300030302084759185)
XLA Ops:
  20.4 167.0 %all-reduce.2.cloned.1.call-done = f32[2048,128]{1,0:T(8,128)} async-done(((f32[2048,128]{1,0:T(8,128)}), f32[2048,128]{1,0:T(8,128)}) %all-reduce.2.cloned.1.call-update) | async-done | bytes 1048592 | tf_op jit(solution)/shard_map/psum | solution.py:31
  189.9 17.0 %collective-permute-done = bf16[16,2048,128]{2,1,0:T(8,128)(2,1)} collective-permute-done((bf16[16,2048,128]{2,1,0:T(8,128)(2,1)}, bf16[16,2048,128]{2,1,0:T(8,128)(2,1)}, u32[]{:S(2)}, u32[]{:S(2)}) %collective-permute-start) | collective-permute-done | bytes 8388640 | tf_op jit(solution)/shard_map/ppermute | solution.py:10
  209.4 17.6 %pad_maximum_fusion = bf16[48,2048,128]{2,1,0:T(8,128)(2,1)} fusion(bf16[16,2048,128]{2,1,0:T(8,128)(2,1)} %collective-permute-done.1, bf16[16,2048,128]{2,1,0:T(8,128)(2,1)} %get-tuple-element.182, bf16[16,2048,128]{2,1,0:T(8,128)(2,1)} %collective-permute-done), kind=kLoop, calls=%fused_computation.19 | loop fusion | flops 25165824 | bytes 50331648 | tf_op jit(solution)/shard_map/concatenate | solution.py:29
  227.0 907.7 %while.14 = (s32[]{:T(128)}, f32[16,2048,128]{2,1,0:T(8,128)}, s32[16]{0:T(128)S(1)}, s32[16,16]{0,1:T(8,128)S(1)}, bf16[32,2048,256]{2,1,0:T(8,128)(2,1)}, /*in...) while((s32[]{:T(128)}, f32[16,2048,128]{2,1,0:T(8,128)}, ...), condition=%wide.region_3.4_spmd.clone, body=%wide.region_2.3_spmd.clone.sunk | while | flops 2172651776 | bytes 142615312 | solution.py:49
  251.8 14.0 %fusion.27 = f32[16,8,256,128]{3,2,1,0:T(8,128)} fusion(bf16[16,8,256,256]{3,2,1,0:T(8,128)(2,1)} %bitcast.29, pred[16]{0:T(512)(128)(4,1)S(1)} %get-tuple-element.231, bf16[16,8,256,128]{3,2,1,0:T(8,128)(2,1)} %bitcast.30, pred[16]{0:T(512)(128)(4,1)S(1)} %get-tuple-element.233), kind=kOutput, calls=%fused_computation.4.clone.1 | convolution fusion | flops 2160066560 | bytes 41943072 | tf_op jit(solution)/shard_map/while/body/eval_jaxpr/kbgc,kbct->kbgt/dot_general | solution.py:39
  277.6 13.4 %gather_fusion = bf16[16,2048,256]{2,1,0:T(8,128)(2,1)} fusion(bf16[32,2048,256]{2,1,0:T(8,128)(2,1)} %get-tuple-element.256, s32[1024]{0:T(1024)S(1)} %pad_clamp_fusion.4), kind=kCustom, calls=%fused_computation.clone.clone.1 | custom fusion | bytes 33554496 | tf_op jit(solution)/shard_map/while/body/eval_jaxpr/jit(_take)/gather | solution.py:38
  291.0 13.0 %gather_fusion.1 = bf16[16,2048,128]{2,1,0:T(8,128)(2,1)} fusion(bf16[48,2048,128]{2,1,0:T(8,128)(2,1)} %get-tuple-element.258, s32[1024]{0:T(1024)S(1)} %pad_clamp_fusion.5), kind=kCustom, calls=%fused_computation.1.clone.clone.1 | custom fusion | bytes 16777280 | tf_op jit(solution)/shard_map/while/body/eval_jaxpr/jit(_take)/gather | solution.py:37
  304.0 14.0 %fusion.27 = f32[16,8,256,128]{3,2,1,0:T(8,128)} fusion(bf16[16,8,256,256]{3,2,1,0:T(8,128)(2,1)} %bitcast.29, pred[16]{0:T(512)(128)(4,1)S(1)} %get-tuple-element.231, bf16[16,8,256,128]{3,2,1,0:T(8,128)(2,1)} %bitcast.30, pred[16]{0:T(512)(128)(4,1)S(1)} %get-tuple-element.233), kind=kOutput, calls=%fused_computation.4.clone.1 | convolution fusion | flops 2160066560 | bytes 41943072 | tf_op jit(solution)/shard_map/while/body/eval_jaxpr/kbgc,kbct->kbgt/dot_general | solution.py:39
  318.0 17.8 %fusion.28 = f32[16,2048,128]{2,1,0:T(8,128)} fusion(f32[16,8,256,128]{3,2,1,0:T(8,128)} %fusion.27, f32[16,2048,128]{2,1,0:T(8,128)} %get-tuple-element.244, pred[16]{0:T(512)(128)(4,1)S(1)} %broadcast_compare_fusion.2, pred[]{:T(512)S(6)} %compare.7), kind=kLoop, calls=%fused_computation.3.clone.1 | loop fusion | flops 12582912 | bytes 50331664 | tf_op jit(solution)/shard_map/while/body/eval_jaxpr/add | solution.py:46
  347.7 13.0 %gather_fusion.1 = bf16[16,2048,128]{2,1,0:T(8,128)(2,1)} fusion(bf16[48,2048,128]{2,1,0:T(8,128)(2,1)} %get-tuple-element.258, s32[1024]{0:T(1024)S(1)} %pad_clamp_fusion.5), kind=kCustom, calls=%fused_computation.1.clone.clone.1 | custom fusion | bytes 16777280 | tf_op jit(solution)/shard_map/while/body/eval_jaxpr/jit(_take)/gather | solution.py:37
  360.7 14.0 %fusion.27 = f32[16,8,256,128]{3,2,1,0:T(8,128)} fusion(bf16[16,8,256,256]{3,2,1,0:T(8,128)(2,1)} %bitcast.29, pred[16]{0:T(512)(128)(4,1)S(1)} %get-tuple-element.231, bf16[16,8,256,128]{3,2,1,0:T(8,128)(2,1)} %bitcast.30, pred[16]{0:T(512)(128)(4,1)S(1)} %get-tuple-element.233), kind=kOutput, calls=%fused_computation.4.clone.1 | convolution fusion | flops 2160066560 | bytes 41943072 | tf_op jit(solution)/shard_map/while/body/eval_jaxpr/kbgc,kbct->kbgt/dot_general | solution.py:39
  374.7 17.8 %fusion.28 = f32[16,2048,128]{2,1,0:T(8,128)} fusion(f32[16,8,256,128]{3,2,1,0:T(8,128)} %fusion.27, f32[16,2048,128]{2,1,0:T(8,128)} %get-tuple-element.244, pred[16]{0:T(512)(128)(4,1)S(1)} %broadcast_compare_fusion.2, pred[]{:T(512)S(6)} %compare.7), kind=kLoop, calls=%fused_computation.3.clone.1 | loop fusion | flops 12582912 | bytes 50331664 | tf_op jit(solution)/shard_map/while/body/eval_jaxpr/add | solution.py:46
  405.3 13.0 %gather_fusion.1 = bf16[16,2048,128]{2,1,0:T(8,128)(2,1)} fusion(bf16[48,2048,128]{2,1,0:T(8,128)(2,1)} %get-tuple-element.258, s32[1024]{0:T(1024)S(1)} %pad_clamp_fusion.5), kind=kCustom, calls=%fused_computation.1.clone.clone.1 | custom fusion | bytes 16777280 | tf_op jit(solution)/shard_map/while/body/eval_jaxpr/jit(_take)/gather | solution.py:37
  418.3 14.0 %fusion.27 = f32[16,8,256,128]{3,2,1,0:T(8,128)} fusion(bf16[16,8,256,256]{3,2,1,0:T(8,128)(2,1)} %bitcast.29, pred[16]{0:T(512)(128)(4,1)S(1)} %get-tuple-element.231, bf16[16,8,256,128]{3,2,1,0:T(8,128)(2,1)} %bitcast.30, pred[16]{0:T(512)(128)(4,1)S(1)} %get-tuple-element.233), kind=kOutput, calls=%fused_computation.4.clone.1 | convolution fusion | flops 2160066560 | bytes 41943072 | tf_op jit(solution)/shard_map/while/body/eval_jaxpr/kbgc,kbct->kbgt/dot_general | solution.py:39
  432.4 17.8 %fusion.28 = f32[16,2048,128]{2,1,0:T(8,128)} fusion(f32[16,8,256,128]{3,2,1,0:T(8,128)} %fusion.27, f32[16,2048,128]{2,1,0:T(8,128)} %get-tuple-element.244, pred[16]{0:T(512)(128)(4,1)S(1)} %broadcast_compare_fusion.2, pred[]{:T(512)S(6)} %compare.7), kind=kLoop, calls=%fused_computation.3.clone.1 | loop fusion | flops 12582912 | bytes 50331664 | tf_op jit(solution)/shard_map/while/body/eval_jaxpr/add | solution.py:46
  462.0 13.0 %gather_fusion.1 = bf16[16,2048,128]{2,1,0:T(8,128)(2,1)} fusion(bf16[48,2048,128]{2,1,0:T(8,128)(2,1)} %get-tuple-element.258, s32[1024]{0:T(1024)S(1)} %pad_clamp_fusion.5), kind=kCustom, calls=%fused_computation.1.clone.clone.1 | custom fusion | bytes 16777280 | tf_op jit(solution)/shard_map/while/body/eval_jaxpr/jit(_take)/gather | solution.py:37
  475.0 14.0 %fusion.27 = f32[16,8,256,128]{3,2,1,0:T(8,128)} fusion(bf16[16,8,256,256]{3,2,1,0:T(8,128)(2,1)} %bitcast.29, pred[16]{0:T(512)(128)(4,1)S(1)} %get-tuple-element.231, bf16[16,8,256,128]{3,2,1,0:T(8,128)(2,1)} %bitcast.30, pred[16]{0:T(512)(128)(4,1)S(1)} %get-tuple-element.233), kind=kOutput, calls=%fused_computation.4.clone.1 | convolution fusion | flops 2160066560 | bytes 41943072 | tf_op jit(solution)/shard_map/while/body/eval_jaxpr/kbgc,kbct->kbgt/dot_general | solution.py:39
  489.0 17.8 %fusion.28 = f32[16,2048,128]{2,1,0:T(8,128)} fusion(f32[16,8,256,128]{3,2,1,0:T(8,128)} %fusion.27, f32[16,2048,128]{2,1,0:T(8,128)} %get-tuple-element.244, pred[16]{0:T(512)(128)(4,1)S(1)} %broadcast_compare_fusion.2, pred[]{:T(512)S(6)} %compare.7), kind=kLoop, calls=%fused_computation.3.clone.1 | loop fusion | flops 12582912 | bytes 50331664 | tf_op jit(solution)/shard_map/while/body/eval_jaxpr/add | solution.py:46
  519.2 13.0 %gather_fusion.1 = bf16[16,2048,128]{2,1,0:T(8,128)(2,1)} fusion(bf16[48,2048,128]{2,1,0:T(8,128)(2,1)} %get-tuple-element.258, s32[1024]{0:T(1024)S(1)} %pad_clamp_fusion.5), kind=kCustom, calls=%fused_computation.1.clone.clone.1 | custom fusion | bytes 16777280 | tf_op jit(solution)/shard_map/while/body/eval_jaxpr/jit(_take)/gather | solution.py:37
  532.2 14.0 %fusion.27 = f32[16,8,256,128]{3,2,1,0:T(8,128)} fusion(bf16[16,8,256,256]{3,2,1,0:T(8,128)(2,1)} %bitcast.29, pred[16]{0:T(512)(128)(4,1)S(1)} %get-tuple-element.231, bf16[16,8,256,128]{3,2,1,0:T(8,128)(2,1)} %bitcast.30, pred[16]{0:T(512)(128)(4,1)S(1)} %get-tuple-element.233), kind=kOutput, calls=%fused_computation.4.clone.1 | convolution fusion | flops 2160066560 | bytes 41943072 | tf_op jit(solution)/shard_map/while/body/eval_jaxpr/kbgc,kbct->kbgt/dot_general | solution.py:39
  546.3 17.8 %fusion.28 = f32[16,2048,128]{2,1,0:T(8,128)} fusion(f32[16,8,256,128]{3,2,1,0:T(8,128)} %fusion.27, f32[16,2048,128]{2,1,0:T(8,128)} %get-tuple-element.244, pred[16]{0:T(512)(128)(4,1)S(1)} %broadcast_compare_fusion.2, pred[]{:T(512)S(6)} %compare.7), kind=kLoop, calls=%fused_computation.3.clone.1 | loop fusion | flops 12582912 | bytes 50331664 | tf_op jit(solution)/shard_map/while/body/eval_jaxpr/add | solution.py:46
  588.9 14.0 %fusion.27 = f32[16,8,256,128]{3,2,1,0:T(8,128)} fusion(bf16[16,8,256,256]{3,2,1,0:T(8,128)(2,1)} %bitcast.29, pred[16]{0:T(512)(128)(4,1)S(1)} %get-tuple-element.231, bf16[16,8,256,128]{3,2,1,0:T(8,128)(2,1)} %bitcast.30, pred[16]{0:T(512)(128)(4,1)S(1)} %get-tuple-element.233), kind=kOutput, calls=%fused_computation.4.clone.1 | convolution fusion | flops 2160066560 | bytes 41943072 | tf_op jit(solution)/shard_map/while/body/eval_jaxpr/kbgc,kbct->kbgt/dot_general | solution.py:39
  602.9 17.8 %fusion.28 = f32[16,2048,128]{2,1,0:T(8,128)} fusion(f32[16,8,256,128]{3,2,1,0:T(8,128)} %fusion.27, f32[16,2048,128]{2,1,0:T(8,128)} %get-tuple-element.244, pred[16]{0:T(512)(128)(4,1)S(1)} %broadcast_compare_fusion.2, pred[]{:T(512)S(6)} %compare.7), kind=kLoop, calls=%fused_computation.3.clone.1 | loop fusion | flops 12582912 | bytes 50331664 | tf_op jit(solution)/shard_map/while/body/eval_jaxpr/add | solution.py:46
  632.6 13.0 %gather_fusion.1 = bf16[16,2048,128]{2,1,0:T(8,128)(2,1)} fusion(bf16[48,2048,128]{2,1,0:T(8,128)(2,1)} %get-tuple-element.258, s32[1024]{0:T(1024)S(1)} %pad_clamp_fusion.5), kind=kCustom, calls=%fused_computation.1.clone.clone.1 | custom fusion | bytes 16777280 | tf_op jit(solution)/shard_map/while/body/eval_jaxpr/jit(_take)/gather | solution.py:37
  645.6 14.0 %fusion.27 = f32[16,8,256,128]{3,2,1,0:T(8,128)} fusion(bf16[16,8,256,256]{3,2,1,0:T(8,128)(2,1)} %bitcast.29, pred[16]{0:T(512)(128)(4,1)S(1)} %get-tuple-element.231, bf16[16,8,256,128]{3,2,1,0:T(8,128)(2,1)} %bitcast.30, pred[16]{0:T(512)(128)(4,1)S(1)} %get-tuple-element.233), kind=kOutput, calls=%fused_computation.4.clone.1 | convolution fusion | flops 2160066560 | bytes 41943072 | tf_op jit(solution)/shard_map/while/body/eval_jaxpr/kbgc,kbct->kbgt/dot_general | solution.py:39
  659.6 17.8 %fusion.28 = f32[16,2048,128]{2,1,0:T(8,128)} fusion(f32[16,8,256,128]{3,2,1,0:T(8,128)} %fusion.27, f32[16,2048,128]{2,1,0:T(8,128)} %get-tuple-element.244, pred[16]{0:T(512)(128)(4,1)S(1)} %broadcast_compare_fusion.2, pred[]{:T(512)S(6)} %compare.7), kind=kLoop, calls=%fused_computation.3.clone.1 | loop fusion | flops 12582912 | bytes 50331664 | tf_op jit(solution)/shard_map/while/body/eval_jaxpr/add | solution.py:46
  677.5 13.3 %gather_fusion = bf16[16,2048,256]{2,1,0:T(8,128)(2,1)} fusion(bf16[32,2048,256]{2,1,0:T(8,128)(2,1)} %get-tuple-element.256, s32[1024]{0:T(1024)S(1)} %pad_clamp_fusion.4), kind=kCustom, calls=%fused_computation.clone.clone.1 | custom fusion | bytes 33554496 | tf_op jit(solution)/shard_map/while/body/eval_jaxpr/jit(_take)/gather | solution.py:38
  703.7 14.0 %fusion.27 = f32[16,8,256,128]{3,2,1,0:T(8,128)} fusion(bf16[16,8,256,256]{3,2,1,0:T(8,128)(2,1)} %bitcast.29, pred[16]{0:T(512)(128)(4,1)S(1)} %get-tuple-element.231, bf16[16,8,256,128]{3,2,1,0:T(8,128)(2,1)} %bitcast.30, pred[16]{0:T(512)(128)(4,1)S(1)} %get-tuple-element.233), kind=kOutput, calls=%fused_computation.4.clone.1 | convolution fusion | flops 2160066560 | bytes 41943072 | tf_op jit(solution)/shard_map/while/body/eval_jaxpr/kbgc,kbct->kbgt/dot_general | solution.py:39
  717.8 17.8 %fusion.28 = f32[16,2048,128]{2,1,0:T(8,128)} fusion(f32[16,8,256,128]{3,2,1,0:T(8,128)} %fusion.27, f32[16,2048,128]{2,1,0:T(8,128)} %get-tuple-element.244, pred[16]{0:T(512)(128)(4,1)S(1)} %broadcast_compare_fusion.2, pred[]{:T(512)S(6)} %compare.7), kind=kLoop, calls=%fused_computation.3.clone.1 | loop fusion | flops 12582912 | bytes 50331664 | tf_op jit(solution)/shard_map/while/body/eval_jaxpr/add | solution.py:46
  747.4 13.0 %gather_fusion.1 = bf16[16,2048,128]{2,1,0:T(8,128)(2,1)} fusion(bf16[48,2048,128]{2,1,0:T(8,128)(2,1)} %get-tuple-element.258, s32[1024]{0:T(1024)S(1)} %pad_clamp_fusion.5), kind=kCustom, calls=%fused_computation.1.clone.clone.1 | custom fusion | bytes 16777280 | tf_op jit(solution)/shard_map/while/body/eval_jaxpr/jit(_take)/gather | solution.py:37
  760.4 14.0 %fusion.27 = f32[16,8,256,128]{3,2,1,0:T(8,128)} fusion(bf16[16,8,256,256]{3,2,1,0:T(8,128)(2,1)} %bitcast.29, pred[16]{0:T(512)(128)(4,1)S(1)} %get-tuple-element.231, bf16[16,8,256,128]{3,2,1,0:T(8,128)(2,1)} %bitcast.30, pred[16]{0:T(512)(128)(4,1)S(1)} %get-tuple-element.233), kind=kOutput, calls=%fused_computation.4.clone.1 | convolution fusion | flops 2160066560 | bytes 41943072 | tf_op jit(solution)/shard_map/while/body/eval_jaxpr/kbgc,kbct->kbgt/dot_general | solution.py:39
  774.4 17.8 %fusion.28 = f32[16,2048,128]{2,1,0:T(8,128)} fusion(f32[16,8,256,128]{3,2,1,0:T(8,128)} %fusion.27, f32[16,2048,128]{2,1,0:T(8,128)} %get-tuple-element.244, pred[16]{0:T(512)(128)(4,1)S(1)} %broadcast_compare_fusion.2, pred[]{:T(512)S(6)} %compare.7), kind=kLoop, calls=%fused_computation.3.clone.1 | loop fusion | flops 12582912 | bytes 50331664 | tf_op jit(solution)/shard_map/while/body/eval_jaxpr/add | solution.py:46
  804.4 13.0 %gather_fusion.1 = bf16[16,2048,128]{2,1,0:T(8,128)(2,1)} fusion(bf16[48,2048,128]{2,1,0:T(8,128)(2,1)} %get-tuple-element.258, s32[1024]{0:T(1024)S(1)} %pad_clamp_fusion.5), kind=kCustom, calls=%fused_computation.1.clone.clone.1 | custom fusion | bytes 16777280 | tf_op jit(solution)/shard_map/while/body/eval_jaxpr/jit(_take)/gather | solution.py:37
  817.4 14.0 %fusion.27 = f32[16,8,256,128]{3,2,1,0:T(8,128)} fusion(bf16[16,8,256,256]{3,2,1,0:T(8,128)(2,1)} %bitcast.29, pred[16]{0:T(512)(128)(4,1)S(1)} %get-tuple-element.231, bf16[16,8,256,128]{3,2,1,0:T(8,128)(2,1)} %bitcast.30, pred[16]{0:T(512)(128)(4,1)S(1)} %get-tuple-element.233), kind=kOutput, calls=%fused_computation.4.clone.1 | convolution fusion | flops 2160066560 | bytes 41943072 | tf_op jit(solution)/shard_map/while/body/eval_jaxpr/kbgc,kbct->kbgt/dot_general | solution.py:39
  831.4 17.8 %fusion.28 = f32[16,2048,128]{2,1,0:T(8,128)} fusion(f32[16,8,256,128]{3,2,1,0:T(8,128)} %fusion.27, f32[16,2048,128]{2,1,0:T(8,128)} %get-tuple-element.244, pred[16]{0:T(512)(128)(4,1)S(1)} %broadcast_compare_fusion.2, pred[]{:T(512)S(6)} %compare.7), kind=kLoop, calls=%fused_computation.3.clone.1 | loop fusion | flops 12582912 | bytes 50331664 | tf_op jit(solution)/shard_map/while/body/eval_jaxpr/add | solution.py:46
  874.7 14.0 %fusion.27 = f32[16,8,256,128]{3,2,1,0:T(8,128)} fusion(bf16[16,8,256,256]{3,2,1,0:T(8,128)(2,1)} %bitcast.29, pred[16]{0:T(512)(128)(4,1)S(1)} %get-tuple-element.231, bf16[16,8,256,128]{3,2,1,0:T(8,128)(2,1)} %bitcast.30, pred[16]{0:T(512)(128)(4,1)S(1)} %get-tuple-element.233), kind=kOutput, calls=%fused_computation.4.clone.1 | convolution fusion | flops 2160066560 | bytes 41943072 | tf_op jit(solution)/shard_map/while/body/eval_jaxpr/kbgc,kbct->kbgt/dot_general | solution.py:39
  888.7 17.8 %fusion.28 = f32[16,2048,128]{2,1,0:T(8,128)} fusion(f32[16,8,256,128]{3,2,1,0:T(8,128)} %fusion.27, f32[16,2048,128]{2,1,0:T(8,128)} %get-tuple-element.244, pred[16]{0:T(512)(128)(4,1)S(1)} %broadcast_compare_fusion.2, pred[]{:T(512)S(6)} %compare.7), kind=kLoop, calls=%fused_computation.3.clone.1 | loop fusion | flops 12582912 | bytes 50331664 | tf_op jit(solution)/shard_map/while/body/eval_jaxpr/add | solution.py:46
  918.4 13.0 %gather_fusion.1 = bf16[16,2048,128]{2,1,0:T(8,128)(2,1)} fusion(bf16[48,2048,128]{2,1,0:T(8,128)(2,1)} %get-tuple-element.258, s32[1024]{0:T(1024)S(1)} %pad_clamp_fusion.5), kind=kCustom, calls=%fused_computation.1.clone.clone.1 | custom fusion | bytes 16777280 | tf_op jit(solution)/shard_map/while/body/eval_jaxpr/jit(_take)/gather | solution.py:37
  931.4 14.0 %fusion.27 = f32[16,8,256,128]{3,2,1,0:T(8,128)} fusion(bf16[16,8,256,256]{3,2,1,0:T(8,128)(2,1)} %bitcast.29, pred[16]{0:T(512)(128)(4,1)S(1)} %get-tuple-element.231, bf16[16,8,256,128]{3,2,1,0:T(8,128)(2,1)} %bitcast.30, pred[16]{0:T(512)(128)(4,1)S(1)} %get-tuple-element.233), kind=kOutput, calls=%fused_computation.4.clone.1 | convolution fusion | flops 2160066560 | bytes 41943072 | tf_op jit(solution)/shard_map/while/body/eval_jaxpr/kbgc,kbct->kbgt/dot_general | solution.py:39
  945.4 17.8 %fusion.28 = f32[16,2048,128]{2,1,0:T(8,128)} fusion(f32[16,8,256,128]{3,2,1,0:T(8,128)} %fusion.27, f32[16,2048,128]{2,1,0:T(8,128)} %get-tuple-element.244, pred[16]{0:T(512)(128)(4,1)S(1)} %broadcast_compare_fusion.2, pred[]{:T(512)S(6)} %compare.7), kind=kLoop, calls=%fused_computation.3.clone.1 | loop fusion | flops 12582912 | bytes 50331664 | tf_op jit(solution)/shard_map/while/body/eval_jaxpr/add | solution.py:46
  988.0 14.0 %fusion.27 = f32[16,8,256,128]{3,2,1,0:T(8,128)} fusion(bf16[16,8,256,256]{3,2,1,0:T(8,128)(2,1)} %bitcast.29, pred[16]{0:T(512)(128)(4,1)S(1)} %get-tuple-element.231, bf16[16,8,256,128]{3,2,1,0:T(8,128)(2,1)} %bitcast.30, pred[16]{0:T(512)(128)(4,1)S(1)} %get-tuple-element.233), kind=kOutput, calls=%fused_computation.4.clone.1 | convolution fusion | flops 2160066560 | bytes 41943072 | tf_op jit(solution)/shard_map/while/body/eval_jaxpr/kbgc,kbct->kbgt/dot_general | solution.py:39
  1002.1 17.8 %fusion.28 = f32[16,2048,128]{2,1,0:T(8,128)} fusion(f32[16,8,256,128]{3,2,1,0:T(8,128)} %fusion.27, f32[16,2048,128]{2,1,0:T(8,128)} %get-tuple-element.244, pred[16]{0:T(512)(128)(4,1)S(1)} %broadcast_compare_fusion.2, pred[]{:T(512)S(6)} %compare.7), kind=kLoop, calls=%fused_computation.3.clone.1 | loop fusion | flops 12582912 | bytes 50331664 | tf_op jit(solution)/shard_map/while/body/eval_jaxpr/add | solution.py:46
  1044.7 14.0 %fusion.27 = f32[16,8,256,128]{3,2,1,0:T(8,128)} fusion(bf16[16,8,256,256]{3,2,1,0:T(8,128)(2,1)} %bitcast.29, pred[16]{0:T(512)(128)(4,1)S(1)} %get-tuple-element.231, bf16[16,8,256,128]{3,2,1,0:T(8,128)(2,1)} %bitcast.30, pred[16]{0:T(512)(128)(4,1)S(1)} %get-tuple-element.233), kind=kOutput, calls=%fused_computation.4.clone.1 | convolution fusion | flops 2160066560 | bytes 41943072 | tf_op jit(solution)/shard_map/while/body/eval_jaxpr/kbgc,kbct->kbgt/dot_general | solution.py:39
  1058.8 17.8 %fusion.28 = f32[16,2048,128]{2,1,0:T(8,128)} fusion(f32[16,8,256,128]{3,2,1,0:T(8,128)} %fusion.27, f32[16,2048,128]{2,1,0:T(8,128)} %get-tuple-element.244, pred[16]{0:T(512)(128)(4,1)S(1)} %broadcast_compare_fusion.2, pred[]{:T(512)S(6)} %compare.7), kind=kLoop, calls=%fused_computation.3.clone.1 | loop fusion | flops 12582912 | bytes 50331664 | tf_op jit(solution)/shard_map/while/body/eval_jaxpr/add | solution.py:46
  1076.6 13.2 %gather_fusion = bf16[16,2048,256]{2,1,0:T(8,128)(2,1)} fusion(bf16[32,2048,256]{2,1,0:T(8,128)(2,1)} %get-tuple-element.256, s32[1024]{0:T(1024)S(1)} %pad_clamp_fusion.4), kind=kCustom, calls=%fused_computation.clone.clone.1 | custom fusion | bytes 33554496 | tf_op jit(solution)/shard_map/while/body/eval_jaxpr/jit(_take)/gather | solution.py:38
  1102.9 14.0 %fusion.27 = f32[16,8,256,128]{3,2,1,0:T(8,128)} fusion(bf16[16,8,256,256]{3,2,1,0:T(8,128)(2,1)} %bitcast.29, pred[16]{0:T(512)(128)(4,1)S(1)} %get-tuple-element.231, bf16[16,8,256,128]{3,2,1,0:T(8,128)(2,1)} %bitcast.30, pred[16]{0:T(512)(128)(4,1)S(1)} %get-tuple-element.233), kind=kOutput, calls=%fused_computation.4.clone.1 | convolution fusion | flops 2160066560 | bytes 41943072 | tf_op jit(solution)/shard_map/while/body/eval_jaxpr/kbgc,kbct->kbgt/dot_general | solution.py:39
  1116.9 17.8 %fusion.28 = f32[16,2048,128]{2,1,0:T(8,128)} fusion(f32[16,8,256,128]{3,2,1,0:T(8,128)} %fusion.27, f32[16,2048,128]{2,1,0:T(8,128)} %get-tuple-element.244, pred[16]{0:T(512)(128)(4,1)S(1)} %broadcast_compare_fusion.2, pred[]{:T(512)S(6)} %compare.7), kind=kLoop, calls=%fused_computation.3.clone.1 | loop fusion | flops 12582912 | bytes 50331664 | tf_op jit(solution)/shard_map/while/body/eval_jaxpr/add | solution.py:46
  1145.9 15.6 %reduce-scatter.2.cloned.1.call-done = f32[16,32,128]{2,1,0:T(8,128)} async-done(((f32[16,64,128]{2,1,0:T(8,128)}), f32[16,32,128]{2,1,0:T(8,128)}) %reduce-scatter.2.cloned.1.call-update) | async-done | bytes 262160 | tf_op jit(solution)/shard_map/reduce_scatter | solution.py:56
  (109 shorter events, 290.5 us)
Async XLA Ops:
  6.5 1139.3 %copy-start = (f32[16,64]{1,0:T(8,128)S(1)}, f32[16,64]{1,0:T(8,128)}, u32[]{:S(2)}) copy-start(f32[16,64]{1,0:T(8,128)} %param.12) | copy-start | bytes 12292
  6.5 180.8 %all-reduce.2.cloned.1.call-start = ((), (), s32[]{:S(2)}) async-start(), calls=%async_computation.1 | async-start | bytes 2097152 | tf_op jit(solution)/shard_map/psum | solution.py:31
  16.1 190.8 %collective-permute-start = (bf16[16,2048,128]{2,1,0:T(8,128)(2,1)}, bf16[16,2048,128]{2,1,0:T(8,128)(2,1)}, u32[]{:S(2)}, u32[]{:S(2)}) collective-permute-start(bf16[16,2048,128]{2,1,0:T(8,128)(2,1)} %get-tuple-element.182), channel_id=1, source_target_pairs={{0,2},{2,4},{4,6},{6,8},{8,10},{10,12},{12,14},{14,16},{16,18},{18... | collective-permute-start | bytes 25165832 | tf_op jit(solution)/shard_map/ppermute | solution.py:10
  18.7 190.7 %collective-permute-start.1 = (bf16[16,2048,128]{2,1,0:T(8,128)(2,1)}, bf16[16,2048,128]{2,1,0:T(8,128)(2,1)}, u32[]{:S(2)}, u32[]{:S(2)}) collective-permute-start(bf16[16,2048,128]{2,1,0:T(8,128)(2,1)} %get-tuple-element.182), channel_id=1, source_target_pairs={{0,30},{2,0},{4,2},{6,4},{8,6},{10,8},{12,10},{14,12},{16,14},{18,... | collective-permute-start | bytes 25165832 | tf_op jit(solution)/shard_map/ppermute | solution.py:10
  18.7 1142.8 %reduce-scatter.2.cloned.1.call-start = ((), (), s32[]{:S(2)}) async-start(), calls=%async_computation.2 | async-start | bytes 786432 | tf_op jit(solution)/shard_map/reduce_scatter | solution.py:56
  189.9 37.2 %copy-start.3 = (s32[16]{0:T(128)S(1)}, s32[16]{0:T(128)}, u32[]{:S(2)}) copy-start(s32[16]{0:T(128)} %param.16) | copy-start | bytes 196
  227.0 907.7 %copy-start.1 = (f32[2048,128]{1,0:T(8,128)S(1)}, f32[2048,128]{1,0:T(8,128)}, u32[]{:S(2)}) copy-start(f32[2048,128]{1,0:T(8,128)} %multiply_multiply_fusion) | copy-start | bytes 3145732
  1134.7 26.8 %copy-start.2 = (bf16[16,64,128]{2,1,0:T(8,128)(2,1)S(1)}, bf16[16,64,128]{2,1,0:T(8,128)(2,1)}, u32[]{:S(2)}) copy-start(bf16[16,64,128]{2,1,0:T(8,128)(2,1)} %param.11) | copy-start | bytes 786436
Sparse Core Ops, SparseCore 0:
  18.9 168.4 all-reduce.1
  1145.9 15.5 reduce-scatter.1
where the time goes:
time: 1170 us
  local copies, waits for them, and re-layouts  405 us (35%)
  other arithmetic  302 us (26%)
  matrix products  245 us (21%)
  waiting for transfers between devices  202 us (17%)
  between operations  13.5 us (1%)
    add x16, other arithmetic, add_slot(): return summed + jnp.where(is_live, coupled, 0.0)  279 us
    dot_general x16, matrix products, add_slot(): jnp.einsum('kbgc,kbct->kbgt', blocks.reshape(local_k, groups, block_size,...  224 us
    gather x16, local copies, waits for them, and re-layouts, add_slot(): picked = jnp.take(window, local_index[:, slot_index], axis=0)  208 us
    gather x16, local copies, waits for them, and re-layouts, add_slot(): blocks = jnp.take(screen, q_index[:, slot_index], axis=0)  196 us
    psum x1, waiting for transfers between devices, on_device(): density_total = lax.psum(partial_value, 'ka')  167 us
  transfers between devices with their start and end apart: 4, of which 4 were waited for; matrix products, arithmetic and copies ran while one was open for 0% of the time, Pallas kernels for 0%

commit v1 on v0

v1 whole, which is shorter than its diff:
```python
import jax
import jax.numpy as jnp
from jax import lax
from jax.experimental import pallas as pl
from jax.experimental.pallas import tpu as pltpu
from jax.sharding import PartitionSpec as P

UNROLL = 16
F32, BF16 = jnp.float32, jnp.bfloat16


def pair_list(n_slot, k_slot, q, valid, q_count, length, spare):
    entries = q.shape[0]
    order = jnp.arange(entries, dtype=jnp.int32)
    qs = jnp.arange(q_count, dtype=jnp.int32)
    same = (q[:, None] == q[None, :]) & valid[None, :] & (order[None, :] < order[:, None])
    within = jnp.sum(same.astype(jnp.int32), axis=1)
    count = jnp.sum(((q[None, :] == qs[:, None]) & valid[None, :]).astype(jnp.int32), axis=1)
    padded = (count + 1) // 2 * 2
    base = jnp.sum(jnp.where(qs[None, :] < q[:, None], padded[None, :], 0), axis=1)
    place = jnp.where(valid, base + within, -1)
    code = n_slot + 64 * k_slot + 4096 * q
    blank = 64 * spare
    rows = jnp.arange(length, dtype=jnp.int32)
    listed = blank + jnp.sum(jnp.where(place[None, :] == rows[:, None], code[None, :] - blank, 0), axis=1)
    rounds = (jnp.sum(padded) + UNROLL - 1) // UNROLL
    return listed, rounds[None]


def couple_kernel(listed, rounds, group, x_ref, y_ref, tx_ref, ty_ref, w_ref, acc_ref, out_ref, prod, total):
    half = x_ref.shape[0]
    width = x_ref.shape[2]
    trials = tx_ref.shape[1]

    @pl.when(pl.program_id(0) == 0)
    def _():
        out_ref[...] = acc_ref[...]

    for ref, vec, first in ((x_ref, tx_ref, 0), (y_ref, ty_ref, half)):

        def make(i, _, ref=ref, vec=vec, first=first):
            for d in range(8):
                n = i * 8 + d
                made = jnp.dot(vec[n], ref[n], preferred_element_type=F32)
                prod[first + n] = made.astype(BF16)
            return 0

        lax.fori_loop(0, half // 8, make, 0)
    total[...] = jnp.zeros_like(total)

    def some(i, _):
        for d in range(0, UNROLL, 2):
            a, b = listed[i * UNROLL + d], listed[i * UNROLL + d + 1]
            both = jnp.concatenate([prod[a & 63], prod[b & 63]], axis=0)
            made = lax.dot_general(both, w_ref[a >> 12], (((1,), (1,)), ((), ())), preferred_element_type=F32)
            total[(a >> 6) & 63] += made[:trials]
            total[(b >> 6) & 63] += made[trials:]
        return 0

    lax.fori_loop(0, rounds[0], some, 0)
    for ref, first in ((x_ref, 0), (y_ref, half)):

        def close(i, _, ref=ref, first=first):
            for d in range(8):
                k = i * 8 + d
                out_ref[first + k] += lax.dot_general(
                    ref[k], total[first + k].astype(BF16), (((1,), (1,)), ((), ())), preferred_element_type=F32
                )
            return 0

        lax.fori_loop(0, half // 8, close, 0)


def couple(listed, rounds, first_group, x, y, tx, ty, screen, acc, groups):
    half, pairs, _ = x.shape
    trials = tx.shape[1]
    q_count, _, width = screen.shape
    slots = 2 * half
    chunk = pl.BlockSpec((half, pairs, width), lambda i, *_: (0, 0, i))
    whole_t = pl.BlockSpec((half, trials, pairs), lambda i, *_: (0, 0, 0))
    sums = pl.BlockSpec((slots, pairs, trials), lambda i, *_: (0, 0, 0))
    work = groups * 2 * 128 * width * width * trials
    return pl.pallas_call(
        couple_kernel,
        out_shape=jax.ShapeDtypeStruct((slots, pairs, trials), F32),
        grid_spec=pltpu.PrefetchScalarGridSpec(
            num_scalar_prefetch=3,
            grid=(groups,),
            in_specs=[
                chunk,
                chunk,
                whole_t,
                whole_t,
                pl.BlockSpec((q_count, width, width), lambda i, l, r, g: (0, g[0] + i, 0)),
                sums,
            ],
            out_specs=sums,
            scratch_shapes=[
                pltpu.VMEM((slots, trials, width), BF16),
                pltpu.VMEM((slots + 1, trials, width), F32),
            ],
        ),
        compiler_params=pltpu.CompilerParams(vmem_limit_bytes=48 << 20),
        cost_estimate=pl.CostEstimate(
            flops=2 * work, transcendentals=0, bytes_accessed=groups * q_count * width * width * 2
        ),
    )(listed, rounds, first_group, x, y, tx, ty, screen, acc)


def ring_sum(part, me, size):
    steps = []
    bit = 2
    while bit < size:
        steps.append(bit)
        bit *= 2
    for bit in steps:
        rows = part.shape[0] // 2
        high = (me // bit) % 2
        keep = lax.dynamic_slice_in_dim(part, high * rows, rows, 0)
        give = lax.dynamic_slice_in_dim(part, (1 - high) * rows, rows, 0).astype(BF16)
        part = keep + lax.ppermute(give, "ka", [(i, i ^ bit) for i in range(size)]).astype(F32)
    part = part.astype(BF16)
    for bit in reversed(steps):
        high = (me // bit) % 2
        other = lax.ppermute(part, "ka", [(i, i ^ bit) for i in range(size)])
        part = jnp.where(high == 0, jnp.concatenate([part, other], 0), jnp.concatenate([other, part], 0))
    return part


def on_device(pair_density, trial_vectors, energy, coulomb, screen, neighbors, live_count, q_index):
    local_k, pair_count, local_g = pair_density.shape
    trial_count = trial_vectors.shape[2]
    q_count, _, width = screen.shape
    slots = neighbors.shape[1]
    size, parts = lax.axis_size("ka"), lax.axis_size("ga")
    me, mine = lax.axis_index("ka"), lax.axis_index("ga")
    core = me % 2
    half_g = local_g // 2
    groups = half_g // width
    first_block = me - core
    sibling = [(i, i ^ 1) for i in range(size)]
    onward = [(i, (i + 2) % size) for i in range(size)]

    def by_block(own, other):
        return jnp.where(core == 0, own, other), jnp.where(core == 0, other, own)

    own_half = lax.dynamic_slice_in_dim(pair_density, core * half_g, half_g, 2)
    give_half = lax.dynamic_slice_in_dim(pair_density, (1 - core) * half_g, half_g, 2)
    dens_a, dens_b = by_block(own_half, lax.ppermute(give_half, "ka", sibling))
    table = jnp.concatenate([neighbors, q_index, live_count[:, None]], axis=1)
    table_a, table_b = by_block(table, lax.ppermute(table, "ka", sibling))
    vec_a, vec_b = by_block(trial_vectors, lax.ppermute(trial_vectors, "ka", sibling))

    quarter = local_k // 2
    vec_half = lax.ppermute(lax.dynamic_slice_in_dim(vec_b, core * quarter, quarter, 0), "ka", onward)
    table_p = lax.ppermute(table_b, "ka", onward)
    chunks = [
        lax.ppermute(dens_b[:, :, c * width : (c + 1) * width], "ka", onward) for c in range(groups)
    ]
    vec_other = lax.ppermute(vec_half, "ka", sibling)
    vec_p = jnp.where(
        core == 0, jnp.concatenate([vec_half, vec_other], 0), jnp.concatenate([vec_other, vec_half], 0)
    )

    part = sum(
        lax.dot_general(d, v, (((0, 1), (0, 1)), ((), ())), preferred_element_type=F32)
        for d, v in ((dens_a, vec_a), (dens_b, vec_b))
    )
    density_total = ring_sum(part, me, size)
    my_coulomb = lax.dynamic_slice_in_dim(coulomb, core * half_g, half_g, 0)
    screened2 = (2.0 * my_coulomb[:, None] * density_total.astype(F32)).astype(BF16)

    def columns(t):
        live = jnp.arange(slots, dtype=jnp.int32)[None, :] < t[:, 2 * slots :]
        near = t[:, :slots]
        return near // local_k, near % local_k, t[:, slots : 2 * slots], live

    row = jnp.broadcast_to(jnp.arange(local_k, dtype=jnp.int32)[:, None], (local_k, slots))
    blk_a, in_a, q_a, live_a = columns(table_a)
    blk_b, in_b, q_b, live_b = columns(table_b)
    blk_p, in_p, q_p, live_p = columns(table_p)
    flat = lambda u, v: jnp.concatenate([u.reshape(-1), v.reshape(-1)])
    last_block = first_block + 1
    before = (first_block + size - 1) % size
    length = 2 * local_k * slots + q_count
    length = (length + UNROLL - 1) // UNROLL * UNROLL
    here = lambda blk, live: live & ((blk == first_block) | (blk == last_block))
    near_list, near_rounds = pair_list(
        flat(in_a + local_k * (blk_a == last_block), in_b + local_k * (blk_b == last_block)),
        flat(row, row + local_k),
        flat(q_a, q_b),
        flat(here(blk_a, live_a), here(blk_b, live_b)),
        q_count,
        length,
        2 * local_k,
    )
    far_list, far_rounds = pair_list(
        flat(in_a + local_k, in_p),
        flat(row, row + local_k),
        flat(q_a, q_p),
        flat(live_a & (blk_a == before), live_p & (blk_p == first_block)),
        q_count,
        length,
        2 * local_k,
    )

    turned = lambda v: jnp.swapaxes(v, 1, 2)
    tv_a, tv_b, tv_p = turned(vec_a), turned(vec_b), turned(vec_p)
    start = (core * groups).astype(jnp.int32)
    zero = jnp.zeros((2 * local_k, pair_count, trial_count), F32)
    near = couple(near_list, near_rounds, start[None], dens_a, dens_b, tv_a, tv_b, screen, zero, groups)
    far = zero
    for c in range(groups):
        part_a = dens_a[:, :, c * width : (c + 1) * width]
        far = couple(
            far_list, far_rounds, (start + c)[None], part_a, chunks[c], tv_a, tv_p, screen, far, 1
        )
    exchange_a, exchange_b = (
        lax.dot_general(d, screened2, (((2,), (0,)), ((), ())), preferred_element_type=F32)
        for d in (dens_a, dens_b)
    )
    sum_a = exchange_a - near[:local_k] - far[:local_k]
    sum_b = exchange_b - near[local_k:]
    sum_p = -far[local_k:]

    got = lax.ppermute(jnp.where(core == 0, sum_b, sum_a).astype(BF16), "ka", sibling).astype(F32)
    own = jnp.where(core == 0, sum_a, sum_b) + got
    passed = lax.ppermute(sum_p.astype(BF16), "ka", [(i, i + 1) for i in range(0, size, 2)])
    back = sum_p + passed.astype(F32)
    rows = pair_count // parts

    def sent(value, steps, ka_pairs):
        rows_of = lax.dynamic_slice_in_dim(value, ((mine + steps) % parts) * rows, rows, 1)
        pairs = [
            (s * parts + g, d * parts + (g + steps) % parts) for s, d in ka_pairs for g in range(parts)
        ]
        return lax.ppermute(rows_of.astype(BF16), ("ka", "ga"), pairs).astype(F32)

    stay = [(i, i) for i in range(size)]
    back_pairs = [(i, (i - 2) % size) for i in range(1, size, 2)]
    answer = lax.dynamic_slice_in_dim(own, mine * rows, rows, 1)
    for steps in range(1, parts):
        answer = answer + sent(own, steps, stay)
    for steps in range(parts):
        answer = answer + sent(back, steps, back_pairs)
    energy_rows = lax.dynamic_slice_in_dim(energy, mine * rows, rows, 1)
    vector_rows = lax.dynamic_slice_in_dim(trial_vectors, mine * rows, rows, 1)
    return (energy_rows[:, :, None] * vector_rows.astype(F32) + answer).astype(BF16)


def solution(mesh):
    in_specs = (
        P("ka", None, "ga"),
        P("ka", None, None),
        P("ka", None),
        P("ga"),
        P(None, "ga", None),
        P("ka", None),
        P("ka"),
        P("ka", None),
    )
    out_specs = P("ka", "ga", None)
    return jax.shard_map(
        on_device, mesh=mesh, in_specs=in_specs, out_specs=out_specs, check_vma=False
    )
```

time: 1170 us -> 191 us (0.16)
  local copies, waits for them, and re-layouts: 405 us -> 27.6 us
  other arithmetic: 302 us -> 16.3 us
  matrix products: 245 us -> 9.07 us
  waiting for transfers between devices: 202 us -> 31.5 us
  Pallas kernels: 0 us -> 77.2 us
  starting transfers between devices: 2.65 us -> 27.9 us
    gather x32 -> x0, local copies, waits for them, and re-layouts: 403 us -> none  [the longest x16 208 us: add_slot(): picked = jnp.take(window, local_index[:, slot_index], axis=0)]
    add x17 -> x8, other arithmetic: 279 us -> 2.54 us  [the longest x1 1.21 us: on_device(): back = sum_p + passed.astype(F32)]
    dot_general x18 -> x4, matrix products: 245 us -> 9.07 us  [the longest x2 5.35 us: on_device(): lax.dot_general(d, screened2, (((2,), (0,)), ((), ())), preferred_element...]
    psum x1 -> x0, waiting for transfers between devices: 167 us -> none  [on_device(): density_total = lax.psum(partial_value, 'ka')]
    pallas_call x0 -> x5, Pallas kernels: none -> 77.2 us  [couple(): pl.pallas_call(couple_kernel, out_shape=jax.ShapeDtypeStruct((slots, pair...]
    ppermute x2 -> x21, starting transfers between devices: 2.6 us -> 27.9 us  [the longest x3 7.35 us: ring_sum(): other = lax.ppermute(part, 'ka', [(i, i ^ bit) for i in range(size)])]
    concatenate x1, other arithmetic: 17.6 us -> 0.79 us  [on_device(): table = jnp.concatenate([neighbors, q_index, live_count[:, None]], axis=1)]
    reduce_scatter x1 -> x0, waiting for transfers between devices: 15.6 us -> none  [on_device(): mine = lax.psum_scatter(pair_terms, 'ga', scatter_dimension=1, tiled=True)]
  transfers between devices with their start and end apart: 4 -> 21, of which waited for: 4 -> 7; matrix products, arithmetic and copies ran while one was open for 0% -> 23% of each run, Pallas kernels for 0% -> 40%
where the time goes in v1:
time: 191 us; the launch traced here: 192 us
  Pallas kernels  77.2 us (40%)
  waiting for transfers between devices  31.5 us (16%)
  starting transfers between devices  27.9 us (15%)
  local copies, waits for them, and re-layouts  27.6 us (14%)
  other arithmetic  16.3 us (9%)
  matrix products  9.07 us (5%)
  between operations  1.92 us (1%)
    pallas_call x5, Pallas kernels, couple(): pl.pallas_call(couple_kernel, out_shape=jax.ShapeDtypeStruct((slots, pair...  77.2 us
    ppermute x3, waiting for transfers between devices, sent(): return lax.ppermute(rows_of.astype(BF16), ('ka', 'ga'), pairs).astype(F32)  15.8 us
    unnamed x46, local copies, waits for them, and re-layouts  12.3 us
    ppermute x1, waiting for transfers between devices, on_device(): lax.ppermute(lax.dynamic_slice_in_dim(vec_b, core * quarter, quarter, 0),...  9.3 us
    ppermute x3, starting transfers between devices, ring_sum(): other = lax.ppermute(part, 'ka', [(i, i ^ bit) for i in range(size)])  7.35 us
    dot_general x2, matrix products, on_device(): lax.dot_general(d, screened2, (((2,), (0,)), ((), ())), preferred_element...  5.35 us
    ppermute x3, starting transfers between devices, sent(): return lax.ppermute(rows_of.astype(BF16), ('ka', 'ga'), pairs).astype(F32)  5.07 us
    select_n x3, other arithmetic, by_block(): return (jnp.where(core == 0, own, other), jnp.where(core == 0, other, own))  4.61 us
  transfers between devices with their start and end apart: 21, of which 7 were waited for; matrix products, arithmetic and copies ran while one was open for 23% of the time, Pallas kernels for 40%

profile of v1, /device:TPU:1, one launch (start us, length us, event | category | flops | bytes accessed | tf_op | source)
XLA Modules:
  0.0 191.6 jit_solution(13288742048151885592)
XLA Ops:
  1.6 1.9 constant_dynamic-slice_fusion.1
  5.7 2.6 %collective-permute-start.9 = (s32[16,33]{1,0:T(8,128)S(1)}, s32[16,33]{1,0:T(8,128)S(1)}, u32[]{:S(2)}, u32[]{:S(2)}) collective-permute-start(s32[16,33]{1,0:T(8,128)S(1)} %get-tuple-element.34), channel_id=1, source_target_pairs={{0,4},{2,6},{4,8},{6,10},{8,12},{10,14},{12,16},{14,18},{16,20},{1... | collective-permute-start | bytes 6344 | tf_op jit(solution)/shard_map/ppermute | solution.py:156
  10.6 1.8 collective-permute-done.9
  14.7 1.2 broadcast_select_fusion.2
  16.2 9.3 %collective-permute-done.11 = bf16[8,64,128]{1,2,0:T(8,128)(2,1)} collective-permute-done((bf16[8,64,128]{1,2,0:T(8,128)(2,1)S(1)}, bf16[8,64,128]{1,2,0:T(8,128)(2,1)}, u32[]{:S(2)}, u32[]{:S(2)}) %collective-permute-start.11) | collective-permute-done | bytes 131104 | tf_op jit(solution)/shard_map/ppermute | solution.py:155
  25.5 2.0 %collective-permute-start.12 = (bf16[8,64,128]{1,2,0:T(8,128)(2,1)}, bf16[8,64,128]{1,2,0:T(8,128)(2,1)}, u32[]{:S(2)}, u32[]{:S(2)}) collective-permute-start(bf16[8,64,128]{1,2,0:T(8,128)(2,1)} %collective-permute-done.11), channel_id=1, source_target_pairs={{0,2},{2,0},{4,6},{6,4},{8,10},{10,8},{12,14},{14,12},{16,18},{18,... | collective-permute-start | bytes 393224 | tf_op jit(solution)/shard_map/ppermute | solution.py:160
  27.5 3.3 %broadcast_select_fusion = (bf16[16,64,1024]{2,1,0:T(8,128)(2,1)S(1)}, bf16[16,64,1024]{2,1,0:T(8,128)(2,1)S(1)}) fusion(bf16[16,64,1024]{2,1,0:T(8,128)(2,1)} %collective-permute-done, pred[]{:T(512)S(6)} %eq.148, bf16[16,64,2048]{2,1,0:T(8,128)(2,1)} %param.8, s32[]{:T(128)S(6)} %select_n.246), kind=kLoop, calls=%fused_computation | loop fusion | flops 2097152 | bytes 8388613 | tf_op jit(solution)/shard_map/jit(_where)/select_n | solution.py:145
  30.9 1.3 convolution_bitcast_fusion
  32.2 2.4 %fusion.1 = f32[1024,128]{1,0:T(8,128)S(1)} fusion(f32[1024,128]{1,0:T(8,128)S(1)} %convolution_bitcast_fusion, bf16[16,64,1024]{2,1,0:T(8,128)(2,1)S(1)} %get-tuple-element.16.x_ref, bf16[16,64,128]{1,2,0:T(8,128)(2,1)S(1)} %copy.53, bf16[16,64,128]{1,2,0:T(8,128)(2,1)} %collective-permute-done.1, pred[]{:T(512)S(6)} %eq.148), kind=kOutput, calls=%fused_computation.7 | convolution fusion | flops 268697600 | bytes 3670017 | tf_op jit(solution)/shard_map/dot_general | solution.py:166
  36.7 1.4 fusion.4.ty_ref
  38.1 2.1 %collective-permute-done.2 = bf16[512,128]{1,0:T(8,128)(2,1)} collective-permute-done((bf16[512,128]{1,0:T(8,128)(2,1)S(1)}, bf16[512,128]{1,0:T(8,128)(2,1)}, u32[]{:S(2)}, u32[]{:S(2)}) %collective-permute-start.2) | collective-permute-done | bytes 131104 | tf_op jit(solution)/shard_map/ppermute | solution.py:121
  40.2 1.0 convert_add_fusion.2
  41.3 3.0 %fusion.35 = (bf16[16,64,256]{2,1,0:T(8,128)(2,1)}, bf16[16,64,256]{2,1,0:T(8,128)(2,1)}, bf16[16,64,256]{2,1,0:T(8,128)(2,1)}, bf16[16,64,256]{2,1,0:T(8,128)(2,1)}) fusion(bf16[16,64,1024]{2,1,0:T(8,128)(2,1)} %copy-done.9), kind=kLoop, calls=%fused_computation.131 | loop fusion | bytes 4194304 | tf_op jit(solution)/shard_map/slice | solution.py:158
  44.3 2.6 %collective-permute-start.13 = (bf16[16,64,256]{2,1,0:T(8,128)(2,1)}, bf16[16,64,256]{2,1,0:T(8,128)(2,1)}, u32[]{:S(2)}, u32[]{:S(2)}) collective-permute-start(bf16[16,64,256]{2,1,0:T(8,128)(2,1)} %get-tuple-element.19), channel_id=1, source_target_pairs={{0,4},{2,6},{4,8},{6,10},{8,12},{10,14},{12,16},{14,18},{16,20},{1... | collective-permute-start | bytes 1572872 | tf_op jit(solution)/shard_map/ppermute | solution.py:158
  47.0 3.3 %collective-permute-start.4 = (bf16[128,128]{1,0:T(8,128)(2,1)S(1)}, bf16[128,128]{1,0:T(8,128)(2,1)S(1)}, u32[]{:S(2)}, u32[]{:S(2)}) collective-permute-start(bf16[128,128]{1,0:T(8,128)(2,1)S(1)} %dynamic-slice_convert_fusion.6), channel_id=1, source_target_pairs={{0,16},{2,18},{4,20},{6,22},{8,24},{10,26},{12,28},{14,30},{16,0},... | collective-permute-start | bytes 98312 | tf_op jit(solution)/shard_map/ppermute | solution.py:121
  50.5 38.4 %shard_map.82 = f32[32,64,128]{2,1,0:T(8,128)S(1)} custom-call(s32[544]{0:T(1024)S(1)} %broadcast_add_fusion.1.listed, s32[1]{0:T(128)} %bitcast.4.rounds, s32[1]{0:T(128)} %bitcast.5.group, bf16[16,64,1024]{2,1,0:T(8,128)(2,1)S(1)} %get-tuple-element.16.x_ref, bf16[16,64,1024]{2,1,0:T(8,128)(2,1)} %copy-done.9, ...), custom_call_target="tpu_custom_call" | custom-call | flops 17179869184 | bytes 16777216 | tf_op jit(solution)/shard_map/pallas_call | solution.py:83
  89.0 1.5 fusion.36
  90.5 2.6 %collective-permute-done.5 = bf16[128,128]{1,0:T(8,128)(2,1)S(1)} collective-permute-done((bf16[128,128]{1,0:T(8,128)(2,1)S(1)}, bf16[128,128]{1,0:T(8,128)(2,1)S(1)}, u32[]{:S(2)}, u32[]{:S(2)}) %collective-permute-start.5) | collective-permute-done | bytes 32800 | tf_op jit(solution)/shard_map/ppermute | solution.py:125
  93.2 1.1 fusion.37
  94.3 2.4 %copy.69 = f32[16,64,128]{1,2,0:T(8,128)} copy(f32[16,64,128]{2,1,0:T(8,128)} %get-tuple-element.25) | data formatting | bytes 1048576
  96.7 2.3 %copy.71 = f32[16,64,128]{1,2,0:T(8,128)} copy(f32[16,64,128]{2,1,0:T(8,128)} %get-tuple-element.26) | data formatting | bytes 1048576
  99.0 1.0 maximum_select_fusion.2
  100.0 7.2 %collective-permute-start.7 = (bf16[512,128]{1,0:T(8,128)(2,1)S(1)}, bf16[512,128]{1,0:T(8,128)(2,1)}, u32[]{:S(2)}, u32[]{:S(2)}) collective-permute-start(bf16[512,128]{1,0:T(8,128)(2,1)S(1)} %maximum_select_fusion.2), channel_id=1, source_target_pairs={{0,4},{2,6},{4,0},{6,2},{8,12},{10,14},{12,8},{14,10},{16,20},{18,... | collective-permute-start | bytes 393224 | tf_op jit(solution)/shard_map/ppermute | solution.py:125
  107.2 1.2 copy-done.2
  108.4 1.0 copy-done.6
  109.5 9.7 %shard_map.83.acc_ref = f32[32,64,128]{2,1,0:T(8,128)S(1)} custom-call(s32[544]{0:T(1024)S(1)} %broadcast_add_fusion.listed, s32[1]{0:T(128)} %bitcast.8.rounds, s32[1]{0:T(128)} %bitcast.5.group, bf16[16,64,256]{2,1,0:T(8,128)(2,1)S(1)} %copy-done.6, bf16[16,64,256]{2,1,0:T(8,128)(2,1)} %collective-permute-done.15.y_ref, ...), custom_call_target="tpu_custom_call" | custom-call | flops 4294967296 | bytes 4194304 | tf_op jit(solution)/shard_map/pallas_call | solution.py:83
  119.2 9.7 %shard_map.84.acc_ref = f32[32,64,128]{2,1,0:T(8,128)S(1)} custom-call(s32[544]{0:T(1024)S(1)} %broadcast_add_fusion.listed, s32[1]{0:T(128)} %bitcast.8.rounds, s32[1]{0:T(128)} %bitcast.12.group, bf16[16,64,256]{2,1,0:T(8,128)(2,1)S(1)} %copy-done.5, bf16[16,64,256]{2,1,0:T(8,128)(2,1)} %collective-permute-done.14.y_ref, ...), custom_call_target="tpu_custom_call" | custom-call | flops 4294967296 | bytes 4194304 | tf_op jit(solution)/shard_map/pallas_call | solution.py:83
  129.0 9.7 %shard_map.85.acc_ref = f32[32,64,128]{2,1,0:T(8,128)S(1)} custom-call(s32[544]{0:T(1024)S(1)} %broadcast_add_fusion.listed, s32[1]{0:T(128)} %bitcast.8.rounds, s32[1]{0:T(128)} %bitcast.11.group, bf16[16,64,256]{2,1,0:T(8,128)(2,1)S(1)} %copy-done.4, bf16[16,64,256]{2,1,0:T(8,128)(2,1)} %collective-permute-done.13.y_ref, ...), custom_call_target="tpu_custom_call" | custom-call | flops 4294967296 | bytes 4194304 | tf_op jit(solution)/shard_map/pallas_call | solution.py:83
  138.7 9.7 %shard_map.86 = f32[32,64,128]{2,1,0:T(8,128)S(1)} custom-call(s32[544]{0:T(1024)S(1)} %broadcast_add_fusion.listed, s32[1]{0:T(128)} %bitcast.8.rounds, s32[1]{0:T(128)} %bitcast.9.group, bf16[16,64,256]{2,1,0:T(8,128)(2,1)S(1)} %copy-done.3, bf16[16,64,256]{2,1,0:T(8,128)(2,1)} %collective-permute-done.10.y_ref, ...), custom_call_target="tpu_custom_call" | custom-call | flops 4294967296 | bytes 4194304 | tf_op jit(solution)/shard_map/pallas_call | solution.py:83
  148.4 1.1 fusion.38
  149.5 1.4 copy.72
  150.8 1.0 negate_convert_fusion
  151.8 1.5 collective-permute-start.18
  153.3 2.4 %copy.70 = f32[16,64,128]{1,2,0:T(8,128)} copy(f32[16,64,128]{2,1,0:T(8,128)} %get-tuple-element.27) | data formatting | bytes 1048576
  155.7 3.1 %fusion = f32[16,64,128]{1,2,0:T(8,128)S(1)} fusion(f32[16,64,128]{1,2,0:T(8,128)} %copy.70, f32[16,64,128]{1,2,0:T(8,128)} %copy.69, bf16[16,64,1024]{2,1,0:T(8,128)(2,1)S(1)} %get-tuple-element.16.x_ref, bf16[512,128]{1,0:T(8,128)(2,1)} %collective-permute-done.7, bf16[512,128]{1,0:T(8,128)(2,1)S(1)} %maximum_select_fusion.2, f32[1024]{0:T(1024)S(1)} %copy-done.15, ...), kind=kOutput, calls=%fused_computation.4 | convolution fusion | flops 270270464 | bytes 3936257 | tf_op jit(solution)/shard_map/dot_general | solution.py:219
  158.8 2.3 %select_convert_fusion = (bf16[16,64,128]{1,2,0:T(8,128)(2,1)S(1)}, f32[16,64,128]{1,2,0:T(8,128)S(1)}) fusion(f32[16,64,128]{1,2,0:T(8,128)S(1)} %fusion, pred[]{:T(512)S(6)} %eq.148, f32[16,64,128]{1,2,0:T(8,128)S(1)} %copy-done.11, bf16[16,64,1024]{2,1,0:T(8,128)(2,1)S(1)} %copy-done.10, bf16[512,128]{1,0:T(8,128)(2,1)} %collective-permute-done.7, ...), kind=kOutput, calls=%fused_computation.18 | convolution fusion | flops 270270464 | bytes 4198402 | tf_op jit(solution)/shard_map/dot_general | solution.py:219
  161.1 2.6 %collective-permute-start.16 = (bf16[16,64,128]{1,2,0:T(8,128)(2,1)S(1)}, bf16[16,64,128]{1,2,0:T(8,128)(2,1)S(1)}, u32[]{:S(2)}, u32[]{:S(2)}) collective-permute-start(bf16[16,64,128]{1,2,0:T(8,128)(2,1)S(1)} %get-tuple-element.46), channel_id=1, source_target_pairs={{0,2},{2,0},{4,6},{6,4},{8,10},{10,8},{12,14},{14,12},{16,18},{18,... | collective-permute-start | bytes 786440 | tf_op jit(solution)/shard_map/ppermute | solution.py:226
  163.7 1.2 convert_add_fusion
  164.9 1.4 dynamic-slice_convert_fusion.1
  166.3 1.9 collective-permute-start.20
  168.2 1.9 %collective-permute-start.19 = (bf16[16,32,128]{1,2,0:T(8,128)(2,1)}, bf16[16,32,128]{1,2,0:T(8,128)(2,1)}, u32[]{:S(2)}, u32[]{:S(2)}) collective-permute-start(bf16[16,32,128]{1,2,0:T(8,128)(2,1)} %get-tuple-element.31), channel_id=1, source_target_pairs={{2,30},{3,31},{6,2},{7,3},{10,6},{11,7},{14,10},{15,11},{18,14},{1... | collective-permute-start | bytes 393224 | tf_op jit(solution)/shard_map/ppermute | solution.py:237
  170.4 1.0 dynamic-slice_convert_fusion.2
  171.4 1.2 collective-permute-start.17
  173.1 4.4 %collective-permute-done.20 = bf16[16,32,128]{1,2,0:T(8,128)(2,1)S(1)} collective-permute-done((bf16[16,32,128]{1,2,0:T(8,128)(2,1)}, bf16[16,32,128]{1,2,0:T(8,128)(2,1)S(1)}, u32[]{:S(2)}, u32[]{:S(2)}) %collective-permute-start.20) | collective-permute-done | bytes 131104 | tf_op jit(solution)/shard_map/ppermute | solution.py:237
  177.4 6.0 %collective-permute-done.19 = bf16[16,32,128]{1,2,0:T(8,128)(2,1)} collective-permute-done((bf16[16,32,128]{1,2,0:T(8,128)(2,1)}, bf16[16,32,128]{1,2,0:T(8,128)(2,1)}, u32[]{:S(2)}, u32[]{:S(2)}) %collective-permute-start.19) | collective-permute-done | bytes 131104 | tf_op jit(solution)/shard_map/ppermute | solution.py:237
  183.4 5.4 %collective-permute-done.17 = bf16[16,32,128]{1,2,0:T(8,128)(2,1)} collective-permute-done((bf16[16,32,128]{1,2,0:T(8,128)(2,1)}, bf16[16,32,128]{1,2,0:T(8,128)(2,1)}, u32[]{:S(2)}, u32[]{:S(2)}) %collective-permute-start.17) | collective-permute-done | bytes 131104 | tf_op jit(solution)/shard_map/ppermute | solution.py:237
  188.9 1.8 add_convert_fusion
  190.7 0.9 copy.64
  (129 shorter events, 10.5 us)
Async XLA Ops:
  0.0 173.0 %copy-start = (f32[16,64]{1,0:T(8,128)S(1)}, f32[16,64]{1,0:T(8,128)}, u32[]{:S(2)}) copy-start(f32[16,64]{1,0:T(8,128)} %param.10) | copy-start | bytes 12292
  1.5 3.9 %collective-permute-start.8 = (s32[16,33]{1,0:T(8,128)S(1)}, s32[16,33]{1,0:T(8,128)S(1)}, u32[]{:S(2)}, u32[]{:S(2)}) collective-permute-start(s32[16,33]{1,0:T(8,128)S(1)} %pad_add_fusion), channel_id=1, source_target_pairs={{0,2},{2,0},{4,6},{6,4},{8,10},{10,8},{12,14},{14,12},{16,18},{18,... | collective-permute-start | bytes 6344 | tf_op jit(solution)/shard_map/ppermute | solution.py:151
  1.6 2.4 %copy-start.12 = (bf16[16,64,128]{2,1,0:T(8,128)(2,1)S(1)}, bf16[16,64,128]{2,1,0:T(8,128)(2,1)}, u32[]{:S(2)}) copy-start(bf16[16,64,128]{2,1,0:T(8,128)(2,1)} %param.9) | copy-start | bytes 786436
  1.6 3.0 %copy-start.18 = (f32[2048]{0:T(1024)S(1)}, f32[2048]{0:T(1024)}, u32[]{:S(2)}) copy-start(f32[2048]{0:T(1024)} %param.11) | copy-start | bytes 24580
  1.6 3.8 %copy-start.16 = (s32[16,16]{1,0:T(8,128)S(1)}, s32[16,16]{1,0:T(8,128)}, u32[]{:S(2)}) copy-start(s32[16,16]{1,0:T(8,128)} %param.15) | copy-start | bytes 3076
  1.6 3.8 %copy-start.17 = (s32[16,16]{1,0:T(8,128)S(1)}, s32[16,16]{1,0:T(8,128)}, u32[]{:S(2)}) copy-start(s32[16,16]{1,0:T(8,128)} %param.13) | copy-start | bytes 3076
  3.5 24.0 %collective-permute-start = (bf16[16,64,1024]{2,1,0:T(8,128)(2,1)S(1)}, bf16[16,64,1024]{2,1,0:T(8,128)(2,1)}, u32[]{:S(2)}, u32[]{:S(2)}) collective-permute-start(bf16[16,64,1024]{2,1,0:T(8,128)(2,1)S(1)} %constant_dynamic-slice_fusion.1), channel_id=1, source_target_pairs={{0,2},{2,0},{4,6},{6,4},{8,10},{10,8},{12,14},{14,12},{16,18},{18,... | collective-permute-start | bytes 6291464 | tf_op jit(solution)/shard_map/ppermute | solution.py:149
  4.3 10.4 %collective-permute-start.1 = (bf16[16,64,128]{1,2,0:T(8,128)(2,1)S(1)}, bf16[16,64,128]{1,2,0:T(8,128)(2,1)}, u32[]{:S(2)}, u32[]{:S(2)}) collective-permute-start(bf16[16,64,128]{1,2,0:T(8,128)(2,1)S(1)} %copy.53), channel_id=1, source_target_pairs={{0,2},{2,0},{4,6},{6,4},{8,10},{10,8},{12,14},{14,12},{16,18},{18,... | collective-permute-start | bytes 786440 | tf_op jit(solution)/shard_map/ppermute | solution.py:152
  5.7 6.6 %collective-permute-start.9 = (s32[16,33]{1,0:T(8,128)S(1)}, s32[16,33]{1,0:T(8,128)S(1)}, u32[]{:S(2)}, u32[]{:S(2)}) collective-permute-start(s32[16,33]{1,0:T(8,128)S(1)} %get-tuple-element.34), channel_id=1, source_target_pairs={{0,4},{2,6},{4,8},{6,10},{8,12},{10,14},{12,16},{14,18},{16,20},{1... | collective-permute-start | bytes 6344 | tf_op jit(solution)/shard_map/ppermute | solution.py:156
  15.9 15.0 %copy-start.7 = (bf16[16,64,128]{1,2,0:T(8,128)(2,1)}, bf16[16,64,128]{1,2,0:T(8,128)(2,1)S(1)}, u32[]{:S(2)}) copy-start(bf16[16,64,128]{1,2,0:T(8,128)(2,1)S(1)} %get-tuple-element.29) | copy-start | bytes 786436
  15.9 9.6 %collective-permute-start.11 = (bf16[8,64,128]{1,2,0:T(8,128)(2,1)S(1)}, bf16[8,64,128]{1,2,0:T(8,128)(2,1)}, u32[]{:S(2)}, u32[]{:S(2)}) collective-permute-start(bf16[8,64,128]{1,2,0:T(8,128)(2,1)S(1)} %constant_dynamic-slice_fusion), channel_id=1, source_target_pairs={{0,4},{2,6},{4,8},{6,10},{8,12},{10,14},{12,16},{14,18},{16,20},{1... | collective-permute-start | bytes 393224 | tf_op jit(solution)/shard_map/ppermute | solution.py:155
  25.5 11.2 %collective-permute-start.12 = (bf16[8,64,128]{1,2,0:T(8,128)(2,1)}, bf16[8,64,128]{1,2,0:T(8,128)(2,1)}, u32[]{:S(2)}, u32[]{:S(2)}) collective-permute-start(bf16[8,64,128]{1,2,0:T(8,128)(2,1)} %collective-permute-done.11), channel_id=1, source_target_pairs={{0,2},{2,0},{4,6},{6,4},{8,10},{10,8},{12,14},{14,12},{16,18},{18,... | collective-permute-start | bytes 393224 | tf_op jit(solution)/shard_map/ppermute | solution.py:160
  30.9 1.3 copy-start.9
  34.6 0.8 copy-start.13
  35.4 4.8 %collective-permute-start.2 = (bf16[512,128]{1,0:T(8,128)(2,1)S(1)}, bf16[512,128]{1,0:T(8,128)(2,1)}, u32[]{:S(2)}, u32[]{:S(2)}) collective-permute-start(bf16[512,128]{1,0:T(8,128)(2,1)S(1)} %dynamic-slice_convert_fusion.3), channel_id=1, source_target_pairs={{0,4},{2,6},{4,0},{6,2},{8,12},{10,14},{12,8},{14,10},{16,20},{18,... | collective-permute-start | bytes 393224 | tf_op jit(solution)/shard_map/ppermute | solution.py:121
  41.2 9.2 %copy-start.8 = (bf16[16,64,128]{1,2,0:T(8,128)(2,1)S(1)}, bf16[16,64,128]{1,2,0:T(8,128)(2,1)}, u32[]{:S(2)}) copy-start(bf16[16,64,128]{1,2,0:T(8,128)(2,1)} %copy-done.7) | copy-start | bytes 786436
  41.2 5.7 %collective-permute-start.3 = (bf16[256,128]{1,0:T(8,128)(2,1)S(1)}, bf16[256,128]{1,0:T(8,128)(2,1)S(1)}, u32[]{:S(2)}, u32[]{:S(2)}) collective-permute-start(bf16[256,128]{1,0:T(8,128)(2,1)S(1)} %dynamic-slice_convert_fusion.4), channel_id=1, source_target_pairs={{0,8},{2,10},{4,12},{6,14},{8,0},{10,2},{12,4},{14,6},{16,24},{18,... | collective-permute-start | bytes 196616 | tf_op jit(solution)/shard_map/ppermute | solution.py:121
  44.3 94.3 %collective-permute-start.10 = (bf16[16,64,256]{2,1,0:T(8,128)(2,1)}, bf16[16,64,256]{2,1,0:T(8,128)(2,1)}, u32[]{:S(2)}, u32[]{:S(2)}) collective-permute-start(bf16[16,64,256]{2,1,0:T(8,128)(2,1)} %get-tuple-element.20), channel_id=1, source_target_pairs={{0,4},{2,6},{4,8},{6,10},{8,12},{10,14},{12,16},{14,18},{16,20},{1... | collective-permute-start | bytes 1572872 | tf_op jit(solution)/shard_map/ppermute | solution.py:158
  44.3 84.6 %collective-permute-start.13 = (bf16[16,64,256]{2,1,0:T(8,128)(2,1)}, bf16[16,64,256]{2,1,0:T(8,128)(2,1)}, u32[]{:S(2)}, u32[]{:S(2)}) collective-permute-start(bf16[16,64,256]{2,1,0:T(8,128)(2,1)} %get-tuple-element.19), channel_id=1, source_target_pairs={{0,4},{2,6},{4,8},{6,10},{8,12},{10,14},{12,16},{14,18},{16,20},{1... | collective-permute-start | bytes 1572872 | tf_op jit(solution)/shard_map/ppermute | solution.py:158
  46.9 72.3 %collective-permute-start.14 = (bf16[16,64,256]{2,1,0:T(8,128)(2,1)}, bf16[16,64,256]{2,1,0:T(8,128)(2,1)}, u32[]{:S(2)}, u32[]{:S(2)}) collective-permute-start(bf16[16,64,256]{2,1,0:T(8,128)(2,1)} %get-tuple-element.18), channel_id=1, source_target_pairs={{0,4},{2,6},{4,8},{6,10},{8,12},{10,14},{12,16},{14,18},{16,20},{1... | collective-permute-start | bytes 1572872 | tf_op jit(solution)/shard_map/ppermute | solution.py:158
  47.0 60.3 %collective-permute-start.15 = (bf16[16,64,256]{2,1,0:T(8,128)(2,1)}, bf16[16,64,256]{2,1,0:T(8,128)(2,1)}, u32[]{:S(2)}, u32[]{:S(2)}) collective-permute-start(bf16[16,64,256]{2,1,0:T(8,128)(2,1)} %get-tuple-element.17), channel_id=1, source_target_pairs={{0,4},{2,6},{4,8},{6,10},{8,12},{10,14},{12,16},{14,18},{16,20},{1... | collective-permute-start | bytes 1572872 | tf_op jit(solution)/shard_map/ppermute | solution.py:158
  47.0 41.9 %collective-permute-start.4 = (bf16[128,128]{1,0:T(8,128)(2,1)S(1)}, bf16[128,128]{1,0:T(8,128)(2,1)S(1)}, u32[]{:S(2)}, u32[]{:S(2)}) collective-permute-start(bf16[128,128]{1,0:T(8,128)(2,1)S(1)} %dynamic-slice_convert_fusion.6), channel_id=1, source_target_pairs={{0,16},{2,18},{4,20},{6,22},{8,24},{10,26},{12,28},{14,30},{16,0},... | collective-permute-start | bytes 98312 | tf_op jit(solution)/shard_map/ppermute | solution.py:121
  50.5 38.4 %copy-start.1 = (f32[32,64,128]{2,1,0:T(8,128)}, f32[32,64,128]{2,1,0:T(8,128)S(1)}, u32[]{:S(2)}) copy-start(f32[32,64,128]{2,1,0:T(8,128)S(1)} %broadcast_in_dim.117.acc_ref) | copy-start | bytes 3145732
  88.9 4.1 %collective-permute-start.5 = (bf16[128,128]{1,0:T(8,128)(2,1)S(1)}, bf16[128,128]{1,0:T(8,128)(2,1)S(1)}, u32[]{:S(2)}, u32[]{:S(2)}) collective-permute-start(bf16[128,128]{1,0:T(8,128)(2,1)S(1)} %add_convert_fusion.1), channel_id=1, source_target_pairs={{0,16},{2,18},{4,20},{6,22},{8,24},{10,26},{12,28},{14,30},{16,0},... | collective-permute-start | bytes 98312 | tf_op jit(solution)/shard_map/ppermute | solution.py:125
  93.1 5.9 %copy-start.14 = (bf16[256,128]{1,0:T(8,128)(2,1)}, bf16[256,128]{1,0:T(8,128)(2,1)S(1)}, u32[]{:S(2)}) copy-start(bf16[256,128]{1,0:T(8,128)(2,1)S(1)} %maximum_select_fusion.3) | copy-start | bytes 196612
  93.1 5.9 %collective-permute-start.6 = (bf16[256,128]{1,0:T(8,128)(2,1)S(1)}, bf16[256,128]{1,0:T(8,128)(2,1)}, u32[]{:S(2)}, u32[]{:S(2)}) collective-permute-start(bf16[256,128]{1,0:T(8,128)(2,1)S(1)} %maximum_select_fusion.3), channel_id=1, source_target_pairs={{0,8},{2,10},{4,12},{6,14},{8,0},{10,2},{12,4},{14,6},{16,24},{18,... | collective-permute-start | bytes 196616 | tf_op jit(solution)/shard_map/ppermute | solution.py:125
  100.0 55.7 %collective-permute-start.7 = (bf16[512,128]{1,0:T(8,128)(2,1)S(1)}, bf16[512,128]{1,0:T(8,128)(2,1)}, u32[]{:S(2)}, u32[]{:S(2)}) collective-permute-start(bf16[512,128]{1,0:T(8,128)(2,1)S(1)} %maximum_select_fusion.2), channel_id=1, source_target_pairs={{0,4},{2,6},{4,0},{6,2},{8,12},{10,14},{12,8},{14,10},{16,20},{18,... | collective-permute-start | bytes 393224 | tf_op jit(solution)/shard_map/ppermute | solution.py:125
  107.2 1.2 copy-start.2
  108.4 1.0 copy-start.6
  109.5 9.7 %copy-start.5 = (bf16[16,64,256]{2,1,0:T(8,128)(2,1)S(1)}, bf16[16,64,256]{2,1,0:T(8,128)(2,1)}, u32[]{:S(2)}) copy-start(bf16[16,64,256]{2,1,0:T(8,128)(2,1)} %get-tuple-element.22.x_ref) | copy-start | bytes 1572868
  119.2 9.7 %copy-start.4 = (bf16[16,64,256]{2,1,0:T(8,128)(2,1)S(1)}, bf16[16,64,256]{2,1,0:T(8,128)(2,1)}, u32[]{:S(2)}) copy-start(bf16[16,64,256]{2,1,0:T(8,128)(2,1)} %get-tuple-element.23.x_ref) | copy-start | bytes 1572868
  128.9 9.7 %copy-start.3 = (bf16[16,64,256]{2,1,0:T(8,128)(2,1)S(1)}, bf16[16,64,256]{2,1,0:T(8,128)(2,1)}, u32[]{:S(2)}) copy-start(bf16[16,64,256]{2,1,0:T(8,128)(2,1)} %get-tuple-element.24.x_ref) | copy-start | bytes 1572868
  149.5 6.2 %copy-start.15 = (f32[1024]{0:T(1024)S(1)}, f32[1024]{0:T(1024)}, u32[]{:S(2)}) copy-start(f32[1024]{0:T(1024)} %dynamic-slice_multiply_fusion) | copy-start | bytes 12292
  151.8 11.9 %collective-permute-start.18 = (bf16[16,64,128]{1,2,0:T(8,128)(2,1)}, bf16[16,64,128]{1,2,0:T(8,128)(2,1)}, u32[]{:S(2)}, u32[]{:S(2)}) collective-permute-start(bf16[16,64,128]{1,2,0:T(8,128)(2,1)} %negate_convert_fusion), channel_id=1, source_target_pairs={{0,2},{4,6},{8,10},{12,14},{16,18},{20,22},{24,26},{28,30},{1,3},{... | collective-permute-start | bytes 786440 | tf_op jit(solution)/shard_map/ppermute | solution.py:228
  155.7 3.1 %copy-start.10 = (bf16[16,64,1024]{2,1,0:T(8,128)(2,1)S(1)}, bf16[16,64,1024]{2,1,0:T(8,128)(2,1)}, u32[]{:S(2)}) copy-start(bf16[16,64,1024]{2,1,0:T(8,128)(2,1)} %copy-done.9) | copy-start | bytes 6291460
  155.7 3.1 %copy-start.11 = (f32[16,64,128]{1,2,0:T(8,128)S(1)}, f32[16,64,128]{1,2,0:T(8,128)}, u32[]{:S(2)}) copy-start(f32[16,64,128]{1,2,0:T(8,128)} %copy.71) | copy-start | bytes 1572868
  161.1 9.1 %collective-permute-start.16 = (bf16[16,64,128]{1,2,0:T(8,128)(2,1)S(1)}, bf16[16,64,128]{1,2,0:T(8,128)(2,1)S(1)}, u32[]{:S(2)}, u32[]{:S(2)}) collective-permute-start(bf16[16,64,128]{1,2,0:T(8,128)(2,1)S(1)} %get-tuple-element.46), channel_id=1, source_target_pairs={{0,2},{2,0},{4,6},{6,4},{8,10},{10,8},{12,14},{14,12},{16,18},{18,... | collective-permute-start | bytes 786440 | tf_op jit(solution)/shard_map/ppermute | solution.py:226
  166.3 11.1 %collective-permute-start.20 = (bf16[16,32,128]{1,2,0:T(8,128)(2,1)}, bf16[16,32,128]{1,2,0:T(8,128)(2,1)S(1)}, u32[]{:S(2)}, u32[]{:S(2)}) collective-permute-start(bf16[16,32,128]{1,2,0:T(8,128)(2,1)} %get-tuple-element.32), channel_id=1, source_target_pairs={{2,31},{3,30},{6,3},{7,2},{10,7},{11,6},{14,11},{15,10},{18,15},{1... | collective-permute-start | bytes 393224 | tf_op jit(solution)/shard_map/ppermute | solution.py:237
  168.2 15.2 %collective-permute-start.19 = (bf16[16,32,128]{1,2,0:T(8,128)(2,1)}, bf16[16,32,128]{1,2,0:T(8,128)(2,1)}, u32[]{:S(2)}, u32[]{:S(2)}) collective-permute-start(bf16[16,32,128]{1,2,0:T(8,128)(2,1)} %get-tuple-element.31), channel_id=1, source_target_pairs={{2,30},{3,31},{6,2},{7,3},{10,6},{11,7},{14,10},{15,11},{18,14},{1... | collective-permute-start | bytes 393224 | tf_op jit(solution)/shard_map/ppermute | solution.py:237
  171.4 17.5 %collective-permute-start.17 = (bf16[16,32,128]{1,2,0:T(8,128)(2,1)}, bf16[16,32,128]{1,2,0:T(8,128)(2,1)}, u32[]{:S(2)}, u32[]{:S(2)}) collective-permute-start(bf16[16,32,128]{1,2,0:T(8,128)(2,1)} %dynamic-slice_convert_fusion.2), channel_id=1, source_target_pairs={{0,1},{1,0},{2,3},{3,2},{4,5},{5,4},{6,7},{7,6},{8,9},{9,8},{10,11... | collective-permute-start | bytes 393224 | tf_op jit(solution)/shard_map/ppermute | solution.py:237

commit v2 on v0

v2 whole, which is shorter than its diff:
```python
import functools

import jax
import jax.numpy as jnp
from jax import lax
from jax.experimental import pallas as pl
from jax.experimental.pallas import tpu as pltpu
from jax.sharding import PartitionSpec as P

UNROLL = 32
F32, BF16 = jnp.float32, jnp.bfloat16
VMEM, SMEM = pltpu.VMEM, pltpu.SMEM
IN_VMEM, IN_SMEM, ANYWHERE = (pl.BlockSpec(memory_space=space) for space in (VMEM, SMEM, pl.ANY))


def pair_list(n_slot, k_slot, q, valid, q_count, length, spare):
    entries = q.shape[0]
    order = jnp.arange(entries, dtype=jnp.int32)
    qs = jnp.arange(q_count, dtype=jnp.int32)
    same = (q[:, None] == q[None, :]) & valid[None, :] & (order[None, :] < order[:, None])
    within = jnp.sum(same.astype(jnp.int32), axis=1)
    count = jnp.sum(((q[None, :] == qs[:, None]) & valid[None, :]).astype(jnp.int32), axis=1)
    padded = (count + 1) // 2 * 2
    base = jnp.sum(jnp.where(qs[None, :] < q[:, None], padded[None, :], 0), axis=1)
    place = jnp.where(valid, base + within, -1)
    code = n_slot + 64 * k_slot + 4096 * q
    blank = 64 * spare
    rows = jnp.arange(length, dtype=jnp.int32)
    listed = blank + jnp.sum(jnp.where(place[None, :] == rows[:, None], code[None, :] - blank, 0), axis=1)
    rounds = (jnp.sum(padded) + UNROLL - 1) // UNROLL
    return listed, rounds[None]


def dot_last(u, v):
    return lax.dot_general(u, v, (((1,), (1,)), ((), ())), preferred_element_type=F32)


def one_group(listed, rounds, w_ref, row, slabs, vectors, out_ref, prod, total, first):
    trials = prod.shape[1]
    width = prod.shape[2]
    slots = prod.shape[0]

    for n in range(slots):
        made = lax.dot_general(vectors(n), slabs(n), (((0,), (0,)), ((), ())), preferred_element_type=F32)
        prod[n] = made.astype(BF16)
    total[...] = jnp.zeros_like(total)

    def some(i, _):
        for d in range(0, UNROLL, 2):
            a, b = listed[i * UNROLL + d], listed[i * UNROLL + d + 1]
            both = jnp.concatenate([prod[a & 63], prod[b & 63]], axis=0)
            made = dot_last(both, w_ref[a >> 12, pl.ds(row, width), :])
            total[(a >> 6) & 63] += made[:trials]
            total[(b >> 6) & 63] += made[trials:]
        return 0

    lax.fori_loop(0, rounds[0], some, 0)
    for k in range(slots):
        made = dot_last(slabs(k), total[k].astype(BF16))

        if first:
            out_ref[k] = made
        else:
            out_ref[k] += made


def near_kernel(start, count, load, *refs):
    if load:
        core, listed, rounds, own, vec, sib, screen, out, w, prod, total, sems = refs
    else:
        core, listed, rounds, own, vec, sib, w, _, out, prod, total = refs
    half, _, _ = own.shape
    width = prod.shape[2]
    half_g = w.shape[1]
    groups = half_g // width
    own_at = core[0] * half_g

    def copy(g):
        return pltpu.make_async_copy(
            screen.at[:, pl.ds(pl.multiple_of(own_at + g * width, width), width), :],
            w.at[:, pl.ds(g * width, width), :],
            sems.at[g],
        )

    if load:
        for g in range(groups):
            copy(g).start()
    for g in range(start, start + count):
        if load:
            copy(g).wait()
        at = pl.multiple_of(own_at + g * width, width)

        def slabs(n, at=at, g=g):
            return own[n, :, pl.ds(at, width)] if n < half else sib[n - half, :, g * width : (g + 1) * width]

        def vectors(n):
            return vec[n] if n < half else sib[n - half, :, half_g:]

        one_group(listed, rounds, w, g * width, slabs, vectors, out, prod, total, load and g == start)
    if load:
        for g in range(start + count, groups):
            copy(g).wait()


def far_kernel(start, count, fresh, core, listed, rounds, own, vec, sib, w, came0, came1, vec_p, *refs):
    if fresh:
        out, prod, total, came, sem = refs
    else:
        _, out, prod, total, came, sem = refs
    half, _, _ = own.shape
    width = prod.shape[2]
    half_g = w.shape[1]
    own_at = core[0] * half_g

    @pl.when(core[0] == 0)
    def _():
        pltpu.make_async_copy(came0.at[:, :, : count * width], came, sem).start()

    @pl.when(core[0] != 0)
    def _():
        pltpu.make_async_copy(came1.at[:, :, : count * width], came, sem).start()

    pltpu.make_async_copy(came0.at[:, :, : count * width], came, sem).wait()
    for g in range(start, start + count):
        at = pl.multiple_of(own_at + g * width, width)

        def slabs(n, at=at, g=g):
            if n >= half:
                return came[n - half, :, (g - start) * width : (g - start + 1) * width]
            return jnp.where(
                core[0] == 0, own[n, :, pl.ds(at, width)], sib[n, :, g * width : (g + 1) * width]
            )

        def vectors(n):
            if n >= half:
                return vec_p[n - half]
            return jnp.where(core[0] == 0, vec[n], sib[n, :, half_g:])

        one_group(listed, rounds, w, g * width, slabs, vectors, out, prod, total, fresh and g == start)


def last_kernel(core, own, sib, s2, near, far, give, keep):
    half, pairs, _ = own.shape
    trials, half_g = s2.shape
    width = 256
    own_at = core[0] * half_g

    def exchange(slab):
        acc = jnp.zeros((half * pairs, trials), F32)
        for g in range(half_g // width):
            acc += dot_last(slab(g).reshape(half * pairs, width), s2[:, g * width : (g + 1) * width])
        return acc.reshape(half, pairs, trials)

    mine = exchange(lambda g: own[:, :, pl.ds(pl.multiple_of(own_at + g * width, width), width)]) - near[:half]
    other = exchange(lambda g: sib[:, :, g * width : (g + 1) * width]) - near[half:]

    @pl.when(core[0] == 0)
    def _():
        keep[:half] = mine - far[:half]
        keep[half:] = other
        give[:half] = (-far[half:]).astype(BF16)
        give[half:] = other.astype(BF16)

    @pl.when(core[0] != 0)
    def _():
        keep[:half] = -far[half:]
        keep[half:] = mine
        give[:half] = (other - far[:half]).astype(BF16)
        give[half:] = mine.astype(BF16)


def density_sum(part, me, size):
    columns = part.shape[1] // 2
    swap = lambda v, bit: lax.ppermute(v, "ka", [(i, i ^ bit) for i in range(size)])
    high = (me // 2) % 2
    keep = lax.dynamic_slice_in_dim(part, high * columns, columns, 1)
    give = lax.dynamic_slice_in_dim(part, (1 - high) * columns, columns, 1).astype(BF16)
    part = keep + swap(give, 2).astype(F32)
    bit = 4
    while bit < size:
        part = part + swap(part.astype(BF16), bit).astype(F32)
        bit *= 2
    part = part.astype(BF16)
    other = swap(part, 2)
    return jnp.where(high == 0, jnp.concatenate([part, other], 1), jnp.concatenate([other, part], 1))


def on_device(pair_density, trial_vectors, energy, coulomb, screen, neighbors, live_count, q_index):
    local_k, pair_count, local_g = pair_density.shape
    trial_count = trial_vectors.shape[2]
    q_count, _, width = screen.shape
    slots = neighbors.shape[1]
    size, parts = lax.axis_size("ka"), lax.axis_size("ga")
    me, mine = lax.axis_index("ka"), lax.axis_index("ga")
    core = me % 2
    core_id = core.astype(jnp.int32)[None]
    half_g = local_g // 2
    groups = half_g // width
    first_block = me - core
    sibling = [(i, i ^ 1) for i in range(size)]
    onward = [(i, (i + 2) % size) for i in range(size)]
    chunk_count = 2 if groups % 2 == 0 else 1
    chunk_groups = groups // chunk_count
    chunk = chunk_groups * width

    table = jnp.concatenate([neighbors, q_index, live_count[:, None]], axis=1)
    table_s = lax.ppermute(table, "ka", sibling)
    give_half = lax.dynamic_slice_in_dim(pair_density, (1 - core) * half_g, half_g, 2)
    sib = lax.ppermute(jnp.concatenate([give_half, trial_vectors], 2), "ka", sibling)
    came = []
    for c in range(chunk_count):
        pieces = []
        for target in range(2):
            piece = lax.slice_in_dim(
                pair_density, target * half_g + c * chunk, target * half_g + (c + 1) * chunk, axis=2
            )
            if c == 0:
                piece = jnp.concatenate([piece, trial_vectors], 2)
            pieces.append(
                lax.ppermute(piece, "ka", [(i, (i + 1 + target) % size) for i in range(1, size, 2)])
            )
        came.append(pieces)
    table_a = jnp.where(core == 0, table, table_s)
    table_b = jnp.where(core == 0, table_s, table)
    table_p = lax.ppermute(table_b, "ka", onward)

    own_half = lax.dynamic_slice_in_dim(pair_density, core * half_g, half_g, 2)
    contract = lambda v, d: lax.dot_general(v, d, (((0, 1), (0, 1)), ((), ())), preferred_element_type=F32)
    part = contract(trial_vectors, own_half) + contract(sib[:, :, half_g:], sib[:, :, :half_g])
    density_total = density_sum(part, me, size)
    my_coulomb = lax.dynamic_slice_in_dim(coulomb, core * half_g, half_g, 0)
    screened2 = (2.0 * my_coulomb[None, :] * density_total.astype(F32)).astype(BF16)

    def columns(t):
        live = jnp.arange(slots, dtype=jnp.int32)[None, :] < t[:, 2 * slots :]
        near = t[:, :slots]
        return near // local_k, near % local_k, t[:, slots : 2 * slots], live

    row = jnp.broadcast_to(jnp.arange(local_k, dtype=jnp.int32)[:, None], (local_k, slots))
    flat = lambda u, v: jnp.concatenate([u.reshape(-1), v.reshape(-1)])
    other_block = me + 1 - 2 * core
    before = (first_block + size - 1) % size
    length = 2 * local_k * slots + q_count
    length = (length + UNROLL - 1) // UNROLL * UNROLL

    def listing(u, v, u_slot, v_slot, u_valid, v_valid):
        return pair_list(
            flat(u_slot, v_slot),
            flat(row, row + local_k),
            flat(u[2], v[2]),
            flat(u[3] & u_valid, v[3] & v_valid),
            q_count,
            length,
            2 * local_k,
        )

    own_t, sib_t, a_t, p_t = columns(table), columns(table_s), columns(table_a), columns(table_p)
    here = lambda blk: (blk == me) | (blk == other_block)
    near_list, near_rounds = listing(
        own_t,
        sib_t,
        own_t[1] + local_k * (own_t[0] == other_block),
        sib_t[1] + local_k * (sib_t[0] == other_block),
        here(own_t[0]),
        here(sib_t[0]),
    )
    far_list, far_rounds = listing(
        a_t, p_t, a_t[1] + local_k, p_t[1], a_t[0] == before, p_t[0] == first_block
    )

    sums = jax.ShapeDtypeStruct((2 * local_k, pair_count, trial_count), F32)
    work = [
        VMEM((2 * local_k, trial_count, width), BF16),
        VMEM((2 * local_k + 1, trial_count, width), F32),
    ]

    def params():
        return pltpu.CompilerParams(vmem_limit_bytes=20 << 20)

    def cost(count, pairs):
        return pl.CostEstimate(
            flops=4 * count * pairs * width * width * trial_count, transcendentals=0, bytes_accessed=1 << 20
        )

    near_groups = (groups + 1) // 2
    near, w_half = pl.pallas_call(
        functools.partial(near_kernel, 0, near_groups, True),
        out_shape=(sums, jax.ShapeDtypeStruct((q_count, half_g, width), BF16)),
        in_specs=[IN_SMEM, IN_SMEM, IN_SMEM, IN_VMEM, IN_VMEM, IN_VMEM, ANYWHERE],
        out_specs=(IN_VMEM, IN_VMEM),
        scratch_shapes=work + [pltpu.SemaphoreType.DMA((groups,))],
        compiler_params=params(),
        cost_estimate=cost(near_groups, 160),
    )(core_id, near_list, near_rounds, pair_density, trial_vectors, sib, screen)
    if groups > near_groups:
        near = pl.pallas_call(
            functools.partial(near_kernel, near_groups, groups - near_groups, False),
            out_shape=sums,
            in_specs=[IN_SMEM, IN_SMEM, IN_SMEM, IN_VMEM, IN_VMEM, IN_VMEM, IN_VMEM, IN_VMEM],
            out_specs=IN_VMEM,
            scratch_shapes=work,
            input_output_aliases={7: 0},
            compiler_params=params(),
            cost_estimate=cost(groups - near_groups, 160),
        )(core_id, near_list, near_rounds, pair_density, trial_vectors, sib, w_half, near)
    vec_p = jnp.where(core == 0, came[0][0][:, :, chunk:], came[0][1][:, :, chunk:])
    far = None
    for c in range(chunk_count):
        far = pl.pallas_call(
            functools.partial(far_kernel, c * chunk_groups, chunk_groups, c == 0),
            out_shape=sums,
            in_specs=[IN_SMEM, IN_SMEM, IN_SMEM, IN_VMEM, IN_VMEM, IN_VMEM, IN_VMEM, ANYWHERE, ANYWHERE, IN_VMEM]
            + [IN_VMEM] * (c > 0),
            out_specs=IN_VMEM,
            scratch_shapes=work + [VMEM((local_k, pair_count, chunk), BF16), pltpu.SemaphoreType.DMA],
            input_output_aliases={10: 0} if c else {},
            compiler_params=params(),
            cost_estimate=cost(chunk_groups, 80),
        )(
            core_id, far_list, far_rounds, pair_density, trial_vectors, sib, w_half, came[c][0], came[c][1], vec_p,
            *([far] if c else []),
        )
    give, keep = pl.pallas_call(
        last_kernel,
        out_shape=(jax.ShapeDtypeStruct(sums.shape, BF16), sums),
        in_specs=[IN_SMEM] + [IN_VMEM] * 5,
        out_specs=(IN_VMEM, IN_VMEM),
        compiler_params=params(),
        cost_estimate=cost(1, 16),
    )(core_id, pair_density, sib, screened2, near, far)

    both = keep + lax.ppermute(give, "ka", sibling).astype(F32)
    edge, inner = both[:local_k], both[local_k:]
    rows = pair_count // parts
    rows_of = lambda value, at: lax.dynamic_slice_in_dim(value, at * rows, rows, 1)
    stay = lambda first: [(i, i) for i in range(first, size, 2)]
    back = [(i, (i - 2) % size) for i in range(1, size, 2)]

    def sent(value, steps, ka_pairs):
        pairs = [
            (s * parts + g, d * parts + (g + steps) % parts) for s, d in ka_pairs for g in range(parts)
        ]
        return lax.ppermute(
            rows_of(value, (mine + steps) % parts).astype(BF16), ("ka", "ga"), pairs
        ).astype(F32)

    answer = jnp.where(core == 0, rows_of(edge, mine), rows_of(inner, mine))
    answer = answer + sent(edge, 0, back)
    for steps in range(1, parts):
        answer = answer + sent(edge, steps, stay(0) + back) + sent(inner, steps, stay(1))
    energy_rows = lax.dynamic_slice_in_dim(energy, mine * rows, rows, 1)
    vector_rows = lax.dynamic_slice_in_dim(trial_vectors, mine * rows, rows, 1)
    return (energy_rows[:, :, None] * vector_rows.astype(F32) + answer).astype(BF16)


def solution(mesh):
    in_specs = (
        P("ka", None, "ga"),
        P("ka", None, None),
        P("ka", None),
        P("ga"),
        P(None, "ga", None),
        P("ka", None),
        P("ka"),
        P("ka", None),
    )
    out_specs = P("ka", "ga", None)
    return jax.shard_map(
        on_device, mesh=mesh, in_specs=in_specs, out_specs=out_specs, check_vma=False
    )
```

time: 1170 us -> 150 us (0.13)
  local copies, waits for them, and re-layouts: 405 us -> 9.54 us
  other arithmetic: 302 us -> 10.6 us
  matrix products: 245 us -> 2.56 us
  waiting for transfers between devices: 202 us -> 50.1 us
  Pallas kernels: 0 us -> 53.9 us
  starting transfers between devices: 2.65 us -> 19.7 us
  between operations: 13.5 us -> 1.78 us
    gather x32 -> x0, local copies, waits for them, and re-layouts: 403 us -> none  [the longest x16 208 us: add_slot(): picked = jnp.take(window, local_index[:, slot_index], axis=0)]
    add x17 -> x5, other arithmetic: 279 us -> 1.4 us  [the longest x1 1.38 us: on_device(): both = keep + lax.ppermute(give, 'ka', sibling).astype(F32)]
    dot_general x18 -> x2, matrix products: 245 us -> 2.56 us  [on_device(): lax.dot_general(v, d, (((0, 1), (0, 1)), ((), ())), preferred_element_typ...]
    psum x1 -> x0, waiting for transfers between devices: 167 us -> none  [on_device(): density_total = lax.psum(partial_value, 'ka')]
    pallas_call x0 -> x5, Pallas kernels: none -> 53.9 us  [the longest x2 21.1 us: on_device(): pl.pallas_call(functools.partial(far_kernel, c * chunk_groups, chunk_grou...]
    ppermute x2 -> x15, waiting for transfers between devices: 19.6 us -> 50.1 us  [the longest x1 28 us: on_device(): table_p = lax.ppermute(table_b, 'ka', onward)]
    ppermute x2 -> x15, starting transfers between devices: 2.6 us -> 19.7 us  [the longest x4 11.4 us: on_device(): lax.ppermute(piece, 'ka', [(i, (i + 1 + target) % size) for i in range(1,...]
    reduce_scatter x1 -> x0, waiting for transfers between devices: 15.6 us -> none  [on_device(): mine = lax.psum_scatter(pair_terms, 'ga', scatter_dimension=1, tiled=True)]
  transfers between devices with their start and end apart: 4 -> 15, of which waited for: 4 -> 6; matrix products, arithmetic and copies ran while one was open for 0% -> 11% of each run, Pallas kernels for 0% -> 35%
where the time goes in v2:
time: 150 us; the launch traced here: 148 us
  Pallas kernels  53.9 us (36%)
  waiting for transfers between devices  50.1 us (33%)
  starting transfers between devices  19.7 us (13%)
  other arithmetic  10.6 us (7%)
  local copies, waits for them, and re-layouts  9.54 us (6%)
  matrix products  2.56 us (2%)
  between operations  1.78 us (1%)
    ppermute x1, waiting for transfers between devices, on_device(): table_p = lax.ppermute(table_b, 'ka', onward)  28 us
    pallas_call x2, Pallas kernels, on_device(): pl.pallas_call(functools.partial(far_kernel, c * chunk_groups, chunk_grou...  21.1 us
    pallas_call x1, Pallas kernels, on_device(): pl.pallas_call(functools.partial(near_kernel, 0, near_groups, True), out_...  16.9 us
    ppermute x4, waiting for transfers between devices, on_device(): lax.ppermute(piece, 'ka', [(i, (i + 1 + target) % size) for i in range(1,...  15.6 us
    pallas_call x1, Pallas kernels, on_device(): pl.pallas_call(functools.partial(near_kernel, near_groups, groups - near_...  14.5 us
    ppermute x4, starting transfers between devices, on_device(): lax.ppermute(piece, 'ka', [(i, (i + 1 + target) % size) for i in range(1,...  11.4 us
    ppermute x3, starting transfers between devices, sent(): lax.ppermute(rows_of(value, (mine + steps) % parts).astype(BF16), ('ka',...  6.3 us
    ppermute x3, waiting for transfers between devices, sent(): lax.ppermute(rows_of(value, (mine + steps) % parts).astype(BF16), ('ka',...  4.62 us
  transfers between devices with their start and end apart: 15, of which 6 were waited for; matrix products, arithmetic and copies ran while one was open for 11% of the time, Pallas kernels for 35%

profile of v2, /device:TPU:1, one launch (start us, length us, event | category | flops | bytes accessed | tf_op | source)
XLA Modules:
  0.0 148.2 jit_solution(9208256464355295475)
XLA Ops:
  0.0 0.7 copy.16
  0.7 0.8 pad_add_fusion
  1.6 1.9 %constant_dynamic-slice_fusion = bf16[16,64,1024]{2,1,0:T(8,128)(2,1)S(1)} fusion(bf16[16,64,2048]{2,1,0:T(8,128)(2,1)} %own.5, s32[]{:T(128)S(6)} %select_n.177), kind=kLoop, calls=%fused_computation.106 | loop fusion | bytes 4194308 | tf_op jit(solution)/shard_map/dynamic_slice | solution.py:208
  3.5 1.7 %pad_maximum_fusion = bf16[16,64,1152]{2,1,0:T(8,128)(2,1)} fusion(bf16[16,64,128]{2,1,0:T(8,128)(2,1)S(1)} %copy-done.3, bf16[16,64,1024]{2,1,0:T(8,128)(2,1)S(1)} %constant_dynamic-slice_fusion), kind=kLoop, calls=%fused_computation | loop fusion | flops 4718592 | bytes 4718592 | tf_op jit(solution)/shard_map/concatenate | solution.py:209
  5.2 0.5 collective-permute-start
  5.6 0.9 copy-done.1
  6.5 2.0 %fusion.48 = (bf16[16,64,512]{2,1,0:T(8,128)(2,1)S(1)}, bf16[16,64,512]{2,1,0:T(8,128)(2,1)S(1)}, bf16[16,64,512]{2,1,0:T(8,128)(2,1)}, bf16[16,64,512]{2,1,0:T(8,128)(2,1)}) fusion(bf16[16,64,2048]{2,1,0:T(8,128)(2,1)S(1)} %copy-done.1), kind=kLoop, calls=%fused_computation.132 | loop fusion | bytes 8388608 | tf_op jit(solution)/shard_map/slice | solution.py:214
  8.5 4.6 %collective-permute-start.8 = (bf16[16,64,512]{2,1,0:T(8,128)(2,1)}, bf16[16,64,512]{2,1,0:T(8,128)(2,1)}, u32[]{:S(2)}, u32[]{:S(2)}) collective-permute-start(bf16[16,64,512]{2,1,0:T(8,128)(2,1)} %get-tuple-element.25), channel_id=1, source_target_pairs={{2,6},{6,10},{10,14},{14,18},{18,22},{22,26},{26,30},{30,2},{3,7},... | collective-permute-start | bytes 3145736 | tf_op jit(solution)/shard_map/ppermute | solution.py:220
  13.1 2.5 %collective-permute-start.7 = (bf16[16,64,512]{2,1,0:T(8,128)(2,1)}, bf16[16,64,512]{2,1,0:T(8,128)(2,1)}, u32[]{:S(2)}, u32[]{:S(2)}) collective-permute-start(bf16[16,64,512]{2,1,0:T(8,128)(2,1)} %get-tuple-element.26), channel_id=1, source_target_pairs={{2,4},{6,8},{10,12},{14,16},{18,20},{22,24},{26,28},{30,0},{3,5},{... | collective-permute-start | bytes 3145736 | tf_op jit(solution)/shard_map/ppermute | solution.py:220
  15.6 1.8 %pad_maximum_fusion.2 = (bf16[16,64,640]{2,1,0:T(8,128)(2,1)}, bf16[16,64,640]{2,1,0:T(8,128)(2,1)}) fusion(bf16[16,64,128]{2,1,0:T(8,128)(2,1)S(1)} %copy-done.3, bf16[16,64,512]{2,1,0:T(8,128)(2,1)S(1)} %get-tuple-element.23, bf16[16,64,512]{2,1,0:T(8,128)(2,1)S(1)} %get-tuple-element.24), kind=kLoop, calls=%fused_computation.6 | loop fusion | flops 4587520 | bytes 4980736 | tf_op jit(solution)/shard_map/concatenate | solution.py:218
  17.5 2.4 %collective-permute-start.9 = (bf16[16,64,640]{2,1,0:T(8,128)(2,1)}, bf16[16,64,640]{2,1,0:T(8,128)(2,1)}, u32[]{:S(2)}, u32[]{:S(2)}) collective-permute-start(bf16[16,64,640]{2,1,0:T(8,128)(2,1)} %get-tuple-element.31), channel_id=1, source_target_pairs={{2,4},{6,8},{10,12},{14,16},{18,20},{22,24},{26,28},{30,0},{3,5},{... | collective-permute-start | bytes 3932168 | tf_op jit(solution)/shard_map/ppermute | solution.py:220
  20.1 2.1 %fusion.4 = f32[128,1024]{1,0:T(8,128)S(1)} fusion(bf16[16,64,128]{2,1,0:T(8,128)(2,1)S(1)} %copy-done.3, bf16[16,64,2048]{2,1,0:T(8,128)(2,1)} %own.5, s32[]{:T(128)S(6)} %select_n.178), kind=kOutput, calls=%fused_computation.7 | convolution fusion | flops 268435456 | bytes 2883588 | tf_op jit(solution)/shard_map/dot_general | solution.py:228
  22.7 0.2 dynamic-update-slice.6
  22.9 0.2 slice_reduce_fusion.2
  23.4 0.2 dynamic-update-slice.7
  23.7 0.1 convert_reduce_fusion.3
  23.8 0.3 convert_reduce_fusion.1
  24.1 0.2 slice_reduce_fusion.1
  24.6 1.3 collective-permute-start.6
  26.1 0.2 dynamic-update-slice.2
  26.3 28.0 %collective-permute-done.6 = s32[16,33]{1,0:T(8,128)S(1)} collective-permute-done((s32[16,33]{1,0:T(8,128)S(1)}, s32[16,33]{1,0:T(8,128)S(1)}, u32[]{:S(2)}, u32[]{:S(2)}) %collective-permute-start.6) | collective-permute-done | bytes 2144 | tf_op jit(solution)/shard_map/ppermute | solution.py:225
  54.3 1.9 %collective-permute-start.10 = (bf16[16,64,640]{2,1,0:T(8,128)(2,1)}, bf16[16,64,640]{2,1,0:T(8,128)(2,1)}, u32[]{:S(2)}, u32[]{:S(2)}) collective-permute-start(bf16[16,64,640]{2,1,0:T(8,128)(2,1)} %get-tuple-element.32), channel_id=1, source_target_pairs={{2,6},{6,10},{10,14},{14,18},{18,22},{22,26},{26,30},{30,2},{3,7},... | collective-permute-start | bytes 3932168 | tf_op jit(solution)/shard_map/ppermute | solution.py:220
  56.2 0.2 slice_reduce_fusion
  56.7 0.2 dynamic-update-slice.3
  56.9 0.1 convert_reduce_fusion.2
  57.1 0.7 fusion.44
  59.3 0.2 select_reduce_fusion.1
  59.5 0.3 convert_reduce_fusion
  59.8 0.2 select_reduce_fusion
  60.1 15.6 %collective-permute-done.10.came1 = bf16[16,64,640]{2,1,0:T(8,128)(2,1)} collective-permute-done((bf16[16,64,640]{2,1,0:T(8,128)(2,1)}, bf16[16,64,640]{2,1,0:T(8,128)(2,1)}, u32[]{:S(2)}, u32[]{:S(2)}) %collective-permute-start.10) | collective-permute-done | bytes 1310752 | tf_op jit(solution)/shard_map/ppermute | solution.py:220
  75.7 1.1 slice_select_fusion.vec_p
  76.8 0.5 fusion.10
  77.4 16.9 %shard_map.82 = (f32[32,64,128]{2,1,0:T(8,128)S(1)}, bf16[32,1024,256]{2,1,0:T(8,128)(2,1)S(1)}) custom-call(s32[1]{0:T(128)} %bitcast.refs_0_.core, s32[544]{0:T(1024)S(1)} %broadcast_add_fusion.1.refs_1_, s32[1]{0:T(128)} %bitcast.5.refs_2_, bf16[16,64,2048]{2,1,0:T(8,128)(2,1)S(1)} %copy-done.2, bf16[16,64,128]{2,1,0:T(8,128)(2,1)S(1)} %copy-done.3, ...), custom_call_target="tpu_custom_call" | custom-call | flops 10737418240 | bytes 1048576 | tf_op jit(solution)/shard_map/pallas_call | solution.py:286
  94.4 14.5 %shard_map.83.near = f32[32,64,128]{2,1,0:T(8,128)S(1)} custom-call(s32[1]{0:T(128)} %bitcast.refs_0_.core, s32[544]{0:T(1024)S(1)} %broadcast_add_fusion.1.refs_1_, s32[1]{0:T(128)} %bitcast.5.refs_2_, bf16[16,64,2048]{2,1,0:T(8,128)(2,1)S(1)} %copy-done.2, bf16[16,64,128]{2,1,0:T(8,128)(2,1)S(1)} %copy-done.3, ...), custom_call_target="tpu_custom_call", output_to_operand_aliasing={{}: (7, {})} | custom-call | flops 10737418240 | bytes 1048576 | tf_op jit(solution)/shard_map/pallas_call | solution.py:296
  109.1 10.4 %shard_map.84.refs_0_ = f32[32,64,128]{2,1,0:T(8,128)S(1)} custom-call(s32[1]{0:T(128)} %bitcast.refs_0_.core, s32[544]{0:T(1024)S(1)} %broadcast_add_fusion.listed, s32[1]{0:T(128)} %bitcast.6.rounds, bf16[16,64,2048]{2,1,0:T(8,128)(2,1)S(1)} %copy-done.2, bf16[16,64,128]{2,1,0:T(8,128)(2,1)S(1)} %copy-done.3, ...), custom_call_target="tpu_custom_call" | custom-call | flops 5368709120 | bytes 1048576 | tf_op jit(solution)/shard_map/pallas_call | solution.py:309
  119.7 10.7 %shard_map.85.far = f32[32,64,128]{2,1,0:T(8,128)S(1)} custom-call(s32[1]{0:T(128)} %bitcast.refs_0_.core, s32[544]{0:T(1024)S(1)} %broadcast_add_fusion.listed, s32[1]{0:T(128)} %bitcast.6.rounds, bf16[16,64,2048]{2,1,0:T(8,128)(2,1)S(1)} %copy-done.2, bf16[16,64,128]{2,1,0:T(8,128)(2,1)S(1)} %copy-done.3, ...), custom_call_target="tpu_custom_call", output_to_operand_aliasing={{}: (10, {})} | custom-call | flops 5368709120 | bytes 1048576 | tf_op jit(solution)/shard_map/pallas_call | solution.py:309
  130.4 0.1 multiply_convert_fusion.s2
  130.5 1.4 shard_map.86
  131.9 1.0 copy-done.4
  132.9 1.9 %collective-permute-done.11 = bf16[32,64,128]{2,1,0:T(8,128)(2,1)S(1)} collective-permute-done((bf16[32,64,128]{2,1,0:T(8,128)(2,1)S(1)}, bf16[32,64,128]{2,1,0:T(8,128)(2,1)S(1)}, u32[]{:S(2)}, u32[]{:S(2)}) %collective-permute-start.11) | collective-permute-done | bytes 524320 | tf_op jit(solution)/shard_map/ppermute | solution.py:332
  134.8 1.4 convert_add_fusion
  136.2 0.1 fusion.49
  136.4 3.1 %collective-permute-start.14 = (bf16[16,32,128]{2,1,0:T(8,128)(2,1)S(1)}, bf16[16,32,128]{2,1,0:T(8,128)(2,1)S(1)}, u32[]{:S(2)}, u32[]{:S(2)}) collective-permute-start(bf16[16,32,128]{2,1,0:T(8,128)(2,1)S(1)} %dynamic-slice_convert_fusion), channel_id=1, source_target_pairs={{2,3},{3,2},{6,7},{7,6},{10,11},{11,10},{14,15},{15,14},{18,19},{1... | collective-permute-start | bytes 393224 | tf_op jit(solution)/shard_map/ppermute | solution.py:343
  139.6 3.1 %collective-permute-start.12 = (bf16[16,32,128]{2,1,0:T(8,128)(2,1)S(1)}, bf16[16,32,128]{2,1,0:T(8,128)(2,1)S(1)}, u32[]{:S(2)}, u32[]{:S(2)}) collective-permute-start(bf16[16,32,128]{2,1,0:T(8,128)(2,1)S(1)} %get-tuple-element.29), channel_id=1, source_target_pairs={{2,30},{3,31},{6,2},{7,3},{10,6},{11,7},{14,10},{15,11},{18,14},{1... | collective-permute-start | bytes 393224 | tf_op jit(solution)/shard_map/ppermute | solution.py:343
  142.8 0.8 collective-permute-done.14
  143.6 1.7 %collective-permute-done.12 = bf16[16,32,128]{2,1,0:T(8,128)(2,1)S(1)} collective-permute-done((bf16[16,32,128]{2,1,0:T(8,128)(2,1)S(1)}, bf16[16,32,128]{2,1,0:T(8,128)(2,1)S(1)}, u32[]{:S(2)}, u32[]{:S(2)}) %collective-permute-start.12) | collective-permute-done | bytes 131104 | tf_op jit(solution)/shard_map/ppermute | solution.py:343
  145.3 2.2 %collective-permute-done.13 = bf16[16,32,128]{2,1,0:T(8,128)(2,1)S(1)} collective-permute-done((bf16[16,32,128]{2,1,0:T(8,128)(2,1)S(1)}, bf16[16,32,128]{2,1,0:T(8,128)(2,1)S(1)}, u32[]{:S(2)}, u32[]{:S(2)}) %collective-permute-start.13) | collective-permute-done | bytes 131104 | tf_op jit(solution)/shard_map/ppermute | solution.py:343
  147.4 0.8 add_convert_fusion
  (81 shorter events, 3.0 us)
Async XLA Ops:
  0.0 142.7 %copy-start = (f32[16,64]{1,0:T(8,128)S(1)}, f32[16,64]{1,0:T(8,128)}, u32[]{:S(2)}) copy-start(f32[16,64]{1,0:T(8,128)} %param.10) | copy-start | bytes 12292
  1.5 21.4 %collective-permute-start.5 = (s32[16,33]{1,0:T(8,128)S(1)}, s32[16,33]{1,0:T(8,128)S(1)}, u32[]{:S(2)}, u32[]{:S(2)}) collective-permute-start(s32[16,33]{1,0:T(8,128)S(1)} %pad_add_fusion), channel_id=1, source_target_pairs={{0,2},{2,0},{4,6},{6,4},{8,10},{10,8},{12,14},{14,12},{16,18},{18,... | collective-permute-start | bytes 6344 | tf_op jit(solution)/shard_map/ppermute | solution.py:207
  1.6 1.9 %copy-start.3 = (bf16[16,64,128]{2,1,0:T(8,128)(2,1)S(1)}, bf16[16,64,128]{2,1,0:T(8,128)(2,1)}, u32[]{:S(2)}) copy-start(bf16[16,64,128]{2,1,0:T(8,128)(2,1)} %vec.3) | copy-start | bytes 786436
  3.5 3.0 %copy-start.1 = (bf16[16,64,2048]{2,1,0:T(8,128)(2,1)S(1)}, bf16[16,64,2048]{2,1,0:T(8,128)(2,1)}, u32[]{:S(2)}) copy-start(bf16[16,64,2048]{2,1,0:T(8,128)(2,1)} %own.5) | copy-start | bytes 12582916
  5.2 71.6 %collective-permute-start = (bf16[16,64,1152]{2,1,0:T(8,128)(2,1)}, bf16[16,64,1152]{2,1,0:T(8,128)(2,1)S(1)}, u32[]{:S(2)}, u32[]{:S(2)}) collective-permute-start(bf16[16,64,1152]{2,1,0:T(8,128)(2,1)} %pad_maximum_fusion), channel_id=1, source_target_pairs={{0,2},{2,0},{4,6},{6,4},{8,10},{10,8},{12,14},{14,12},{16,18},{18,... | collective-permute-start | bytes 7077896 | tf_op jit(solution)/shard_map/ppermute | solution.py:209
  8.5 111.1 %collective-permute-start.8 = (bf16[16,64,512]{2,1,0:T(8,128)(2,1)}, bf16[16,64,512]{2,1,0:T(8,128)(2,1)}, u32[]{:S(2)}, u32[]{:S(2)}) collective-permute-start(bf16[16,64,512]{2,1,0:T(8,128)(2,1)} %get-tuple-element.25), channel_id=1, source_target_pairs={{2,6},{6,10},{10,14},{14,18},{18,22},{22,26},{26,30},{30,2},{3,7},... | collective-permute-start | bytes 3145736 | tf_op jit(solution)/shard_map/ppermute | solution.py:220
  13.1 106.6 %collective-permute-start.7 = (bf16[16,64,512]{2,1,0:T(8,128)(2,1)}, bf16[16,64,512]{2,1,0:T(8,128)(2,1)}, u32[]{:S(2)}, u32[]{:S(2)}) collective-permute-start(bf16[16,64,512]{2,1,0:T(8,128)(2,1)} %get-tuple-element.26), channel_id=1, source_target_pairs={{2,4},{6,8},{10,12},{14,16},{18,20},{22,24},{26,28},{30,0},{3,5},{... | collective-permute-start | bytes 3145736 | tf_op jit(solution)/shard_map/ppermute | solution.py:220
  15.6 4.2 %copy-start.6 = (s32[16,16]{1,0:T(8,128)S(1)}, s32[16,16]{1,0:T(8,128)}, u32[]{:S(2)}) copy-start(s32[16,16]{1,0:T(8,128)} %param.15) | copy-start | bytes 3076
  15.6 4.3 %copy-start.5 = (s32[16,16]{1,0:T(8,128)S(1)}, s32[16,16]{1,0:T(8,128)}, u32[]{:S(2)}) copy-start(s32[16,16]{1,0:T(8,128)} %param.13) | copy-start | bytes 3076
  15.6 4.3 %copy-start.7 = (s32[16]{0:T(128)S(1)}, s32[16]{0:T(128)}, u32[]{:S(2)}) copy-start(s32[16]{0:T(128)} %param.14) | copy-start | bytes 196
  17.5 42.6 %collective-permute-start.9 = (bf16[16,64,640]{2,1,0:T(8,128)(2,1)}, bf16[16,64,640]{2,1,0:T(8,128)(2,1)}, u32[]{:S(2)}, u32[]{:S(2)}) collective-permute-start(bf16[16,64,640]{2,1,0:T(8,128)(2,1)} %get-tuple-element.31), channel_id=1, source_target_pairs={{2,4},{6,8},{10,12},{14,16},{18,20},{22,24},{26,28},{30,0},{3,5},{... | collective-permute-start | bytes 3932168 | tf_op jit(solution)/shard_map/ppermute | solution.py:220
  20.1 2.1 %copy-start.8 = (f32[2048]{0:T(1024)S(1)}, f32[2048]{0:T(1024)}, u32[]{:S(2)}) copy-start(f32[2048]{0:T(1024)} %param.11) | copy-start | bytes 24580
  24.6 29.7 %collective-permute-start.6 = (s32[16,33]{1,0:T(8,128)S(1)}, s32[16,33]{1,0:T(8,128)S(1)}, u32[]{:S(2)}, u32[]{:S(2)}) collective-permute-start(s32[16,33]{1,0:T(8,128)S(1)} %get-tuple-element.34), channel_id=1, source_target_pairs={{0,4},{2,6},{4,8},{6,10},{8,12},{10,14},{12,16},{14,18},{16,20},{1... | collective-permute-start | bytes 6344 | tf_op jit(solution)/shard_map/ppermute | solution.py:225
  54.3 21.4 %collective-permute-start.10 = (bf16[16,64,640]{2,1,0:T(8,128)(2,1)}, bf16[16,64,640]{2,1,0:T(8,128)(2,1)}, u32[]{:S(2)}, u32[]{:S(2)}) collective-permute-start(bf16[16,64,640]{2,1,0:T(8,128)(2,1)} %get-tuple-element.32), channel_id=1, source_target_pairs={{2,6},{6,10},{10,14},{14,18},{18,22},{22,26},{26,30},{30,2},{3,7},... | collective-permute-start | bytes 3932168 | tf_op jit(solution)/shard_map/ppermute | solution.py:220
  60.0 17.3 %copy-start.2 = (bf16[16,64,2048]{2,1,0:T(8,128)(2,1)S(1)}, bf16[16,64,2048]{2,1,0:T(8,128)(2,1)}, u32[]{:S(2)}) copy-start(bf16[16,64,2048]{2,1,0:T(8,128)(2,1)} %own.5) | copy-start | bytes 12582916
  77.3 17.0 %collective-permute-start.1 = (bf16[128,512]{1,0:T(8,128)(2,1)S(1)}, bf16[128,512]{1,0:T(8,128)(2,1)S(1)}, u32[]{:S(2)}, u32[]{:S(2)}) collective-permute-start(bf16[128,512]{1,0:T(8,128)(2,1)S(1)} %dynamic-slice_convert_fusion.3), channel_id=1, source_target_pairs={{0,4},{2,6},{4,0},{6,2},{8,12},{10,14},{12,8},{14,10},{16,20},{18,... | collective-permute-start | bytes 393224 | tf_op jit(solution)/shard_map/ppermute | solution.py:174
  94.3 14.6 %collective-permute-start.2 = (bf16[128,512]{1,0:T(8,128)(2,1)S(1)}, bf16[128,512]{1,0:T(8,128)(2,1)S(1)}, u32[]{:S(2)}, u32[]{:S(2)}) collective-permute-start(bf16[128,512]{1,0:T(8,128)(2,1)S(1)} %fusion.17), channel_id=1, source_target_pairs={{0,8},{2,10},{4,12},{6,14},{8,0},{10,2},{12,4},{14,6},{16,24},{18,... | collective-permute-start | bytes 393224 | tf_op jit(solution)/shard_map/ppermute | solution.py:174
  109.0 10.5 %collective-permute-start.3 = (bf16[128,512]{1,0:T(8,128)(2,1)S(1)}, bf16[128,512]{1,0:T(8,128)(2,1)S(1)}, u32[]{:S(2)}, u32[]{:S(2)}) collective-permute-start(bf16[128,512]{1,0:T(8,128)(2,1)S(1)} %fusion.16), channel_id=1, source_target_pairs={{0,16},{2,18},{4,20},{6,22},{8,24},{10,26},{12,28},{14,30},{16,0},... | collective-permute-start | bytes 393224 | tf_op jit(solution)/shard_map/ppermute | solution.py:174
  119.6 10.8 %collective-permute-start.4 = (bf16[128,512]{1,0:T(8,128)(2,1)S(1)}, bf16[128,512]{1,0:T(8,128)(2,1)S(1)}, u32[]{:S(2)}, u32[]{:S(2)}) collective-permute-start(bf16[128,512]{1,0:T(8,128)(2,1)S(1)} %add_convert_fusion.1), channel_id=1, source_target_pairs={{0,4},{2,6},{4,0},{6,2},{8,12},{10,14},{12,8},{14,10},{16,20},{18,... | collective-permute-start | bytes 393224 | tf_op jit(solution)/shard_map/ppermute | solution.py:174
  131.9 1.0 copy-start.4
  132.9 1.9 %collective-permute-start.11 = (bf16[32,64,128]{2,1,0:T(8,128)(2,1)S(1)}, bf16[32,64,128]{2,1,0:T(8,128)(2,1)S(1)}, u32[]{:S(2)}, u32[]{:S(2)}) collective-permute-start(bf16[32,64,128]{2,1,0:T(8,128)(2,1)S(1)} %get-tuple-element.12), channel_id=1, source_target_pairs={{0,2},{2,0},{4,6},{6,4},{8,10},{10,8},{12,14},{14,12},{16,18},{18,... | collective-permute-start | bytes 1572872 | tf_op jit(solution)/shard_map/ppermute | solution.py:332
  136.4 7.2 %collective-permute-start.14 = (bf16[16,32,128]{2,1,0:T(8,128)(2,1)S(1)}, bf16[16,32,128]{2,1,0:T(8,128)(2,1)S(1)}, u32[]{:S(2)}, u32[]{:S(2)}) collective-permute-start(bf16[16,32,128]{2,1,0:T(8,128)(2,1)S(1)} %dynamic-slice_convert_fusion), channel_id=1, source_target_pairs={{2,3},{3,2},{6,7},{7,6},{10,11},{11,10},{14,15},{15,14},{18,19},{1... | collective-permute-start | bytes 393224 | tf_op jit(solution)/shard_map/ppermute | solution.py:343
  139.6 5.7 %collective-permute-start.12 = (bf16[16,32,128]{2,1,0:T(8,128)(2,1)S(1)}, bf16[16,32,128]{2,1,0:T(8,128)(2,1)S(1)}, u32[]{:S(2)}, u32[]{:S(2)}) collective-permute-start(bf16[16,32,128]{2,1,0:T(8,128)(2,1)S(1)} %get-tuple-element.29), channel_id=1, source_target_pairs={{2,30},{3,31},{6,2},{7,3},{10,6},{11,7},{14,10},{15,11},{18,14},{1... | collective-permute-start | bytes 393224 | tf_op jit(solution)/shard_map/ppermute | solution.py:343
  142.7 4.8 %collective-permute-start.13 = (bf16[16,32,128]{2,1,0:T(8,128)(2,1)S(1)}, bf16[16,32,128]{2,1,0:T(8,128)(2,1)S(1)}, u32[]{:S(2)}, u32[]{:S(2)}) collective-permute-start(bf16[16,32,128]{2,1,0:T(8,128)(2,1)S(1)} %get-tuple-element.30), channel_id=1, source_target_pairs={{0,1},{1,0},{4,5},{5,4},{8,9},{9,8},{12,13},{13,12},{16,17},{17,16... | collective-permute-start | bytes 393224 | tf_op jit(solution)/shard_map/ppermute | solution.py:343

commit v3 on v2

--- a/solution.py
+++ b/solution.py
@@ -66,9 +66,9 @@
 
 def near_kernel(start, count, load, *refs):
     if load:
-        core, listed, rounds, own, vec, sib, screen, out, w, prod, total, sems = refs
+        core, listed, rounds, own, vec, sib, vec_s, screen, out, w, prod, total, sems = refs
     else:
-        core, listed, rounds, own, vec, sib, w, _, out, prod, total = refs
+        core, listed, rounds, own, vec, sib, vec_s, w, _, out, prod, total = refs
     half, _, _ = own.shape
     width = prod.shape[2]
     half_g = w.shape[1]
@@ -94,7 +94,7 @@
             return own[n, :, pl.ds(at, width)] if n < half else sib[n - half, :, g * width : (g + 1) * width]
 
         def vectors(n):
-            return vec[n] if n < half else sib[n - half, :, half_g:]
+            return vec[n] if n < half else vec_s[n - half]
 
         one_group(listed, rounds, w, g * width, slabs, vectors, out, prod, total, load and g == start)
     if load:
@@ -102,25 +102,26 @@
             copy(g).wait()
 
 
-def far_kernel(start, count, fresh, core, listed, rounds, own, vec, sib, w, came0, came1, vec_p, *refs):
-    if fresh:
-        out, prod, total, came, sem = refs
-    else:
-        _, out, prod, total, came, sem = refs
+def far_kernel(start, count, fresh, sources, core, listed, rounds, own, vec, sib, vec_s, w, vec_p, *refs):
+    refs = refs[0 if fresh else 1 :]
+    sources, (out, prod, total, came, sem) = refs[:sources], refs[sources:]
     half, _, _ = own.shape
     width = prod.shape[2]
     half_g = w.shape[1]
     own_at = core[0] * half_g
-
-    @pl.when(core[0] == 0)
-    def _():
-        pltpu.make_async_copy(came0.at[:, :, : count * width], came, sem).start()
-
-    @pl.when(core[0] != 0)
-    def _():
-        pltpu.make_async_copy(came1.at[:, :, : count * width], came, sem).start()
-
-    pltpu.make_async_copy(came0.at[:, :, : count * width], came, sem).wait()
+    if len(sources) == 1:
+        pltpu.make_async_copy(sources[0], came, sem).start()
+    else:
+
+        @pl.when(core[0] == 0)
+        def _():
+            pltpu.make_async_copy(sources[0], came, sem).start()
+
+        @pl.when(core[0] != 0)
+        def _():
+            pltpu.make_async_copy(sources[1], came, sem).start()
+
+    pltpu.make_async_copy(sources[0], came, sem).wait()
     for g in range(start, start + count):
         at = pl.multiple_of(own_at + g * width, width)
 
@@ -134,21 +135,22 @@
         def vectors(n):
             if n >= half:
                 return vec_p[n - half]
-            return jnp.where(core[0] == 0, vec[n], sib[n, :, half_g:])
+            return jnp.where(core[0] == 0, vec[n], vec_s[n])
 
         one_group(listed, rounds, w, g * width, slabs, vectors, out, prod, total, fresh and g == start)
 
 
 def last_kernel(core, own, sib, s2, near, far, give, keep):
     half, pairs, _ = own.shape
-    trials, half_g = s2.shape
+    half_g, trials = s2.shape
     width = 256
     own_at = core[0] * half_g
 
     def exchange(slab):
         acc = jnp.zeros((half * pairs, trials), F32)
         for g in range(half_g // width):
-            acc += dot_last(slab(g).reshape(half * pairs, width), s2[:, g * width : (g + 1) * width])
+            flat = slab(g).reshape(half * pairs, width)
+            acc += jnp.dot(flat, s2[g * width : (g + 1) * width], preferred_element_type=F32)
         return acc.reshape(half, pairs, trials)
 
     mine = exchange(lambda g: own[:, :, pl.ds(pl.multiple_of(own_at + g * width, width), width)]) - near[:half]
@@ -169,20 +171,46 @@
         give[half:] = mine.astype(BF16)
 
 
-def density_sum(part, me, size):
-    columns = part.shape[1] // 2
-    swap = lambda v, bit: lax.ppermute(v, "ka", [(i, i ^ bit) for i in range(size)])
+def density_steps(part, me, size):
+    rows = part.shape[0] // 2
     high = (me // 2) % 2
-    keep = lax.dynamic_slice_in_dim(part, high * columns, columns, 1)
-    give = lax.dynamic_slice_in_dim(part, (1 - high) * columns, columns, 1).astype(BF16)
-    part = keep + swap(give, 2).astype(F32)
+    keep = lax.dynamic_slice_in_dim(part, high * rows, rows, 0)
+    part = keep + (yield lax.dynamic_slice_in_dim(part, (1 - high) * rows, rows, 0).astype(BF16), 2).astype(F32)
     bit = 4
     while bit < size:
-        part = part + swap(part.astype(BF16), bit).astype(F32)
+        part = part + (yield part.astype(BF16), bit).astype(F32)
         bit *= 2
     part = part.astype(BF16)
-    other = swap(part, 2)
-    return jnp.where(high == 0, jnp.concatenate([part, other], 1), jnp.concatenate([other, part], 1))
+    other = yield part, 2
+    return jnp.where(high == 0, jnp.concatenate([part, other], 0), jnp.concatenate([other, part], 0))
+
+
+class Density:
+    def __init__(self, steps, size):
+        self.steps, self.size, self.result = steps, size, None
+        self.send(None)
+
+    def send(self, got):
+        try:
+            self.give, self.bit = self.steps.send(got)
+        except StopIteration as stop:
+            self.give, self.result = stop.value, stop.value
+
+    def after(self, value):
+        if self.result is None:
+            came = lax.ppermute(self.give, "ka", [(i, i ^ self.bit) for i in range(self.size)])
+            came, value = lax.optimization_barrier((came, value))
+            self.send(came)
+        return self.before(value)
+
+    def before(self, value):
+        self.give, value = lax.optimization_barrier((self.give, value))
+        return value
+
+    def finish(self):
+        while self.result is None:
+            self.after(jnp.zeros((1,), F32))
+        return self.give
 
 
 def on_device(pair_density, trial_vectors, energy, coulomb, screen, neighbors, live_count, q_index):
@@ -196,40 +224,42 @@
     core_id = core.astype(jnp.int32)[None]
     half_g = local_g // 2
     groups = half_g // width
-    first_block = me - core
     sibling = [(i, i ^ 1) for i in range(size)]
     onward = [(i, (i + 2) % size) for i in range(size)]
-    chunk_count = 2 if groups % 2 == 0 else 1
-    chunk_groups = groups // chunk_count
-    chunk = chunk_groups * width
-
-    table = jnp.concatenate([neighbors, q_index, live_count[:, None]], axis=1)
+    to_next = [[(i, (i + 1 + target) % size) for i in range(1, size, 2)] for target in range(2)]
+
+    def pick(first, second):
+        return jnp.where(core == 0, first, second)
+
+    offset = (neighbors // local_k - me + 1) % size
+    table = jnp.concatenate([offset * local_k + neighbors % local_k, q_index, live_count[:, None]], axis=1)
     table_s = lax.ppermute(table, "ka", sibling)
+    vec_s = lax.ppermute(trial_vectors, "ka", sibling)
+    table_p, vec_p = (
+        pick(*(lax.ppermute(value, "ka", pairs) for pairs in to_next)) for value in (table, trial_vectors)
+    )
+
     give_half = lax.dynamic_slice_in_dim(pair_density, (1 - core) * half_g, half_g, 2)
-    sib = lax.ppermute(jnp.concatenate([give_half, trial_vectors], 2), "ka", sibling)
-    came = []
-    for c in range(chunk_count):
-        pieces = []
-        for target in range(2):
-            piece = lax.slice_in_dim(
-                pair_density, target * half_g + c * chunk, target * half_g + (c + 1) * chunk, axis=2
-            )
-            if c == 0:
-                piece = jnp.concatenate([piece, trial_vectors], 2)
-            pieces.append(
-                lax.ppermute(piece, "ka", [(i, (i + 1 + target) % size) for i in range(1, size, 2)])
-            )
-        came.append(pieces)
-    table_a = jnp.where(core == 0, table, table_s)
-    table_b = jnp.where(core == 0, table_s, table)
-    table_p = lax.ppermute(table_b, "ka", onward)
-
+    sib = lax.ppermute(give_half, "ka", sibling)
     own_half = lax.dynamic_slice_in_dim(pair_density, core * half_g, half_g, 2)
-    contract = lambda v, d: lax.dot_general(v, d, (((0, 1), (0, 1)), ((), ())), preferred_element_type=F32)
-    part = contract(trial_vectors, own_half) + contract(sib[:, :, half_g:], sib[:, :, :half_g])
-    density_total = density_sum(part, me, size)
+    lead = max(groups // 2, 1)
+    chunks = [(0, lead)] + [(g, 1) for g in range(lead, groups)]
+    came = [
+        [
+            lax.ppermute(pair_density[:, :, low : low + lead * width], "ka", pairs)
+            for low, pairs in zip((0, half_g), to_next)
+        ]
+    ]
+    sending = [
+        pick(sib[:, :, g * width : (g + 1) * width], own_half[:, :, g * width : (g + 1) * width])
+        for g in range(lead, groups)
+    ]
+    came += [[lax.ppermute(piece, "ka", onward)] for piece in sending]
+
+    contract = lambda v, d: lax.dot_general(d, v, (((0, 1), (0, 1)), ((), ())), preferred_element_type=F32)
+    part = contract(trial_vectors, own_half) + contract(vec_s, sib)
+    density = Density(density_steps(part, me, size), size)
     my_coulomb = lax.dynamic_slice_in_dim(coulomb, core * half_g, half_g, 0)
-    screened2 = (2.0 * my_coulomb[None, :] * density_total.astype(F32)).astype(BF16)
 
     def columns(t):
         live = jnp.arange(slots, dtype=jnp.int32)[None, :] < t[:, 2 * slots :]
@@ -238,8 +268,6 @@
 
     row = jnp.broadcast_to(jnp.arange(local_k, dtype=jnp.int32)[:, None], (local_k, slots))
     flat = lambda u, v: jnp.concatenate([u.reshape(-1), v.reshape(-1)])
-    other_block = me + 1 - 2 * core
-    before = (first_block + size - 1) % size
     length = 2 * local_k * slots + q_count
     length = (length + UNROLL - 1) // UNROLL * UNROLL
 
@@ -254,19 +282,18 @@
             2 * local_k,
         )
 
-    own_t, sib_t, a_t, p_t = columns(table), columns(table_s), columns(table_a), columns(table_p)
-    here = lambda blk: (blk == me) | (blk == other_block)
+    own_t, sib_t = columns(table), columns(table_s)
+    own_cross, sib_cross = own_t[0] == 2 - 2 * core, sib_t[0] == 2 * core
     near_list, near_rounds = listing(
         own_t,
         sib_t,
-        own_t[1] + local_k * (own_t[0] == other_block),
-        sib_t[1] + local_k * (sib_t[0] == other_block),
-        here(own_t[0]),
-        here(sib_t[0]),
+        own_t[1] + local_k * own_cross,
+        sib_t[1] + local_k * (sib_t[0] == 1),
+        own_cross | (own_t[0] == 1),
+        sib_cross | (sib_t[0] == 1),
     )
-    far_list, far_rounds = listing(
-        a_t, p_t, a_t[1] + local_k, p_t[1], a_t[0] == before, p_t[0] == first_block
-    )
+    a_t, p_t = columns(pick(table, table_s)), columns(table_p)
+    far_list, far_rounds = listing(a_t, p_t, a_t[1] + local_k, p_t[1], a_t[0] == 0, p_t[0] == 2)
 
     sums = jax.ShapeDtypeStruct((2 * local_k, pair_count, trial_count), F32)
     work = [
@@ -283,43 +310,53 @@
         )
 
     near_groups = (groups + 1) // 2
+    near_rounds, vec_p, far_list, far_rounds, *_ = lax.optimization_barrier(
+        (near_rounds, vec_p, far_list, far_rounds, *sending)
+    )
+    near_rounds = density.before(near_rounds)
     near, w_half = pl.pallas_call(
         functools.partial(near_kernel, 0, near_groups, True),
         out_shape=(sums, jax.ShapeDtypeStruct((q_count, half_g, width), BF16)),
-        in_specs=[IN_SMEM, IN_SMEM, IN_SMEM, IN_VMEM, IN_VMEM, IN_VMEM, ANYWHERE],
+        in_specs=[IN_SMEM] * 3 + [IN_VMEM] * 4 + [ANYWHERE],
         out_specs=(IN_VMEM, IN_VMEM),
         scratch_shapes=work + [pltpu.SemaphoreType.DMA((groups,))],
         compiler_params=params(),
         cost_estimate=cost(near_groups, 160),
-    )(core_id, near_list, near_rounds, pair_density, trial_vectors, sib, screen)
+    )(core_id, near_list, near_rounds, pair_density, trial_vectors, sib, vec_s, screen)
+    near = density.after(near)
     if groups > near_groups:
         near = pl.pallas_call(
             functools.partial(near_kernel, near_groups, groups - near_groups, False),
             out_shape=sums,
-            in_specs=[IN_SMEM, IN_SMEM, IN_SMEM, IN_VMEM, IN_VMEM, IN_VMEM, IN_VMEM, IN_VMEM],
+            in_specs=[IN_SMEM] * 3 + [IN_VMEM] * 6,
             out_specs=IN_VMEM,
             scratch_shapes=work,
-            input_output_aliases={7: 0},
+            input_output_aliases={8: 0},
             compiler_params=params(),
             cost_estimate=cost(groups - near_groups, 160),
-        )(core_id, near_list, near_rounds, pair_density, trial_vectors, sib, w_half, near)
-    vec_p = jnp.where(core == 0, came[0][0][:, :, chunk:], came[0][1][:, :, chunk:])
+        )(core_id, near_list, near_rounds, pair_density, trial_vectors, sib, vec_s, w_half, near)
+        near = density.after(near)
+    near, far_rounds = lax.optimization_barrier((near, far_rounds))
+    far_rounds = density.before(far_rounds)
     far = None
-    for c in range(chunk_count):
+    for c, (start, count) in enumerate(chunks):
         far = pl.pallas_call(
-            functools.partial(far_kernel, c * chunk_groups, chunk_groups, c == 0),
+            functools.partial(far_kernel, start, count, c == 0, len(came[c])),
             out_shape=sums,
-            in_specs=[IN_SMEM, IN_SMEM, IN_SMEM, IN_VMEM, IN_VMEM, IN_VMEM, IN_VMEM, ANYWHERE, ANYWHERE, IN_VMEM]
-            + [IN_VMEM] * (c > 0),
+            in_specs=[IN_SMEM] * 3 + [IN_VMEM] * (6 + (c > 0)) + [ANYWHERE] * len(came[c]),
             out_specs=IN_VMEM,
-            scratch_shapes=work + [VMEM((local_k, pair_count, chunk), BF16), pltpu.SemaphoreType.DMA],
-            input_output_aliases={10: 0} if c else {},
+            scratch_shapes=work
+            + [VMEM((local_k, pair_count, count * width), BF16), pltpu.SemaphoreType.DMA],
+            input_output_aliases={9: 0} if c else {},
             compiler_params=params(),
-            cost_estimate=cost(chunk_groups, 80),
+            cost_estimate=cost(count, 80),
         )(
-            core_id, far_list, far_rounds, pair_density, trial_vectors, sib, w_half, came[c][0], came[c][1], vec_p,
-            *([far] if c else []),
+            core_id, far_list, far_rounds, pair_density, trial_vectors, sib, vec_s, w_half, vec_p,
+            *([far] if c else []), *came[c],
         )
+        if c + 1 < len(chunks):
+            far = density.after(far)
+    screened2 = (2.0 * my_coulomb[:, None] * density.finish().astype(F32)).astype(BF16)
     give, keep = pl.pallas_call(
         last_kernel,
         out_shape=(jax.ShapeDtypeStruct(sums.shape, BF16), sums),

time: 150 us -> 139 us (0.927); the launches traced: 148 us -> 140 us
  waiting for transfers between devices: 50.1 us -> 24.1 us
  starting transfers between devices: 19.7 us -> 31.6 us
  Pallas kernels: 53.9 us -> 59.7 us
  other arithmetic: 10.6 us -> 7.9 us
    ppermute x10 -> x14, waiting for transfers between devices: 43.6 us -> 18.6 us  [the longest x4 18.6 us: after(): lax.ppermute(self.give, 'ka', [(i, i ^ self.bit) for i in range(self.size)])]
    ppermute x10 -> x14, starting transfers between devices: 13.4 us -> 24.9 us  [the longest x4 14.3 us: on_device(): lax.ppermute(value, 'ka', pairs)]
    concatenate x3 -> x1, other arithmetic: 4.31 us -> 0.78 us  [on_device(): jnp.concatenate([offset * local_k + neighbors % local_k, q_index, live_co...]
    pallas_call x2 -> x3, Pallas kernels: 21.1 us -> 22.9 us  [on_device(): pl.pallas_call(functools.partial(far_kernel, start, count, c == 0, len(ca...]
    unnamed x22 -> x14, local copies, waits for them, and re-layouts: 2.38 us -> 0.78 us
    pallas_call x1, Pallas kernels: 14.5 us -> 16.1 us  [on_device(): pl.pallas_call(functools.partial(near_kernel, near_groups, groups - near_...]
    pallas_call x1, Pallas kernels: 16.9 us -> 18.4 us  [on_device(): pl.pallas_call(functools.partial(near_kernel, 0, near_groups, True), out_...]
    ppermute x1, starting transfers between devices: 0.01 us -> 1.55 us  [on_device(): both = keep + lax.ppermute(give, 'ka', sibling).astype(F32)]
  transfers between devices with their start and end apart: 15 -> 19, of which waited for: 6 -> 4; matrix products, arithmetic and copies ran while one was open for 11% -> 14% of each run, Pallas kernels for 35% -> 37%
where the time goes in v3:
time: 139 us; the launch traced here: 140 us
  Pallas kernels  59.7 us (43%)
  starting transfers between devices  31.6 us (23%)
  waiting for transfers between devices  24.1 us (17%)
  local copies, waits for them, and re-layouts  11 us (8%)
  other arithmetic  7.9 us (6%)
  matrix products  3.9 us (3%)
  between operations  1.79 us (1%)
    pallas_call x3, Pallas kernels, on_device(): pl.pallas_call(functools.partial(far_kernel, start, count, c == 0, len(ca...  22.9 us
    ppermute x4, waiting for transfers between devices, after(): lax.ppermute(self.give, 'ka', [(i, i ^ self.bit) for i in range(self.size)])  18.6 us
    pallas_call x1, Pallas kernels, on_device(): pl.pallas_call(functools.partial(near_kernel, 0, near_groups, True), out_...  18.4 us
    pallas_call x1, Pallas kernels, on_device(): pl.pallas_call(functools.partial(near_kernel, near_groups, groups - near_...  16.1 us
    ppermute x4, starting transfers between devices, on_device(): lax.ppermute(value, 'ka', pairs)  14.3 us
    ppermute x2, starting transfers between devices, on_device(): lax.ppermute(pair_density[:, :, low:low + lead * width], 'ka', pairs)  7.77 us
    ppermute x3, starting transfers between devices, sent(): lax.ppermute(rows_of(value, (mine + steps) % parts).astype(BF16), ('ka',...  5.12 us
    dot_general x2, matrix products, on_device(): lax.dot_general(d, v, (((0, 1), (0, 1)), ((), ())), preferred_element_typ...  3.9 us
  transfers between devices with their start and end apart: 19, of which 4 were waited for; matrix products, arithmetic and copies ran while one was open for 14% of the time, Pallas kernels for 37%

profile of v3, /device:TPU:1, one launch (start us, length us, event | category | flops | bytes accessed | tf_op | source)
XLA Modules:
  0.0 140.0 jit_solution(5752348564244887362)
XLA Ops:
  0.0 0.7 copy.14
  0.7 0.7 fusion.20
  1.5 0.8 pad_add_fusion
  2.3 4.5 %collective-permute-start.5 = (s32[16,33]{1,0:T(8,128)S(1)}, s32[16,33]{1,0:T(8,128)S(1)}, u32[]{:S(2)}, u32[]{:S(2)}) collective-permute-start(s32[16,33]{1,0:T(8,128)S(1)} %pad_add_fusion), channel_id=1, source_target_pairs={{2,4},{6,8},{10,12},{14,16},{18,20},{22,24},{26,28},{30,0},{3,5},{... | collective-permute-start | bytes 6344 | tf_op jit(solution)/shard_map/ppermute | solution.py:239
  6.8 3.2 %collective-permute-start.6 = (s32[16,33]{1,0:T(8,128)S(1)}, s32[16,33]{1,0:T(8,128)S(1)}, u32[]{:S(2)}, u32[]{:S(2)}) collective-permute-start(s32[16,33]{1,0:T(8,128)S(1)} %pad_add_fusion), channel_id=1, source_target_pairs={{2,6},{6,10},{10,14},{14,18},{18,22},{22,26},{26,30},{30,2},{3,7},... | collective-permute-start | bytes 6344 | tf_op jit(solution)/shard_map/ppermute | solution.py:239
  10.0 3.5 %collective-permute-start.3 = (bf16[16,64,128]{2,1,0:T(8,128)(2,1)}, bf16[16,64,128]{2,1,0:T(8,128)(2,1)S(1)}, u32[]{:S(2)}, u32[]{:S(2)}) collective-permute-start(bf16[16,64,128]{2,1,0:T(8,128)(2,1)} %vec.5), channel_id=1, source_target_pairs={{2,4},{6,8},{10,12},{14,16},{18,20},{22,24},{26,28},{30,0},{3,5},{... | collective-permute-start | bytes 786440 | tf_op jit(solution)/shard_map/ppermute | solution.py:239
  13.6 0.8 reshape.223
  14.4 0.7 fusion.23
  15.1 3.1 %fusion.47 = (bf16[16,64,512]{2,1,0:T(8,128)(2,1)}, bf16[16,64,512]{2,1,0:T(8,128)(2,1)}) fusion(bf16[16,64,2048]{2,1,0:T(8,128)(2,1)} %own.7), kind=kLoop, calls=%fused_computation.143 | loop fusion | bytes 4194304 | tf_op jit(solution)/shard_map/slice | solution.py:249
  18.2 3.2 %constant_dynamic-slice_fusion = bf16[16,64,1024]{2,1,0:T(8,128)(2,1)} fusion(bf16[16,64,2048]{2,1,0:T(8,128)(2,1)} %own.7, s32[]{:T(128)S(6)} %select_n.196), kind=kLoop, calls=%fused_computation.117 | loop fusion | bytes 4194308 | tf_op jit(solution)/shard_map/dynamic_slice | solution.py:242
  21.4 3.2 %fusion.2 = f32[1024,128]{1,0:T(8,128)} fusion(bf16[16,64,128]{2,1,0:T(8,128)(2,1)S(1)} %copy-done.2, bf16[16,64,2048]{2,1,0:T(8,128)(2,1)} %own.7, s32[]{:T(128)S(6)} %select_n.197), kind=kOutput, calls=%fused_computation.2 | convolution fusion | flops 268435456 | bytes 2883588 | tf_op jit(solution)/shard_map/dot_general | solution.py:259
  25.0 0.2 dynamic-update-slice.4
  25.3 3.2 %collective-permute-start.4 = (bf16[16,64,128]{2,1,0:T(8,128)(2,1)S(1)}, bf16[16,64,128]{2,1,0:T(8,128)(2,1)S(1)}, u32[]{:S(2)}, u32[]{:S(2)}) collective-permute-start(bf16[16,64,128]{2,1,0:T(8,128)(2,1)S(1)} %copy-done.2), channel_id=1, source_target_pairs={{2,6},{6,10},{10,14},{14,18},{18,22},{22,26},{26,30},{30,2},{3,7},... | collective-permute-start | bytes 786440 | tf_op jit(solution)/shard_map/ppermute | solution.py:239
  28.4 0.2 slice_reduce_fusion.1
  29.0 4.5 %collective-permute-start.10 = (bf16[16,64,512]{2,1,0:T(8,128)(2,1)}, bf16[16,64,512]{2,1,0:T(8,128)(2,1)}, u32[]{:S(2)}, u32[]{:S(2)}) collective-permute-start(bf16[16,64,512]{2,1,0:T(8,128)(2,1)} %get-tuple-element.80), channel_id=1, source_target_pairs={{2,4},{6,8},{10,12},{14,16},{18,20},{22,24},{26,28},{30,0},{3,5},{... | collective-permute-start | bytes 3145736 | tf_op jit(solution)/shard_map/ppermute | solution.py:249
  33.4 0.2 slice_reduce_fusion
  34.2 0.2 slice_reduce_fusion.2
  34.6 0.2 dynamic-update-slice.2
  34.8 0.2 dynamic-update-slice.3
  35.0 0.1 convert_reduce_fusion.2
  35.1 0.2 dynamic-update-slice.5
  35.5 0.7 fusion.43
  36.6 0.3 convert_reduce_fusion.1
  37.0 0.2 select_reduce_fusion.1
  37.2 0.3 convert_reduce_fusion
  37.5 0.2 select_reduce_fusion
  39.0 3.3 %collective-permute-start.11 = (bf16[16,64,512]{2,1,0:T(8,128)(2,1)}, bf16[16,64,512]{2,1,0:T(8,128)(2,1)S(1)}, u32[]{:S(2)}, u32[]{:S(2)}) collective-permute-start(bf16[16,64,512]{2,1,0:T(8,128)(2,1)} %get-tuple-element.79), channel_id=1, source_target_pairs={{2,6},{6,10},{10,14},{14,18},{18,22},{22,26},{26,30},{30,2},{3,7},... | collective-permute-start | bytes 3145736 | tf_op jit(solution)/shard_map/ppermute | solution.py:249
  42.4 1.6 %dynamic-slice_select_fusion = (bf16[16,64,256]{2,1,0:T(8,128)(2,1)S(1)}, bf16[16,64,256]{2,1,0:T(8,128)(2,1)S(1)}) fusion(bf16[16,64,2048]{2,1,0:T(8,128)(2,1)} %own.7, s32[]{:T(128)S(6)} %add.269, bf16[16,64,1024]{2,1,0:T(8,128)(2,1)S(1)} %collective-permute-done.refs_5_.sib, pred[]{:T(512)S(6)} %eq.131, s32[]{:T(128)S(6)} %add.268), kind=kLoop, calls=%fused_computation.15 | loop fusion | flops 524288 | bytes 3145737 | tf_op jit(solution)/shard_map/jit(_where)/select_n | solution.py:232
  43.9 1.3 collective-permute-start.13
  45.3 0.7 fusion.5
  46.1 1.1 collective-permute-start.7
  47.2 0.3 copy-done.1
  47.5 18.4 %shard_map.82 = (f32[32,64,128]{2,1,0:T(8,128)S(1)}, bf16[32,1024,256]{2,1,0:T(8,128)(2,1)S(1)}) custom-call(s32[1]{0:T(128)} %bitcast.refs_0_.core, s32[544]{0:T(1024)S(1)} %broadcast_add_fusion.refs_1_, s32[1]{0:T(128)} %bitcast.4.refs_2_, bf16[16,64,2048]{2,1,0:T(8,128)(2,1)S(1)} %copy-done.1, bf16[16,64,128]{2,1,0:T(8,128)(2,1)S(1)} %copy-done.2, ...), custom_call_target="tpu_custom_call" | custom-call | flops 10737418240 | bytes 1048576 | tf_op jit(solution)/shard_map/pallas_call | solution.py:317
  65.9 18.6 %collective-permute-done.7 = bf16[512,128]{1,0:T(8,128)(2,1)S(1)} collective-permute-done((bf16[512,128]{1,0:T(8,128)(2,1)S(1)}, bf16[512,128]{1,0:T(8,128)(2,1)S(1)}, u32[]{:S(2)}, u32[]{:S(2)}) %collective-permute-start.7) | collective-permute-done | bytes 131104 | tf_op jit(solution)/shard_map/ppermute | solution.py:201
  84.6 16.1 %shard_map.83.near = f32[32,64,128]{2,1,0:T(8,128)S(1)} custom-call(s32[1]{0:T(128)} %bitcast.refs_0_.core, s32[544]{0:T(1024)S(1)} %broadcast_add_fusion.refs_1_, s32[1]{0:T(128)} %bitcast.4.refs_2_, bf16[16,64,2048]{2,1,0:T(8,128)(2,1)S(1)} %copy-done.1, bf16[16,64,128]{2,1,0:T(8,128)(2,1)S(1)} %copy-done.2, ...), custom_call_target="tpu_custom_call", output_to_operand_aliasing={{}: (8, {})} | custom-call | flops 10737418240 | bytes 1048576 | tf_op jit(solution)/shard_map/pallas_call | solution.py:328
  100.9 10.9 %shard_map.84.refs_0_ = f32[32,64,128]{2,1,0:T(8,128)S(1)} custom-call(s32[1]{0:T(128)} %bitcast.refs_0_.core, s32[544]{0:T(1024)S(1)} %broadcast_add_fusion.1.listed, s32[1]{0:T(128)} %bitcast.5.rounds, bf16[16,64,2048]{2,1,0:T(8,128)(2,1)S(1)} %copy-done.1, bf16[16,64,128]{2,1,0:T(8,128)(2,1)S(1)} %copy-done.2, ...), custom_call_target="tpu_custom_call" | custom-call | flops 5368709120 | bytes 1048576 | tf_op jit(solution)/shard_map/pallas_call | solution.py:343
  112.0 5.9 %shard_map.85.refs_0_ = f32[32,64,128]{2,1,0:T(8,128)S(1)} custom-call(s32[1]{0:T(128)} %bitcast.refs_0_.core, s32[544]{0:T(1024)S(1)} %broadcast_add_fusion.1.listed, s32[1]{0:T(128)} %bitcast.5.rounds, bf16[16,64,2048]{2,1,0:T(8,128)(2,1)S(1)} %copy-done.1, bf16[16,64,128]{2,1,0:T(8,128)(2,1)S(1)} %copy-done.2, ...), custom_call_target="tpu_custom_call", output_to_operand_aliasing={{}: (9, {})} | custom-call | flops 2684354560 | bytes 1048576 | tf_op jit(solution)/shard_map/pallas_call | solution.py:343
  118.0 0.2 multiply_convert_fusion.s2
  118.2 6.1 %shard_map.86.far = f32[32,64,128]{2,1,0:T(8,128)S(1)} custom-call(s32[1]{0:T(128)} %bitcast.refs_0_.core, s32[544]{0:T(1024)S(1)} %broadcast_add_fusion.1.listed, s32[1]{0:T(128)} %bitcast.5.rounds, bf16[16,64,2048]{2,1,0:T(8,128)(2,1)S(1)} %copy-done.1, bf16[16,64,128]{2,1,0:T(8,128)(2,1)S(1)} %copy-done.2, ...), custom_call_target="tpu_custom_call", output_to_operand_aliasing={{}: (9, {})} | custom-call | flops 2684354560 | bytes 1048576 | tf_op jit(solution)/shard_map/pallas_call | solution.py:343
  124.4 2.2 %shard_map.87 = (bf16[32,64,128]{2,1,0:T(8,128)(2,1)}, f32[32,64,128]{2,1,0:T(8,128)S(1)}) custom-call(s32[1]{0:T(128)} %bitcast.refs_0_.core, bf16[16,64,2048]{2,1,0:T(8,128)(2,1)S(1)} %copy-done.1, bf16[16,64,1024]{2,1,0:T(8,128)(2,1)S(1)} %collective-permute-done.refs_5_.sib, bf16[1024,128]{1,0:T(8,128)(2,1)S(1)} %multiply_convert_fusion.s2, ...), custom_call_target="tpu_custom_call" | custom-call | flops 536870912 | bytes 1048576 | tf_op jit(solution)/shard_map/pallas_call | solution.py:360
  126.6 1.6 %collective-permute-start.15 = (bf16[32,64,128]{2,1,0:T(8,128)(2,1)}, bf16[32,64,128]{2,1,0:T(8,128)(2,1)S(1)}, u32[]{:S(2)}, u32[]{:S(2)}) collective-permute-start(bf16[32,64,128]{2,1,0:T(8,128)(2,1)} %get-tuple-element.64), channel_id=1, source_target_pairs={{0,2},{2,0},{4,6},{6,4},{8,10},{10,8},{12,14},{14,12},{16,18},{18,... | collective-permute-start | bytes 1572872 | tf_op jit(solution)/shard_map/ppermute | solution.py:369
  128.1 1.7 %collective-permute-done.15 = bf16[32,64,128]{2,1,0:T(8,128)(2,1)S(1)} collective-permute-done((bf16[32,64,128]{2,1,0:T(8,128)(2,1)}, bf16[32,64,128]{2,1,0:T(8,128)(2,1)S(1)}, u32[]{:S(2)}, u32[]{:S(2)}) %collective-permute-start.15) | collective-permute-done | bytes 524320 | tf_op jit(solution)/shard_map/ppermute | solution.py:369
  129.9 0.2 convert_add_fusion
  130.2 3.1 %collective-permute-start.18 = (bf16[16,32,128]{2,1,0:T(8,128)(2,1)S(1)}, bf16[16,32,128]{2,1,0:T(8,128)(2,1)S(1)}, u32[]{:S(2)}, u32[]{:S(2)}) collective-permute-start(bf16[16,32,128]{2,1,0:T(8,128)(2,1)S(1)} %dynamic-slice_convert_fusion), channel_id=1, source_target_pairs={{2,3},{3,2},{6,7},{7,6},{10,11},{11,10},{14,15},{15,14},{18,19},{1... | collective-permute-start | bytes 393224 | tf_op jit(solution)/shard_map/ppermute | solution.py:380
  133.5 1.9 %collective-permute-start.16 = (bf16[16,32,128]{2,1,0:T(8,128)(2,1)S(1)}, bf16[16,32,128]{2,1,0:T(8,128)(2,1)S(1)}, u32[]{:S(2)}, u32[]{:S(2)}) collective-permute-start(bf16[16,32,128]{2,1,0:T(8,128)(2,1)S(1)} %get-tuple-element.83), channel_id=1, source_target_pairs={{2,30},{3,31},{6,2},{7,3},{10,6},{11,7},{14,10},{15,11},{18,14},{1... | collective-permute-start | bytes 393224 | tf_op jit(solution)/shard_map/ppermute | solution.py:380
  135.5 3.0 %collective-permute-done.18 = bf16[16,32,128]{2,1,0:T(8,128)(2,1)S(1)} collective-permute-done((bf16[16,32,128]{2,1,0:T(8,128)(2,1)S(1)}, bf16[16,32,128]{2,1,0:T(8,128)(2,1)S(1)}, u32[]{:S(2)}, u32[]{:S(2)}) %collective-permute-start.18) | collective-permute-done | bytes 131104 | tf_op jit(solution)/shard_map/ppermute | solution.py:380
  138.4 0.7 collective-permute-done.16
  139.2 0.8 add_convert_fusion
  (83 shorter events, 3.2 us)
Async XLA Ops:
  0.0 135.4 %copy-start = (f32[16,64]{1,0:T(8,128)S(1)}, f32[16,64]{1,0:T(8,128)}, u32[]{:S(2)}) copy-start(f32[16,64]{1,0:T(8,128)} %param.10) | copy-start | bytes 12292
  2.3 23.0 %collective-permute-start.2 = (s32[16,33]{1,0:T(8,128)S(1)}, s32[16,33]{1,0:T(8,128)S(1)}, u32[]{:S(2)}, u32[]{:S(2)}) collective-permute-start(s32[16,33]{1,0:T(8,128)S(1)} %pad_add_fusion), channel_id=1, source_target_pairs={{0,2},{2,0},{4,6},{6,4},{8,10},{10,8},{12,14},{14,12},{16,18},{18,... | collective-permute-start | bytes 6344 | tf_op jit(solution)/shard_map/ppermute | solution.py:236
  2.3 26.5 %collective-permute-start.5 = (s32[16,33]{1,0:T(8,128)S(1)}, s32[16,33]{1,0:T(8,128)S(1)}, u32[]{:S(2)}, u32[]{:S(2)}) collective-permute-start(s32[16,33]{1,0:T(8,128)S(1)} %pad_add_fusion), channel_id=1, source_target_pairs={{2,4},{6,8},{10,12},{14,16},{18,20},{22,24},{26,28},{30,0},{3,5},{... | collective-permute-start | bytes 6344 | tf_op jit(solution)/shard_map/ppermute | solution.py:239
  6.8 22.2 %collective-permute-start.6 = (s32[16,33]{1,0:T(8,128)S(1)}, s32[16,33]{1,0:T(8,128)S(1)}, u32[]{:S(2)}, u32[]{:S(2)}) collective-permute-start(s32[16,33]{1,0:T(8,128)S(1)} %pad_add_fusion), channel_id=1, source_target_pairs={{2,6},{6,10},{10,14},{14,18},{18,22},{22,26},{26,30},{30,2},{3,7},... | collective-permute-start | bytes 6344 | tf_op jit(solution)/shard_map/ppermute | solution.py:239
  10.0 35.3 %collective-permute-start.1 = (bf16[16,64,128]{2,1,0:T(8,128)(2,1)}, bf16[16,64,128]{2,1,0:T(8,128)(2,1)S(1)}, u32[]{:S(2)}, u32[]{:S(2)}) collective-permute-start(bf16[16,64,128]{2,1,0:T(8,128)(2,1)} %vec.5), channel_id=1, source_target_pairs={{0,2},{2,0},{4,6},{6,4},{8,10},{10,8},{12,14},{14,12},{16,18},{18,... | collective-permute-start | bytes 786440 | tf_op jit(solution)/shard_map/ppermute | solution.py:237
  10.0 28.9 %collective-permute-start.3 = (bf16[16,64,128]{2,1,0:T(8,128)(2,1)}, bf16[16,64,128]{2,1,0:T(8,128)(2,1)S(1)}, u32[]{:S(2)}, u32[]{:S(2)}) collective-permute-start(bf16[16,64,128]{2,1,0:T(8,128)(2,1)} %vec.5), channel_id=1, source_target_pairs={{2,4},{6,8},{10,12},{14,16},{18,20},{22,24},{26,28},{30,0},{3,5},{... | collective-permute-start | bytes 786440 | tf_op jit(solution)/shard_map/ppermute | solution.py:239
  18.2 3.2 %copy-start.2 = (bf16[16,64,128]{2,1,0:T(8,128)(2,1)S(1)}, bf16[16,64,128]{2,1,0:T(8,128)(2,1)}, u32[]{:S(2)}) copy-start(bf16[16,64,128]{2,1,0:T(8,128)(2,1)} %vec.5) | copy-start | bytes 786436
  21.4 3.2 %copy-start.3 = (f32[2048]{0:T(1024)S(1)}, f32[2048]{0:T(1024)}, u32[]{:S(2)}) copy-start(f32[2048]{0:T(1024)} %param.11) | copy-start | bytes 24580
  25.3 17.1 %collective-permute-start.4 = (bf16[16,64,128]{2,1,0:T(8,128)(2,1)S(1)}, bf16[16,64,128]{2,1,0:T(8,128)(2,1)S(1)}, u32[]{:S(2)}, u32[]{:S(2)}) collective-permute-start(bf16[16,64,128]{2,1,0:T(8,128)(2,1)S(1)} %copy-done.2), channel_id=1, source_target_pairs={{2,6},{6,10},{10,14},{14,18},{18,22},{22,26},{26,30},{30,2},{3,7},... | collective-permute-start | bytes 786440 | tf_op jit(solution)/shard_map/ppermute | solution.py:239
  28.9 13.5 %collective-permute-start = (bf16[16,64,1024]{2,1,0:T(8,128)(2,1)}, bf16[16,64,1024]{2,1,0:T(8,128)(2,1)S(1)}, u32[]{:S(2)}, u32[]{:S(2)}) collective-permute-start(bf16[16,64,1024]{2,1,0:T(8,128)(2,1)} %constant_dynamic-slice_fusion), channel_id=1, source_target_pairs={{0,2},{2,0},{4,6},{6,4},{8,10},{10,8},{12,14},{14,12},{16,18},{18,... | collective-permute-start | bytes 6291464 | tf_op jit(solution)/shard_map/ppermute | solution.py:243
  29.0 71.9 %collective-permute-start.10 = (bf16[16,64,512]{2,1,0:T(8,128)(2,1)}, bf16[16,64,512]{2,1,0:T(8,128)(2,1)}, u32[]{:S(2)}, u32[]{:S(2)}) collective-permute-start(bf16[16,64,512]{2,1,0:T(8,128)(2,1)} %get-tuple-element.80), channel_id=1, source_target_pairs={{2,4},{6,8},{10,12},{14,16},{18,20},{22,24},{26,28},{30,0},{3,5},{... | collective-permute-start | bytes 3145736 | tf_op jit(solution)/shard_map/ppermute | solution.py:249
  39.0 6.3 %copy-start.4 = (f32[1024,128]{1,0:T(8,128)S(1)}, f32[1024,128]{1,0:T(8,128)}, u32[]{:S(2)}) copy-start(f32[1024,128]{1,0:T(8,128)} %fusion.2) | copy-start | bytes 1572868
  39.0 61.9 %collective-permute-start.11 = (bf16[16,64,512]{2,1,0:T(8,128)(2,1)}, bf16[16,64,512]{2,1,0:T(8,128)(2,1)S(1)}, u32[]{:S(2)}, u32[]{:S(2)}) collective-permute-start(bf16[16,64,512]{2,1,0:T(8,128)(2,1)} %get-tuple-element.79), channel_id=1, source_target_pairs={{2,6},{6,10},{10,14},{14,18},{18,22},{22,26},{26,30},{30,2},{3,7},... | collective-permute-start | bytes 3145736 | tf_op jit(solution)/shard_map/ppermute | solution.py:249
  43.9 68.0 %collective-permute-start.13 = (bf16[16,64,256]{2,1,0:T(8,128)(2,1)S(1)}, bf16[16,64,256]{2,1,0:T(8,128)(2,1)S(1)}, u32[]{:S(2)}, u32[]{:S(2)}) collective-permute-start(bf16[16,64,256]{2,1,0:T(8,128)(2,1)S(1)} %get-tuple-element.78), channel_id=1, source_target_pairs={{0,4},{2,6},{4,8},{6,10},{8,12},{10,14},{12,16},{14,18},{16,20},{1... | collective-permute-start | bytes 1572872 | tf_op jit(solution)/shard_map/ppermute | solution.py:257
  45.2 73.0 %collective-permute-start.14 = (bf16[16,64,256]{2,1,0:T(8,128)(2,1)S(1)}, bf16[16,64,256]{2,1,0:T(8,128)(2,1)S(1)}, u32[]{:S(2)}, u32[]{:S(2)}) collective-permute-start(bf16[16,64,256]{2,1,0:T(8,128)(2,1)S(1)} %get-tuple-element.77), channel_id=1, source_target_pairs={{0,4},{2,6},{4,8},{6,10},{8,12},{10,14},{12,16},{14,18},{16,20},{1... | collective-permute-start | bytes 1572872 | tf_op jit(solution)/shard_map/ppermute | solution.py:257
  45.3 2.2 %copy-start.1 = (bf16[16,64,2048]{2,1,0:T(8,128)(2,1)S(1)}, bf16[16,64,2048]{2,1,0:T(8,128)(2,1)}, u32[]{:S(2)}) copy-start(bf16[16,64,2048]{2,1,0:T(8,128)(2,1)} %own.7) | copy-start | bytes 12582916
  46.1 38.4 %collective-permute-start.7 = (bf16[512,128]{1,0:T(8,128)(2,1)S(1)}, bf16[512,128]{1,0:T(8,128)(2,1)S(1)}, u32[]{:S(2)}, u32[]{:S(2)}) collective-permute-start(bf16[512,128]{1,0:T(8,128)(2,1)S(1)} %dynamic-slice_convert_fusion.3), channel_id=1, source_target_pairs={{0,4},{2,6},{4,0},{6,2},{8,12},{10,14},{12,8},{14,10},{16,20},{18,... | collective-permute-start | bytes 393224 | tf_op jit(solution)/shard_map/ppermute | solution.py:201
  84.5 16.2 %collective-permute-start.8 = (bf16[512,128]{1,0:T(8,128)(2,1)S(1)}, bf16[512,128]{1,0:T(8,128)(2,1)S(1)}, u32[]{:S(2)}, u32[]{:S(2)}) collective-permute-start(bf16[512,128]{1,0:T(8,128)(2,1)S(1)} %fusion.9), channel_id=1, source_target_pairs={{0,8},{2,10},{4,12},{6,14},{8,0},{10,2},{12,4},{14,6},{16,24},{18,... | collective-permute-start | bytes 393224 | tf_op jit(solution)/shard_map/ppermute | solution.py:201
  100.8 11.0 %collective-permute-start.9 = (bf16[512,128]{1,0:T(8,128)(2,1)S(1)}, bf16[512,128]{1,0:T(8,128)(2,1)S(1)}, u32[]{:S(2)}, u32[]{:S(2)}) collective-permute-start(bf16[512,128]{1,0:T(8,128)(2,1)S(1)} %fusion.8), channel_id=1, source_target_pairs={{0,16},{2,18},{4,20},{6,22},{8,24},{10,26},{12,28},{14,30},{16,0},... | collective-permute-start | bytes 393224 | tf_op jit(solution)/shard_map/ppermute | solution.py:201
  111.9 6.0 %collective-permute-start.12 = (bf16[512,128]{1,0:T(8,128)(2,1)S(1)}, bf16[512,128]{1,0:T(8,128)(2,1)S(1)}, u32[]{:S(2)}, u32[]{:S(2)}) collective-permute-start(bf16[512,128]{1,0:T(8,128)(2,1)S(1)} %add_convert_fusion.1), channel_id=1, source_target_pairs={{0,4},{2,6},{4,0},{6,2},{8,12},{10,14},{12,8},{14,10},{16,20},{18,... | collective-permute-start | bytes 393224 | tf_op jit(solution)/shard_map/ppermute | solution.py:201
  126.6 3.3 %collective-permute-start.15 = (bf16[32,64,128]{2,1,0:T(8,128)(2,1)}, bf16[32,64,128]{2,1,0:T(8,128)(2,1)S(1)}, u32[]{:S(2)}, u32[]{:S(2)}) collective-permute-start(bf16[32,64,128]{2,1,0:T(8,128)(2,1)} %get-tuple-element.64), channel_id=1, source_target_pairs={{0,2},{2,0},{4,6},{6,4},{8,10},{10,8},{12,14},{14,12},{16,18},{18,... | collective-permute-start | bytes 1572872 | tf_op jit(solution)/shard_map/ppermute | solution.py:369
  130.2 8.2 %collective-permute-start.18 = (bf16[16,32,128]{2,1,0:T(8,128)(2,1)S(1)}, bf16[16,32,128]{2,1,0:T(8,128)(2,1)S(1)}, u32[]{:S(2)}, u32[]{:S(2)}) collective-permute-start(bf16[16,32,128]{2,1,0:T(8,128)(2,1)S(1)} %dynamic-slice_convert_fusion), channel_id=1, source_target_pairs={{2,3},{3,2},{6,7},{7,6},{10,11},{11,10},{14,15},{15,14},{18,19},{1... | collective-permute-start | bytes 393224 | tf_op jit(solution)/shard_map/ppermute | solution.py:380
  133.4 5.0 %collective-permute-start.17 = (bf16[16,32,128]{2,1,0:T(8,128)(2,1)S(1)}, bf16[16,32,128]{2,1,0:T(8,128)(2,1)S(1)}, u32[]{:S(2)}, u32[]{:S(2)}) collective-permute-start(bf16[16,32,128]{2,1,0:T(8,128)(2,1)S(1)} %get-tuple-element.84), channel_id=1, source_target_pairs={{0,1},{1,0},{4,5},{5,4},{8,9},{9,8},{12,13},{13,12},{16,17},{17,16... | collective-permute-start | bytes 393224 | tf_op jit(solution)/shard_map/ppermute | solution.py:380
  133.5 5.7 %collective-permute-start.16 = (bf16[16,32,128]{2,1,0:T(8,128)(2,1)S(1)}, bf16[16,32,128]{2,1,0:T(8,128)(2,1)S(1)}, u32[]{:S(2)}, u32[]{:S(2)}) collective-permute-start(bf16[16,32,128]{2,1,0:T(8,128)(2,1)S(1)} %get-tuple-element.83), channel_id=1, source_target_pairs={{2,30},{3,31},{6,2},{7,3},{10,6},{11,7},{14,10},{15,11},{18,14},{1... | collective-permute-start | bytes 393224 | tf_op jit(solution)/shard_map/ppermute | solution.py:380

commit v4 on v3

--- a/solution.py
+++ b/solution.py
@@ -64,6 +64,23 @@
             out_ref[k] += made
 
 
+def pack_kernel(core, source, *refs):
+    outs, sems = refs[:-1], refs[-1]
+    half_g, size = source.shape[2] // 2, outs[0].shape[2]
+    if len(outs) == 1:
+        starts = [pl.multiple_of((1 - core[0]) * half_g, size)]
+    else:
+        starts = [0, half_g]
+    copies = [
+        pltpu.make_async_copy(source.at[:, :, pl.ds(start, size)], out, sems.at[i])
+        for i, (start, out) in enumerate(zip(starts, outs))
+    ]
+    for copy in copies:
+        copy.start()
+    for copy in copies:
+        copy.wait()
+
+
 def near_kernel(start, count, load, *refs):
     if load:
         core, listed, rounds, own, vec, sib, vec_s, screen, out, w, prod, total, sems = refs
@@ -235,26 +252,30 @@
     table = jnp.concatenate([offset * local_k + neighbors % local_k, q_index, live_count[:, None]], axis=1)
     table_s = lax.ppermute(table, "ka", sibling)
     vec_s = lax.ppermute(trial_vectors, "ka", sibling)
-    table_p, vec_p = (
-        pick(*(lax.ppermute(value, "ka", pairs) for pairs in to_next)) for value in (table, trial_vectors)
-    )
-
-    give_half = lax.dynamic_slice_in_dim(pair_density, (1 - core) * half_g, half_g, 2)
+    edge = (pick(table_s, table), pick(vec_s, trial_vectors))
+    table_p, vec_p = (lax.ppermute(value, "ka", onward) for value in edge)
+
+    def packed(core_id, last, count):
+        return pl.pallas_call(
+            pack_kernel,
+            out_shape=[jax.ShapeDtypeStruct((local_k, pair_count, last), BF16)] * count,
+            in_specs=[IN_SMEM, ANYWHERE],
+            out_specs=[ANYWHERE] * count,
+            scratch_shapes=[pltpu.SemaphoreType.DMA((count,))],
+        )(core_id, pair_density)
+
+    (give_half,) = packed(core_id, half_g, 1)
+    first_pieces = packed(lax.optimization_barrier((core_id, *edge))[0], width, 2)
     sib = lax.ppermute(give_half, "ka", sibling)
     own_half = lax.dynamic_slice_in_dim(pair_density, core * half_g, half_g, 2)
-    lead = max(groups // 2, 1)
-    chunks = [(0, lead)] + [(g, 1) for g in range(lead, groups)]
-    came = [
-        [
-            lax.ppermute(pair_density[:, :, low : low + lead * width], "ka", pairs)
-            for low, pairs in zip((0, half_g), to_next)
-        ]
-    ]
-    sending = [
-        pick(sib[:, :, g * width : (g + 1) * width], own_half[:, :, g * width : (g + 1) * width])
-        for g in range(lead, groups)
-    ]
-    came += [[lax.ppermute(piece, "ka", onward)] for piece in sending]
+    came = [[lax.ppermute(piece, "ka", pairs) for piece, pairs in zip(first_pieces, to_next)]]
+
+    def send_group(g, value):
+        piece = pick(sib[:, :, g * width : (g + 1) * width], own_half[:, :, g * width : (g + 1) * width])
+        piece, value = lax.optimization_barrier((piece, value))
+        came.append([lax.ppermute(piece, "ka", onward)])
+        piece, value = lax.optimization_barrier((piece, value))
+        return value
 
     contract = lambda v, d: lax.dot_general(d, v, (((0, 1), (0, 1)), ((), ())), preferred_element_type=F32)
     part = contract(trial_vectors, own_half) + contract(vec_s, sib)
@@ -310,10 +331,12 @@
         )
 
     near_groups = (groups + 1) // 2
-    near_rounds, vec_p, far_list, far_rounds, *_ = lax.optimization_barrier(
-        (near_rounds, vec_p, far_list, far_rounds, *sending)
+    near_rounds, vec_p, far_list, far_rounds = lax.optimization_barrier(
+        (near_rounds, vec_p, far_list, far_rounds)
     )
     near_rounds = density.before(near_rounds)
+    if groups > 1:
+        near_rounds = send_group(1, near_rounds)
     near, w_half = pl.pallas_call(
         functools.partial(near_kernel, 0, near_groups, True),
         out_shape=(sums, jax.ShapeDtypeStruct((q_count, half_g, width), BF16)),
@@ -324,6 +347,8 @@
         cost_estimate=cost(near_groups, 160),
     )(core_id, near_list, near_rounds, pair_density, trial_vectors, sib, vec_s, screen)
     near = density.after(near)
+    if groups > 2:
+        near = send_group(2, near)
     if groups > near_groups:
         near = pl.pallas_call(
             functools.partial(near_kernel, near_groups, groups - near_groups, False),
@@ -336,25 +361,26 @@
             cost_estimate=cost(groups - near_groups, 160),
         )(core_id, near_list, near_rounds, pair_density, trial_vectors, sib, vec_s, w_half, near)
         near = density.after(near)
+    for g in range(3, groups):
+        near = send_group(g, near)
     near, far_rounds = lax.optimization_barrier((near, far_rounds))
-    far_rounds = density.before(far_rounds)
     far = None
-    for c, (start, count) in enumerate(chunks):
+    for c in range(groups):
         far = pl.pallas_call(
-            functools.partial(far_kernel, start, count, c == 0, len(came[c])),
+            functools.partial(far_kernel, c, 1, c == 0, len(came[c])),
             out_shape=sums,
             in_specs=[IN_SMEM] * 3 + [IN_VMEM] * (6 + (c > 0)) + [ANYWHERE] * len(came[c]),
             out_specs=IN_VMEM,
             scratch_shapes=work
-            + [VMEM((local_k, pair_count, count * width), BF16), pltpu.SemaphoreType.DMA],
+            + [VMEM((local_k, pair_count, width), BF16), pltpu.SemaphoreType.DMA],
             input_output_aliases={9: 0} if c else {},
             compiler_params=params(),
-            cost_estimate=cost(count, 80),
+            cost_estimate=cost(1, 80),
         )(
             core_id, far_list, far_rounds, pair_density, trial_vectors, sib, vec_s, w_half, vec_p,
             *([far] if c else []), *came[c],
         )
-        if c + 1 < len(chunks):
+        if c % 2 == 1:
             far = density.after(far)
     screened2 = (2.0 * my_coulomb[:, None] * density.finish().astype(F32)).astype(BF16)
     give, keep = pl.pallas_call(

time: 139 us -> 210 us (1.51)
  Pallas kernels: 59.7 us -> 148 us
  waiting for transfers between devices: 24.1 us -> 15.9 us
  local copies, waits for them, and re-layouts: 11 us -> 3.13 us
  other arithmetic: 7.9 us -> 4.91 us
    pallas_call x3 -> x6, Pallas kernels: 22.9 us -> 118 us  [the longest x2 97.5 us: packed(): pl.pallas_call(pack_kernel, out_shape=[jax.ShapeDtypeStruct((local_k, pai...]
    ppermute x8 -> x7, starting transfers between devices: 23.4 us -> 10.9 us  [the longest x2 6.13 us: on_device(): lax.ppermute(piece, 'ka', pairs)]
    ppermute x4, waiting for transfers between devices: 18.6 us -> 6.88 us  [after(): lax.ppermute(self.give, 'ka', [(i, i ^ self.bit) for i in range(self.size)])]
    ppermute x4, starting transfers between devices: 1.34 us -> 12.2 us  [after(): lax.ppermute(self.give, 'ka', [(i, i ^ self.bit) for i in range(self.size)])]
    ppermute x8 -> x7, waiting for transfers between devices: 0.02 us -> 3.61 us  [the longest x2 3.59 us: on_device(): table_p, vec_p = (lax.ppermute(value, 'ka', onward) for value in edge)]
    pallas_call x1, Pallas kernels: 16.1 us -> 12.7 us  [on_device(): pl.pallas_call(functools.partial(near_kernel, near_groups, groups - near_...]
    pallas_call x1, Pallas kernels: 18.4 us -> 15 us  [on_device(): pl.pallas_call(functools.partial(near_kernel, 0, near_groups, True), out_...]
    dynamic_slice x1 -> x0, local copies, waits for them, and re-layouts: 3.22 us -> none  [on_device(): lax.dynamic_slice_in_dim(pair_density, (1 - core) * half_g, half_g, 2)]
  transfers between devices with their start and end apart: 19 -> 18, of which waited for: 4 -> 6; matrix products, arithmetic and copies ran while one was open for 14% -> 6% of each run, Pallas kernels for 37% -> 39%
where the time goes in v4:
time: 210 us
  Pallas kernels  148 us (70%)
  starting transfers between devices  31.2 us (15%)
  waiting for transfers between devices  15.9 us (8%)
  matrix products  5.07 us (2%)
  other arithmetic  4.91 us (2%)
  local copies, waits for them, and re-layouts  3.13 us (1%)
    pallas_call x2, Pallas kernels, packed(): pl.pallas_call(pack_kernel, out_shape=[jax.ShapeDtypeStruct((local_k, pai...  97.5 us
    pallas_call x4, Pallas kernels, on_device(): pl.pallas_call(functools.partial(far_kernel, c, 1, c == 0, len(came[c])),...  20.6 us
    pallas_call x1, Pallas kernels, on_device(): pl.pallas_call(functools.partial(near_kernel, 0, near_groups, True), out_...  15 us
    pallas_call x1, Pallas kernels, on_device(): pl.pallas_call(functools.partial(near_kernel, near_groups, groups - near_...  12.7 us
    ppermute x4, starting transfers between devices, after(): lax.ppermute(self.give, 'ka', [(i, i ^ self.bit) for i in range(self.size)])  12.2 us
    ppermute x4, waiting for transfers between devices, after(): lax.ppermute(self.give, 'ka', [(i, i ^ self.bit) for i in range(self.size)])  6.88 us
    ppermute x2, starting transfers between devices, on_device(): lax.ppermute(piece, 'ka', pairs)  6.13 us
    ppermute x3, starting transfers between devices, sent(): lax.ppermute(rows_of(value, (mine + steps) % parts).astype(BF16), ('ka',...  5.32 us
  transfers between devices with their start and end apart: 18, of which 6 were waited for; matrix products, arithmetic and copies ran while one was open for 6% of the time, Pallas kernels for 39%

profile of v4, /device:TPU:1, one launch (start us, length us, event | category | flops | bytes accessed | tf_op | source)
XLA Modules:
  0.0 210.0 jit_solution(9506161275237735966)
XLA Ops:
  0.0 64.6 %shard_map.82 = bf16[16,64,1024]{2,1,0:T(8,128)(2,1)} custom-call(s32[1]{0:T(128)} %bitcast.core.refs_0_, bf16[16,64,2048]{2,1,0:T(8,128)(2,1)} %own.9), custom_call_target="tpu_custom_call" | custom-call | tf_op jit(solution)/shard_map/pallas_call | solution.py:259
  64.7 0.1 collective-permute-start
  64.8 0.5 collective-permute-start.1
  65.7 3.1 %fusion.2 = f32[1024,128]{1,0:T(8,128)} fusion(bf16[16,64,128]{2,1,0:T(8,128)(2,1)S(1)} %copy-done.2, bf16[16,64,2048]{2,1,0:T(8,128)(2,1)} %own.9, s32[]{:T(128)S(6)} %select_n.197), kind=kOutput, calls=%fused_computation.2 | convolution fusion | flops 268435456 | bytes 2883588 | tf_op jit(solution)/shard_map/dot_general | solution.py:280
  69.4 0.2 dynamic-update-slice.4
  69.7 0.2 slice_reduce_fusion.2
  70.1 0.2 dynamic-update-slice.5
  70.3 0.1 convert_reduce_fusion.3
  70.5 0.3 convert_reduce_fusion
  70.8 0.2 slice_reduce_fusion.1
  71.2 2.7 %collective-permute-start.4 = (s32[16,33]{1,0:T(8,128)S(1)}, s32[16,33]{1,0:T(8,128)S(1)}, u32[]{:S(2)}, u32[]{:S(2)}) collective-permute-start(s32[16,33]{1,0:T(8,128)S(1)} %get-tuple-element.102), channel_id=1, source_target_pairs={{0,4},{2,6},{4,8},{6,10},{8,12},{10,14},{12,16},{14,18},{16,20},{1... | collective-permute-start | bytes 6344 | tf_op jit(solution)/shard_map/ppermute | solution.py:256
  74.2 0.2 dynamic-update-slice.2
  74.4 3.6 %collective-permute-done.4 = s32[16,33]{1,0:T(8,128)S(1)} collective-permute-done((s32[16,33]{1,0:T(8,128)S(1)}, s32[16,33]{1,0:T(8,128)S(1)}, u32[]{:S(2)}, u32[]{:S(2)}) %collective-permute-start.4) | collective-permute-done | bytes 2144 | tf_op jit(solution)/shard_map/ppermute | solution.py:256
  78.0 0.2 slice_reduce_fusion
  78.5 0.2 dynamic-update-slice.3
  78.7 0.1 convert_reduce_fusion.2
  78.8 0.7 fusion.43
  79.8 0.3 convert_reduce_fusion.1
  80.1 0.2 select_reduce_fusion.1
  80.5 0.2 select_reduce_fusion
  82.0 32.9 %shard_map.85 = (bf16[16,64,256]{2,1,0:T(8,128)(2,1)}, bf16[16,64,256]{2,1,0:T(8,128)(2,1)}) custom-call(s32[1]{0:T(128)} %bitcast.core.refs_0_, bf16[16,64,2048]{2,1,0:T(8,128)(2,1)} %own.9), custom_call_target="tpu_custom_call" | custom-call | tf_op jit(solution)/shard_map/pallas_call | solution.py:259
  114.9 3.9 %collective-permute-start.8 = (bf16[16,64,256]{2,1,0:T(8,128)(2,1)}, bf16[16,64,256]{2,1,0:T(8,128)(2,1)S(1)}, u32[]{:S(2)}, u32[]{:S(2)}) collective-permute-start(bf16[16,64,256]{2,1,0:T(8,128)(2,1)} %get-tuple-element.66), channel_id=1, source_target_pairs={{2,4},{6,8},{10,12},{14,16},{18,20},{22,24},{26,28},{30,0},{3,5},{... | collective-permute-start | bytes 1572872 | tf_op jit(solution)/shard_map/ppermute | solution.py:271
  118.8 2.2 %collective-permute-start.9 = (bf16[16,64,256]{2,1,0:T(8,128)(2,1)}, bf16[16,64,256]{2,1,0:T(8,128)(2,1)S(1)}, u32[]{:S(2)}, u32[]{:S(2)}) collective-permute-start(bf16[16,64,256]{2,1,0:T(8,128)(2,1)} %get-tuple-element.67), channel_id=1, source_target_pairs={{2,6},{6,10},{10,14},{14,18},{18,22},{22,26},{26,30},{30,2},{3,7},... | collective-permute-start | bytes 1572872 | tf_op jit(solution)/shard_map/ppermute | solution.py:271
  121.0 1.9 fusion.5
  123.0 2.2 %collective-permute-start.5 = (bf16[512,128]{1,0:T(8,128)(2,1)S(1)}, bf16[512,128]{1,0:T(8,128)(2,1)S(1)}, u32[]{:S(2)}, u32[]{:S(2)}) collective-permute-start(bf16[512,128]{1,0:T(8,128)(2,1)S(1)} %dynamic-slice_convert_fusion.3), channel_id=1, source_target_pairs={{0,4},{2,6},{4,0},{6,2},{8,12},{10,14},{12,8},{14,10},{16,20},{18,... | collective-permute-start | bytes 393224 | tf_op jit(solution)/shard_map/ppermute | solution.py:218
  125.2 0.6 dynamic-slice_select_fusion
  125.8 0.3 collective-permute-start.10
  126.2 15.0 %shard_map.83 = (f32[32,64,128]{2,1,0:T(8,128)S(1)}, bf16[32,1024,256]{2,1,0:T(8,128)(2,1)S(1)}) custom-call(s32[1]{0:T(128)} %bitcast.core.refs_0_, s32[544]{0:T(1024)S(1)} %broadcast_add_fusion.refs_1_, s32[1]{0:T(128)} %bitcast.4.refs_2_, bf16[16,64,2048]{2,1,0:T(8,128)(2,1)S(1)} %copy-done.1, bf16[16,64,128]{2,1,0:T(8,128)(2,1)S(1)} %copy-done.2, ...), custom_call_target="tpu_custom_call" | custom-call | flops 10737418240 | bytes 1048576 | tf_op jit(solution)/shard_map/pallas_call | solution.py:340
  141.2 6.9 %collective-permute-done.5 = bf16[512,128]{1,0:T(8,128)(2,1)S(1)} collective-permute-done((bf16[512,128]{1,0:T(8,128)(2,1)S(1)}, bf16[512,128]{1,0:T(8,128)(2,1)S(1)}, u32[]{:S(2)}, u32[]{:S(2)}) %collective-permute-start.5) | collective-permute-done | bytes 131104 | tf_op jit(solution)/shard_map/ppermute | solution.py:218
  148.3 12.7 %shard_map.84.near = f32[32,64,128]{2,1,0:T(8,128)S(1)} custom-call(s32[1]{0:T(128)} %bitcast.core.refs_0_, s32[544]{0:T(1024)S(1)} %broadcast_add_fusion.refs_1_, s32[1]{0:T(128)} %bitcast.4.refs_2_, bf16[16,64,2048]{2,1,0:T(8,128)(2,1)S(1)} %copy-done.1, bf16[16,64,128]{2,1,0:T(8,128)(2,1)S(1)} %copy-done.2, ...), custom_call_target="tpu_custom_call", output_to_operand_aliasing={{}: (8, {})} | custom-call | flops 10737418240 | bytes 1048576 | tf_op jit(solution)/shard_map/pallas_call | solution.py:353
  161.0 1.1 collective-permute-start.7
  162.1 1.6 collective-permute-start.13
  163.7 5.0 %shard_map.86.refs_0_ = f32[32,64,128]{2,1,0:T(8,128)S(1)} custom-call(s32[1]{0:T(128)} %bitcast.core.refs_0_, s32[544]{0:T(1024)S(1)} %broadcast_add_fusion.1.listed, s32[1]{0:T(128)} %bitcast.5.rounds, bf16[16,64,2048]{2,1,0:T(8,128)(2,1)S(1)} %copy-done.1, bf16[16,64,128]{2,1,0:T(8,128)(2,1)S(1)} %copy-done.2, ...), custom_call_target="tpu_custom_call" | custom-call | flops 2684354560 | bytes 1048576 | tf_op jit(solution)/shard_map/pallas_call | solution.py:369
  168.8 5.1 %shard_map.87.refs_0_ = f32[32,64,128]{2,1,0:T(8,128)S(1)} custom-call(s32[1]{0:T(128)} %bitcast.core.refs_0_, s32[544]{0:T(1024)S(1)} %broadcast_add_fusion.1.listed, s32[1]{0:T(128)} %bitcast.5.rounds, bf16[16,64,2048]{2,1,0:T(8,128)(2,1)S(1)} %copy-done.1, bf16[16,64,128]{2,1,0:T(8,128)(2,1)S(1)} %copy-done.2, ...), custom_call_target="tpu_custom_call", output_to_operand_aliasing={{}: (9, {})} | custom-call | flops 2684354560 | bytes 1048576 | tf_op jit(solution)/shard_map/pallas_call | solution.py:369
  174.0 8.9 %collective-permute-start.11 = (bf16[512,128]{1,0:T(8,128)(2,1)S(1)}, bf16[512,128]{1,0:T(8,128)(2,1)S(1)}, u32[]{:S(2)}, u32[]{:S(2)}) collective-permute-start(bf16[512,128]{1,0:T(8,128)(2,1)S(1)} %add_convert_fusion.1), channel_id=1, source_target_pairs={{0,4},{2,6},{4,0},{6,2},{8,12},{10,14},{12,8},{14,10},{16,20},{18,... | collective-permute-start | bytes 393224 | tf_op jit(solution)/shard_map/ppermute | solution.py:218
  182.9 5.1 %shard_map.88.refs_0_ = f32[32,64,128]{2,1,0:T(8,128)S(1)} custom-call(s32[1]{0:T(128)} %bitcast.core.refs_0_, s32[544]{0:T(1024)S(1)} %broadcast_add_fusion.1.listed, s32[1]{0:T(128)} %bitcast.5.rounds, bf16[16,64,2048]{2,1,0:T(8,128)(2,1)S(1)} %copy-done.1, bf16[16,64,128]{2,1,0:T(8,128)(2,1)S(1)} %copy-done.2, ...), custom_call_target="tpu_custom_call", output_to_operand_aliasing={{}: (9, {})} | custom-call | flops 2684354560 | bytes 1048576 | tf_op jit(solution)/shard_map/pallas_call | solution.py:369
  188.0 5.4 %shard_map.89.far = f32[32,64,128]{2,1,0:T(8,128)S(1)} custom-call(s32[1]{0:T(128)} %bitcast.core.refs_0_, s32[544]{0:T(1024)S(1)} %broadcast_add_fusion.1.listed, s32[1]{0:T(128)} %bitcast.5.rounds, bf16[16,64,2048]{2,1,0:T(8,128)(2,1)S(1)} %copy-done.1, bf16[16,64,128]{2,1,0:T(8,128)(2,1)S(1)} %copy-done.2, ...), custom_call_target="tpu_custom_call", output_to_operand_aliasing={{}: (9, {})} | custom-call | flops 2684354560 | bytes 1048576 | tf_op jit(solution)/shard_map/pallas_call | solution.py:369
  193.5 0.2 multiply_convert_fusion.s2
  193.7 2.2 %shard_map.90 = (bf16[32,64,128]{2,1,0:T(8,128)(2,1)}, f32[32,64,128]{2,1,0:T(8,128)S(1)}) custom-call(s32[1]{0:T(128)} %bitcast.core.refs_0_, bf16[16,64,2048]{2,1,0:T(8,128)(2,1)S(1)} %copy-done.1, bf16[16,64,1024]{2,1,0:T(8,128)(2,1)S(1)} %collective-permute-done.refs_5_.sib, bf16[1024,128]{1,0:T(8,128)(2,1)S(1)} %multiply_convert_fusion.s2, ...), custom_call_target="tpu_custom_call" | custom-call | flops 536870912 | bytes 1048576 | tf_op jit(solution)/shard_map/pallas_call | solution.py:386
  195.9 2.1 collective-permute-start.14
  197.9 1.7 collective-permute-done.14
  199.7 0.2 convert_add_fusion
  200.0 3.3 %collective-permute-start.17 = (bf16[16,32,128]{2,1,0:T(8,128)(2,1)S(1)}, bf16[16,32,128]{2,1,0:T(8,128)(2,1)S(1)}, u32[]{:S(2)}, u32[]{:S(2)}) collective-permute-start(bf16[16,32,128]{2,1,0:T(8,128)(2,1)S(1)} %dynamic-slice_convert_fusion), channel_id=1, source_target_pairs={{2,3},{3,2},{6,7},{7,6},{10,11},{11,10},{14,15},{15,14},{18,19},{1... | collective-permute-start | bytes 393224 | tf_op jit(solution)/shard_map/ppermute | solution.py:406
  203.5 1.9 collective-permute-start.15
  205.5 2.3 %collective-permute-done.17 = bf16[16,32,128]{2,1,0:T(8,128)(2,1)S(1)} collective-permute-done((bf16[16,32,128]{2,1,0:T(8,128)(2,1)S(1)}, bf16[16,32,128]{2,1,0:T(8,128)(2,1)S(1)}, u32[]{:S(2)}, u32[]{:S(2)}) %collective-permute-start.17) | collective-permute-done | bytes 131104 | tf_op jit(solution)/shard_map/ppermute | solution.py:406
  207.8 0.5 collective-permute-done.16
  208.2 0.9 collective-permute-done.15
  209.2 0.8 add_convert_fusion
  (85 shorter events, 3.3 us)
Async XLA Ops:
  0.0 205.4 %copy-start = (f32[16,64]{1,0:T(8,128)S(1)}, f32[16,64]{1,0:T(8,128)}, u32[]{:S(2)}) copy-start(f32[16,64]{1,0:T(8,128)} %param.10) | copy-start | bytes 12292
  0.0 64.8 %copy-start.2 = (bf16[16,64,128]{2,1,0:T(8,128)(2,1)S(1)}, bf16[16,64,128]{2,1,0:T(8,128)(2,1)}, u32[]{:S(2)}) copy-start(bf16[16,64,128]{2,1,0:T(8,128)(2,1)} %vec.7) | copy-start | bytes 786436
  0.0 65.3 %copy-start.5 = (s32[16]{0:T(128)S(1)}, s32[16]{0:T(128)}, u32[]{:S(2)}) copy-start(s32[16]{0:T(128)} %param.14) | copy-start | bytes 196
  0.0 65.3 %copy-start.4 = (s32[16,16]{1,0:T(8,128)S(1)}, s32[16,16]{1,0:T(8,128)}, u32[]{:S(2)}) copy-start(s32[16,16]{1,0:T(8,128)} %param.13) | copy-start | bytes 3076
  0.0 65.4 %copy-start.3 = (s32[16,16]{1,0:T(8,128)S(1)}, s32[16,16]{1,0:T(8,128)}, u32[]{:S(2)}) copy-start(s32[16,16]{1,0:T(8,128)} %param.15) | copy-start | bytes 3076
  64.7 56.3 %collective-permute-start = (bf16[16,64,1024]{2,1,0:T(8,128)(2,1)}, bf16[16,64,1024]{2,1,0:T(8,128)(2,1)S(1)}, u32[]{:S(2)}, u32[]{:S(2)}) collective-permute-start(bf16[16,64,1024]{2,1,0:T(8,128)(2,1)} %shard_map.82), channel_id=1, source_target_pairs={{0,2},{2,0},{4,6},{6,4},{8,10},{10,8},{12,14},{14,12},{16,18},{18,... | collective-permute-start | bytes 6291464 | tf_op jit(solution)/shard_map/ppermute | solution.py:269
  64.8 15.6 %collective-permute-start.1 = (bf16[16,64,128]{2,1,0:T(8,128)(2,1)S(1)}, bf16[16,64,128]{2,1,0:T(8,128)(2,1)S(1)}, u32[]{:S(2)}, u32[]{:S(2)}) collective-permute-start(bf16[16,64,128]{2,1,0:T(8,128)(2,1)S(1)} %copy-done.2), channel_id=1, source_target_pairs={{0,2},{2,0},{4,6},{6,4},{8,10},{10,8},{12,14},{14,12},{16,18},{18,... | collective-permute-start | bytes 786440 | tf_op jit(solution)/shard_map/ppermute | solution.py:254
  65.5 4.1 %collective-permute-start.2 = (s32[16,33]{1,0:T(8,128)S(1)}, s32[16,33]{1,0:T(8,128)S(1)}, u32[]{:S(2)}, u32[]{:S(2)}) collective-permute-start(s32[16,33]{1,0:T(8,128)S(1)} %pad_add_fusion), channel_id=1, source_target_pairs={{0,2},{2,0},{4,6},{6,4},{8,10},{10,8},{12,14},{14,12},{16,18},{18,... | collective-permute-start | bytes 6344 | tf_op jit(solution)/shard_map/ppermute | solution.py:253
  65.7 3.1 %copy-start.6 = (f32[2048]{0:T(1024)S(1)}, f32[2048]{0:T(1024)}, u32[]{:S(2)}) copy-start(f32[2048]{0:T(1024)} %param.11) | copy-start | bytes 24580
  71.2 6.7 %collective-permute-start.4 = (s32[16,33]{1,0:T(8,128)S(1)}, s32[16,33]{1,0:T(8,128)S(1)}, u32[]{:S(2)}, u32[]{:S(2)}) collective-permute-start(s32[16,33]{1,0:T(8,128)S(1)} %get-tuple-element.102), channel_id=1, source_target_pairs={{0,4},{2,6},{4,8},{6,10},{8,12},{10,14},{12,16},{14,18},{16,20},{1... | collective-permute-start | bytes 6344 | tf_op jit(solution)/shard_map/ppermute | solution.py:256
  80.4 40.6 %collective-permute-start.3 = (bf16[16,64,128]{2,1,0:T(8,128)(2,1)S(1)}, bf16[16,64,128]{2,1,0:T(8,128)(2,1)S(1)}, u32[]{:S(2)}, u32[]{:S(2)}) collective-permute-start(bf16[16,64,128]{2,1,0:T(8,128)(2,1)S(1)} %broadcast_select_fusion), channel_id=1, source_target_pairs={{0,4},{2,6},{4,8},{6,10},{8,12},{10,14},{12,16},{14,18},{16,20},{1... | collective-permute-start | bytes 786440 | tf_op jit(solution)/shard_map/ppermute | solution.py:256
  114.9 47.3 %collective-permute-start.8 = (bf16[16,64,256]{2,1,0:T(8,128)(2,1)}, bf16[16,64,256]{2,1,0:T(8,128)(2,1)S(1)}, u32[]{:S(2)}, u32[]{:S(2)}) collective-permute-start(bf16[16,64,256]{2,1,0:T(8,128)(2,1)} %get-tuple-element.66), channel_id=1, source_target_pairs={{2,4},{6,8},{10,12},{14,16},{18,20},{22,24},{26,28},{30,0},{3,5},{... | collective-permute-start | bytes 1572872 | tf_op jit(solution)/shard_map/ppermute | solution.py:271
  118.8 45.0 %collective-permute-start.9 = (bf16[16,64,256]{2,1,0:T(8,128)(2,1)}, bf16[16,64,256]{2,1,0:T(8,128)(2,1)S(1)}, u32[]{:S(2)}, u32[]{:S(2)}) collective-permute-start(bf16[16,64,256]{2,1,0:T(8,128)(2,1)} %get-tuple-element.67), channel_id=1, source_target_pairs={{2,6},{6,10},{10,14},{14,18},{18,22},{22,26},{26,30},{30,2},{3,7},... | collective-permute-start | bytes 1572872 | tf_op jit(solution)/shard_map/ppermute | solution.py:271
  121.0 4.2 %copy-start.1 = (bf16[16,64,2048]{2,1,0:T(8,128)(2,1)S(1)}, bf16[16,64,2048]{2,1,0:T(8,128)(2,1)}, u32[]{:S(2)}) copy-start(bf16[16,64,2048]{2,1,0:T(8,128)(2,1)} %own.9) | copy-start | bytes 12582916
  123.0 25.1 %collective-permute-start.5 = (bf16[512,128]{1,0:T(8,128)(2,1)S(1)}, bf16[512,128]{1,0:T(8,128)(2,1)S(1)}, u32[]{:S(2)}, u32[]{:S(2)}) collective-permute-start(bf16[512,128]{1,0:T(8,128)(2,1)S(1)} %dynamic-slice_convert_fusion.3), channel_id=1, source_target_pairs={{0,4},{2,6},{4,0},{6,2},{8,12},{10,14},{12,8},{14,10},{16,20},{18,... | collective-permute-start | bytes 393224 | tf_op jit(solution)/shard_map/ppermute | solution.py:218
  125.8 42.9 %collective-permute-start.10 = (bf16[16,64,256]{2,1,0:T(8,128)(2,1)S(1)}, bf16[16,64,256]{2,1,0:T(8,128)(2,1)S(1)}, u32[]{:S(2)}, u32[]{:S(2)}) collective-permute-start(bf16[16,64,256]{2,1,0:T(8,128)(2,1)S(1)} %get-tuple-element.68), channel_id=1, source_target_pairs={{0,4},{2,6},{4,8},{6,10},{8,12},{10,14},{12,16},{14,18},{16,20},{1... | collective-permute-start | bytes 1572872 | tf_op jit(solution)/shard_map/ppermute | solution.py:276
  148.1 12.9 %collective-permute-start.6 = (bf16[512,128]{1,0:T(8,128)(2,1)S(1)}, bf16[512,128]{1,0:T(8,128)(2,1)S(1)}, u32[]{:S(2)}, u32[]{:S(2)}) collective-permute-start(bf16[512,128]{1,0:T(8,128)(2,1)S(1)} %fusion.9), channel_id=1, source_target_pairs={{0,8},{2,10},{4,12},{6,14},{8,0},{10,2},{12,4},{14,6},{16,24},{18,... | collective-permute-start | bytes 393224 | tf_op jit(solution)/shard_map/ppermute | solution.py:218
  148.2 34.7 %collective-permute-start.12 = (bf16[16,64,256]{2,1,0:T(8,128)(2,1)S(1)}, bf16[16,64,256]{2,1,0:T(8,128)(2,1)S(1)}, u32[]{:S(2)}, u32[]{:S(2)}) collective-permute-start(bf16[16,64,256]{2,1,0:T(8,128)(2,1)S(1)} %get-tuple-element.73), channel_id=1, source_target_pairs={{0,4},{2,6},{4,8},{6,10},{8,12},{10,14},{12,16},{14,18},{16,20},{1... | collective-permute-start | bytes 1572872 | tf_op jit(solution)/shard_map/ppermute | solution.py:276
  161.0 12.9 %collective-permute-start.7 = (bf16[512,128]{1,0:T(8,128)(2,1)S(1)}, bf16[512,128]{1,0:T(8,128)(2,1)S(1)}, u32[]{:S(2)}, u32[]{:S(2)}) collective-permute-start(bf16[512,128]{1,0:T(8,128)(2,1)S(1)} %fusion.8), channel_id=1, source_target_pairs={{0,16},{2,18},{4,20},{6,22},{8,24},{10,26},{12,28},{14,30},{16,0},... | collective-permute-start | bytes 393224 | tf_op jit(solution)/shard_map/ppermute | solution.py:218
  162.1 25.9 %collective-permute-start.13 = (bf16[16,64,256]{2,1,0:T(8,128)(2,1)S(1)}, bf16[16,64,256]{2,1,0:T(8,128)(2,1)S(1)}, u32[]{:S(2)}, u32[]{:S(2)}) collective-permute-start(bf16[16,64,256]{2,1,0:T(8,128)(2,1)S(1)} %get-tuple-element.74), channel_id=1, source_target_pairs={{0,4},{2,6},{4,8},{6,10},{8,12},{10,14},{12,16},{14,18},{16,20},{1... | collective-permute-start | bytes 1572872 | tf_op jit(solution)/shard_map/ppermute | solution.py:276
  174.0 19.4 %collective-permute-start.11 = (bf16[512,128]{1,0:T(8,128)(2,1)S(1)}, bf16[512,128]{1,0:T(8,128)(2,1)S(1)}, u32[]{:S(2)}, u32[]{:S(2)}) collective-permute-start(bf16[512,128]{1,0:T(8,128)(2,1)S(1)} %add_convert_fusion.1), channel_id=1, source_target_pairs={{0,4},{2,6},{4,0},{6,2},{8,12},{10,14},{12,8},{14,10},{16,20},{18,... | collective-permute-start | bytes 393224 | tf_op jit(solution)/shard_map/ppermute | solution.py:218
  195.9 3.8 %collective-permute-start.14 = (bf16[32,64,128]{2,1,0:T(8,128)(2,1)}, bf16[32,64,128]{2,1,0:T(8,128)(2,1)S(1)}, u32[]{:S(2)}, u32[]{:S(2)}) collective-permute-start(bf16[32,64,128]{2,1,0:T(8,128)(2,1)} %get-tuple-element.81), channel_id=1, source_target_pairs={{0,2},{2,0},{4,6},{6,4},{8,10},{10,8},{12,14},{14,12},{16,18},{18,... | collective-permute-start | bytes 1572872 | tf_op jit(solution)/shard_map/ppermute | solution.py:395
  200.0 7.8 %collective-permute-start.17 = (bf16[16,32,128]{2,1,0:T(8,128)(2,1)S(1)}, bf16[16,32,128]{2,1,0:T(8,128)(2,1)S(1)}, u32[]{:S(2)}, u32[]{:S(2)}) collective-permute-start(bf16[16,32,128]{2,1,0:T(8,128)(2,1)S(1)} %dynamic-slice_convert_fusion), channel_id=1, source_target_pairs={{2,3},{3,2},{6,7},{7,6},{10,11},{11,10},{14,15},{15,14},{18,19},{1... | collective-permute-start | bytes 393224 | tf_op jit(solution)/shard_map/ppermute | solution.py:406
  203.4 4.8 %collective-permute-start.16 = (bf16[16,32,128]{2,1,0:T(8,128)(2,1)S(1)}, bf16[16,32,128]{2,1,0:T(8,128)(2,1)S(1)}, u32[]{:S(2)}, u32[]{:S(2)}) collective-permute-start(bf16[16,32,128]{2,1,0:T(8,128)(2,1)S(1)} %get-tuple-element.100), channel_id=1, source_target_pairs={{0,1},{1,0},{4,5},{5,4},{8,9},{9,8},{12,13},{13,12},{16,17},{17,16... | collective-permute-start | bytes 393224 | tf_op jit(solution)/shard_map/ppermute | solution.py:406
  203.5 5.7 %collective-permute-start.15 = (bf16[16,32,128]{2,1,0:T(8,128)(2,1)S(1)}, bf16[16,32,128]{2,1,0:T(8,128)(2,1)S(1)}, u32[]{:S(2)}, u32[]{:S(2)}) collective-permute-start(bf16[16,32,128]{2,1,0:T(8,128)(2,1)S(1)} %get-tuple-element.99), channel_id=1, source_target_pairs={{2,30},{3,31},{6,2},{7,3},{10,6},{11,7},{14,10},{15,11},{18,14},{1... | collective-permute-start | bytes 393224 | tf_op jit(solution)/shard_map/ppermute | solution.py:406

commit v5 on v4

--- a/solution.py
+++ b/solution.py
@@ -159,15 +159,14 @@
 
 def last_kernel(core, own, sib, s2, near, far, give, keep):
     half, pairs, _ = own.shape
-    half_g, trials = s2.shape
+    trials, half_g = s2.shape
     width = 256
     own_at = core[0] * half_g
 
     def exchange(slab):
         acc = jnp.zeros((half * pairs, trials), F32)
         for g in range(half_g // width):
-            flat = slab(g).reshape(half * pairs, width)
-            acc += jnp.dot(flat, s2[g * width : (g + 1) * width], preferred_element_type=F32)
+            acc += dot_last(slab(g).reshape(half * pairs, width), s2[:, g * width : (g + 1) * width])
         return acc.reshape(half, pairs, trials)
 
     mine = exchange(lambda g: own[:, :, pl.ds(pl.multiple_of(own_at + g * width, width), width)]) - near[:half]
@@ -189,17 +188,18 @@
 
 
 def density_steps(part, me, size):
-    rows = part.shape[0] // 2
+    columns = part.shape[1] // 2
     high = (me // 2) % 2
-    keep = lax.dynamic_slice_in_dim(part, high * rows, rows, 0)
-    part = keep + (yield lax.dynamic_slice_in_dim(part, (1 - high) * rows, rows, 0).astype(BF16), 2).astype(F32)
+    keep = lax.dynamic_slice_in_dim(part, high * columns, columns, 1)
+    give = lax.dynamic_slice_in_dim(part, (1 - high) * columns, columns, 1).astype(BF16)
+    part = keep + (yield give, 2).astype(F32)
     bit = 4
     while bit < size:
         part = part + (yield part.astype(BF16), bit).astype(F32)
         bit *= 2
     part = part.astype(BF16)
     other = yield part, 2
-    return jnp.where(high == 0, jnp.concatenate([part, other], 0), jnp.concatenate([other, part], 0))
+    return jnp.where(high == 0, jnp.concatenate([part, other], 1), jnp.concatenate([other, part], 1))
 
 
 class Density:
@@ -260,7 +260,7 @@
             pack_kernel,
             out_shape=[jax.ShapeDtypeStruct((local_k, pair_count, last), BF16)] * count,
             in_specs=[IN_SMEM, ANYWHERE],
-            out_specs=[ANYWHERE] * count,
+            out_specs=[IN_VMEM] * count,
             scratch_shapes=[pltpu.SemaphoreType.DMA((count,))],
         )(core_id, pair_density)
 
@@ -277,7 +277,7 @@
         piece, value = lax.optimization_barrier((piece, value))
         return value
 
-    contract = lambda v, d: lax.dot_general(d, v, (((0, 1), (0, 1)), ((), ())), preferred_element_type=F32)
+    contract = lambda v, d: lax.dot_general(v, d, (((0, 1), (0, 1)), ((), ())), preferred_element_type=F32)
     part = contract(trial_vectors, own_half) + contract(vec_s, sib)
     density = Density(density_steps(part, me, size), size)
     my_coulomb = lax.dynamic_slice_in_dim(coulomb, core * half_g, half_g, 0)
@@ -323,46 +323,43 @@
     ]
 
     def params():
-        return pltpu.CompilerParams(vmem_limit_bytes=20 << 20)
+        return pltpu.CompilerParams(vmem_limit_bytes=12 << 20)
 
     def cost(count, pairs):
         return pl.CostEstimate(
             flops=4 * count * pairs * width * width * trial_count, transcendentals=0, bytes_accessed=1 << 20
         )
 
-    near_groups = (groups + 1) // 2
     near_rounds, vec_p, far_list, far_rounds = lax.optimization_barrier(
         (near_rounds, vec_p, far_list, far_rounds)
     )
     near_rounds = density.before(near_rounds)
-    if groups > 1:
-        near_rounds = send_group(1, near_rounds)
     near, w_half = pl.pallas_call(
-        functools.partial(near_kernel, 0, near_groups, True),
+        functools.partial(near_kernel, 0, 1, True),
         out_shape=(sums, jax.ShapeDtypeStruct((q_count, half_g, width), BF16)),
         in_specs=[IN_SMEM] * 3 + [IN_VMEM] * 4 + [ANYWHERE],
         out_specs=(IN_VMEM, IN_VMEM),
         scratch_shapes=work + [pltpu.SemaphoreType.DMA((groups,))],
         compiler_params=params(),
-        cost_estimate=cost(near_groups, 160),
+        cost_estimate=cost(1, 160),
     )(core_id, near_list, near_rounds, pair_density, trial_vectors, sib, vec_s, screen)
     near = density.after(near)
-    if groups > 2:
-        near = send_group(2, near)
-    if groups > near_groups:
+    for start, count, going in ((1, 1, (1,)), (2, groups - 2, range(2, groups))):
+        if count < 1 or start >= groups:
+            continue
+        for g in going:
+            near = send_group(g, near)
         near = pl.pallas_call(
-            functools.partial(near_kernel, near_groups, groups - near_groups, False),
+            functools.partial(near_kernel, start, count, False),
             out_shape=sums,
             in_specs=[IN_SMEM] * 3 + [IN_VMEM] * 6,
             out_specs=IN_VMEM,
             scratch_shapes=work,
             input_output_aliases={8: 0},
             compiler_params=params(),
-            cost_estimate=cost(groups - near_groups, 160),
+            cost_estimate=cost(count, 160),
         )(core_id, near_list, near_rounds, pair_density, trial_vectors, sib, vec_s, w_half, near)
         near = density.after(near)
-    for g in range(3, groups):
-        near = send_group(g, near)
     near, far_rounds = lax.optimization_barrier((near, far_rounds))
     far = None
     for c in range(groups):
@@ -382,7 +379,7 @@
         )
         if c % 2 == 1:
             far = density.after(far)
-    screened2 = (2.0 * my_coulomb[:, None] * density.finish().astype(F32)).astype(BF16)
+    screened2 = (2.0 * my_coulomb[None, :] * density.finish().astype(F32)).astype(BF16)
     give, keep = pl.pallas_call(
         last_kernel,
         out_shape=(jax.ShapeDtypeStruct(sums.shape, BF16), sums),

time: 210 us -> 133 us (0.63)
  Pallas kernels: 148 us -> 62.7 us
  starting transfers between devices: 31.2 us -> 34.6 us
  local copies, waits for them, and re-layouts: 3.13 us -> 6.3 us
  other arithmetic: 4.91 us -> 7.98 us
  matrix products: 5.07 us -> 2.58 us
    pallas_call x2, Pallas kernels: 97.5 us -> 5.2 us  [packed(): pl.pallas_call(pack_kernel, out_shape=[jax.ShapeDtypeStruct((local_k, pai...]
    ppermute x3, starting transfers between devices: 2.03 us -> 19.9 us  [send_group(): came.append([lax.ppermute(piece, 'ka', onward)])]
    ppermute x4, starting transfers between devices: 12.2 us -> 0.28 us  [after(): lax.ppermute(self.give, 'ka', [(i, i ^ self.bit) for i in range(self.size)])]
    pallas_call x2 -> x3, Pallas kernels: 27.7 us -> 35.5 us  [the longest x2 24.8 us: on_device(): pl.pallas_call(functools.partial(near_kernel, start, count, False), out_s...]
    unnamed x18, local copies, waits for them, and re-layouts: 0.48 us -> 3.02 us
    dot_general x2, matrix products: 5.07 us -> 2.58 us  [on_device(): lax.dot_general(v, d, (((0, 1), (0, 1)), ((), ())), preferred_element_typ...]
  transfers between devices with their start and end apart: 18 -> 18, of which waited for: 6 -> 8; matrix products, arithmetic and copies ran while one was open for 6% -> 7% of each run, Pallas kernels for 39% -> 43%
where the time goes in v5:
time: 133 us; the launch traced here: 131 us
  Pallas kernels  62.7 us (47%)
  starting transfers between devices  34.6 us (26%)
  waiting for transfers between devices  15.3 us (12%)
  other arithmetic  7.98 us (6%)
  local copies, waits for them, and re-layouts  6.3 us (5%)
  matrix products  2.58 us (2%)
  between operations  1.67 us (1%)
    pallas_call x2, Pallas kernels, on_device(): pl.pallas_call(functools.partial(near_kernel, start, count, False), out_s...  24.8 us
    pallas_call x4, Pallas kernels, on_device(): pl.pallas_call(functools.partial(far_kernel, c, 1, c == 0, len(came[c])),...  20.5 us
    ppermute x3, starting transfers between devices, send_group(): came.append([lax.ppermute(piece, 'ka', onward)])  19.9 us
    pallas_call x1, Pallas kernels, on_device(): pl.pallas_call(functools.partial(near_kernel, 0, 1, True), out_shape=(sum...  10.7 us
    pallas_call x2, Pallas kernels, packed(): pl.pallas_call(pack_kernel, out_shape=[jax.ShapeDtypeStruct((local_k, pai...  5.2 us
    ppermute x4, waiting for transfers between devices, after(): lax.ppermute(self.give, 'ka', [(i, i ^ self.bit) for i in range(self.size)])  5.19 us
    ppermute x3, starting transfers between devices, sent(): lax.ppermute(rows_of(value, (mine + steps) % parts).astype(BF16), ('ka',...  5.12 us
    ppermute x2, waiting for transfers between devices, on_device(): table_p, vec_p = (lax.ppermute(value, 'ka', onward) for value in edge)  4.65 us
  transfers between devices with their start and end apart: 18, of which 8 were waited for; matrix products, arithmetic and copies ran while one was open for 7% of the time, Pallas kernels for 43%

profile of v5, /device:TPU:1, one launch (start us, length us, event | category | flops | bytes accessed | tf_op | source)
XLA Modules:
  0.0 131.1 jit_solution(15659561235123640129)
XLA Ops:
  0.0 0.7 copy.22
  0.7 0.7 fusion.21
  1.5 0.8 pad_add_fusion
  2.3 0.5 collective-permute-start.1
  2.8 3.0 %shard_map.82 = bf16[16,64,1024]{2,1,0:T(8,128)(2,1)} custom-call(s32[1]{0:T(128)} %bitcast.core.refs_0_, bf16[16,64,2048]{2,1,0:T(8,128)(2,1)} %own.9), custom_call_target="tpu_custom_call" | custom-call | tf_op jit(solution)/shard_map/pallas_call | solution.py:259
  6.1 2.1 %fusion.2 = f32[1024,128]{0,1:T(8,128)S(1)} fusion(bf16[16,64,128]{2,1,0:T(8,128)(2,1)S(1)} %copy-done.2, bf16[16,64,2048]{2,1,0:T(8,128)(2,1)} %own.9, s32[]{:T(128)S(6)} %select_n.197), kind=kOutput, calls=%fused_computation.2 | convolution fusion | flops 268435456 | bytes 2883588 | tf_op jit(solution)/shard_map/dot_general | solution.py:280
  8.7 0.2 dynamic-update-slice.4
  9.4 0.2 dynamic-update-slice.5
  9.8 0.3 convert_reduce_fusion
  10.1 2.7 %collective-permute-start.4 = (s32[16,33]{1,0:T(8,128)S(1)}, s32[16,33]{1,0:T(8,128)S(1)}, u32[]{:S(2)}, u32[]{:S(2)}) collective-permute-start(s32[16,33]{1,0:T(8,128)S(1)} %get-tuple-element.106), channel_id=1, source_target_pairs={{0,4},{2,6},{4,8},{6,10},{8,12},{10,14},{12,16},{14,18},{16,20},{1... | collective-permute-start | bytes 6344 | tf_op jit(solution)/shard_map/ppermute | solution.py:256
  12.8 0.2 slice_reduce_fusion.1
  13.5 0.2 dynamic-update-slice.2
  13.7 3.2 %collective-permute-done.4 = s32[16,33]{1,0:T(8,128)S(1)} collective-permute-done((s32[16,33]{1,0:T(8,128)S(1)}, s32[16,33]{1,0:T(8,128)S(1)}, u32[]{:S(2)}, u32[]{:S(2)}) %collective-permute-start.4) | collective-permute-done | bytes 2144 | tf_op jit(solution)/shard_map/ppermute | solution.py:256
  17.4 0.2 dynamic-update-slice.3
  17.7 0.7 fusion.44
  18.6 0.3 convert_reduce_fusion.1
  19.0 0.2 select_reduce_fusion.1
  19.2 0.7 broadcast_select_fusion
  19.9 0.2 select_reduce_fusion
  21.3 2.2 %shard_map.86 = (bf16[16,64,256]{2,1,0:T(8,128)(2,1)}, bf16[16,64,256]{2,1,0:T(8,128)(2,1)}) custom-call(s32[1]{0:T(128)} %bitcast.core.refs_0_, bf16[16,64,2048]{2,1,0:T(8,128)(2,1)} %own.9), custom_call_target="tpu_custom_call" | custom-call | tf_op jit(solution)/shard_map/pallas_call | solution.py:259
  23.6 2.5 %collective-permute-start.10 = (bf16[16,64,256]{2,1,0:T(8,128)(2,1)}, bf16[16,64,256]{2,1,0:T(8,128)(2,1)S(1)}, u32[]{:S(2)}, u32[]{:S(2)}) collective-permute-start(bf16[16,64,256]{2,1,0:T(8,128)(2,1)} %get-tuple-element.73), channel_id=1, source_target_pairs={{2,6},{6,10},{10,14},{14,18},{18,22},{22,26},{26,30},{30,2},{3,7},... | collective-permute-start | bytes 1572872 | tf_op jit(solution)/shard_map/ppermute | solution.py:271
  26.1 2.1 %collective-permute-start.9 = (bf16[16,64,256]{2,1,0:T(8,128)(2,1)}, bf16[16,64,256]{2,1,0:T(8,128)(2,1)S(1)}, u32[]{:S(2)}, u32[]{:S(2)}) collective-permute-start(bf16[16,64,256]{2,1,0:T(8,128)(2,1)} %get-tuple-element.72), channel_id=1, source_target_pairs={{2,4},{6,8},{10,12},{14,16},{18,20},{22,24},{26,28},{30,0},{3,5},{... | collective-permute-start | bytes 1572872 | tf_op jit(solution)/shard_map/ppermute | solution.py:271
  28.2 1.5 %collective-permute-done.3.vec_p = bf16[16,64,128]{2,1,0:T(8,128)(2,1)S(1)} collective-permute-done((bf16[16,64,128]{2,1,0:T(8,128)(2,1)}, bf16[16,64,128]{2,1,0:T(8,128)(2,1)S(1)}, u32[]{:S(2)}, u32[]{:S(2)}) %collective-permute-start.3) | collective-permute-done | bytes 262176 | tf_op jit(solution)/shard_map/ppermute | solution.py:256
  29.7 0.5 fusion.5
  30.3 1.6 %copy-done.1 = bf16[16,64,2048]{2,1,0:T(8,128)(2,1)S(1)} copy-done((bf16[16,64,2048]{2,1,0:T(8,128)(2,1)S(1)}, bf16[16,64,2048]{2,1,0:T(8,128)(2,1)}, u32[]{:S(2)}) %copy-start.1) | copy-done | bytes 4194328
  31.9 10.7 %shard_map.83 = (f32[32,64,128]{2,1,0:T(8,128)S(1)}, bf16[32,1024,256]{2,1,0:T(8,128)(2,1)S(1)}) custom-call(s32[1]{0:T(128)} %bitcast.core.refs_0_, s32[544]{0:T(1024)S(1)} %broadcast_add_fusion.refs_1_, s32[1]{0:T(128)} %bitcast.6.refs_2_, bf16[16,64,2048]{2,1,0:T(8,128)(2,1)S(1)} %copy-done.1, bf16[16,64,128]{2,1,0:T(8,128)(2,1)S(1)} %copy-done.2, ...), custom_call_target="tpu_custom_call" | custom-call | flops 5368709120 | bytes 1048576 | tf_op jit(solution)/shard_map/pallas_call | solution.py:337
  42.6 0.6 dynamic-slice_select_fusion
  43.1 1.9 %collective-permute-done.5 = bf16[128,512]{1,0:T(8,128)(2,1)S(1)} collective-permute-done((bf16[128,512]{1,0:T(8,128)(2,1)S(1)}, bf16[128,512]{1,0:T(8,128)(2,1)S(1)}, u32[]{:S(2)}, u32[]{:S(2)}) %collective-permute-start.5) | collective-permute-done | bytes 131104 | tf_op jit(solution)/shard_map/ppermute | solution.py:218
  45.3 8.5 %shard_map.84.refs_8_ = f32[32,64,128]{2,1,0:T(8,128)S(1)} custom-call(s32[1]{0:T(128)} %bitcast.core.refs_0_, s32[544]{0:T(1024)S(1)} %broadcast_add_fusion.refs_1_, s32[1]{0:T(128)} %bitcast.6.refs_2_, bf16[16,64,2048]{2,1,0:T(8,128)(2,1)S(1)} %copy-done.1, bf16[16,64,128]{2,1,0:T(8,128)(2,1)S(1)} %copy-done.2, ...), custom_call_target="tpu_custom_call", output_to_operand_aliasing={{}: (8, {})} | custom-call | flops 5368709120 | bytes 1048576 | tf_op jit(solution)/shard_map/pallas_call | solution.py:352
  53.9 0.9 collective-permute-start.12
  54.8 16.4 %shard_map.85.near = f32[32,64,128]{2,1,0:T(8,128)S(1)} custom-call(s32[1]{0:T(128)} %bitcast.core.refs_0_, s32[544]{0:T(1024)S(1)} %broadcast_add_fusion.refs_1_, s32[1]{0:T(128)} %bitcast.6.refs_2_, bf16[16,64,2048]{2,1,0:T(8,128)(2,1)S(1)} %copy-done.1, bf16[16,64,128]{2,1,0:T(8,128)(2,1)S(1)} %copy-done.2, ...), custom_call_target="tpu_custom_call", output_to_operand_aliasing={{}: (8, {})} | custom-call | flops 10737418240 | bytes 1048576 | tf_op jit(solution)/shard_map/pallas_call | solution.py:352
  71.2 19.0 %collective-permute-start.13 = (bf16[16,64,256]{2,1,0:T(8,128)(2,1)S(1)}, bf16[16,64,256]{2,1,0:T(8,128)(2,1)S(1)}, u32[]{:S(2)}, u32[]{:S(2)}) collective-permute-start(bf16[16,64,256]{2,1,0:T(8,128)(2,1)S(1)} %get-tuple-element.80), channel_id=1, source_target_pairs={{0,4},{2,6},{4,8},{6,10},{8,12},{10,14},{12,16},{14,18},{16,20},{1... | collective-permute-start | bytes 1572872 | tf_op jit(solution)/shard_map/ppermute | solution.py:276
  90.3 5.1 %shard_map.87.refs_0_ = f32[32,64,128]{2,1,0:T(8,128)S(1)} custom-call(s32[1]{0:T(128)} %bitcast.core.refs_0_, s32[544]{0:T(1024)S(1)} %broadcast_add_fusion.1.listed, s32[1]{0:T(128)} %bitcast.7.rounds, bf16[16,64,2048]{2,1,0:T(8,128)(2,1)S(1)} %copy-done.1, bf16[16,64,128]{2,1,0:T(8,128)(2,1)S(1)} %copy-done.2, ...), custom_call_target="tpu_custom_call" | custom-call | flops 2684354560 | bytes 1048576 | tf_op jit(solution)/shard_map/pallas_call | solution.py:366
  95.4 5.1 %shard_map.88.refs_0_ = f32[32,64,128]{2,1,0:T(8,128)S(1)} custom-call(s32[1]{0:T(128)} %bitcast.core.refs_0_, s32[544]{0:T(1024)S(1)} %broadcast_add_fusion.1.listed, s32[1]{0:T(128)} %bitcast.7.rounds, bf16[16,64,2048]{2,1,0:T(8,128)(2,1)S(1)} %copy-done.1, bf16[16,64,128]{2,1,0:T(8,128)(2,1)S(1)} %copy-done.2, ...), custom_call_target="tpu_custom_call", output_to_operand_aliasing={{}: (9, {})} | custom-call | flops 2684354560 | bytes 1048576 | tf_op jit(solution)/shard_map/pallas_call | solution.py:366
  100.5 3.2 %collective-permute-done.8 = bf16[128,512]{1,0:T(8,128)(2,1)S(1)} collective-permute-done((bf16[128,512]{1,0:T(8,128)(2,1)S(1)}, bf16[128,512]{1,0:T(8,128)(2,1)S(1)}, u32[]{:S(2)}, u32[]{:S(2)}) %collective-permute-start.8) | collective-permute-done | bytes 131104 | tf_op jit(solution)/shard_map/ppermute | solution.py:218
  103.9 5.1 %shard_map.89.refs_0_ = f32[32,64,128]{2,1,0:T(8,128)S(1)} custom-call(s32[1]{0:T(128)} %bitcast.core.refs_0_, s32[544]{0:T(1024)S(1)} %broadcast_add_fusion.1.listed, s32[1]{0:T(128)} %bitcast.7.rounds, bf16[16,64,2048]{2,1,0:T(8,128)(2,1)S(1)} %copy-done.1, bf16[16,64,128]{2,1,0:T(8,128)(2,1)S(1)} %copy-done.2, ...), custom_call_target="tpu_custom_call", output_to_operand_aliasing={{}: (9, {})} | custom-call | flops 2684354560 | bytes 1048576 | tf_op jit(solution)/shard_map/pallas_call | solution.py:366
  109.0 5.3 %shard_map.90.far = f32[32,64,128]{2,1,0:T(8,128)S(1)} custom-call(s32[1]{0:T(128)} %bitcast.core.refs_0_, s32[544]{0:T(1024)S(1)} %broadcast_add_fusion.1.listed, s32[1]{0:T(128)} %bitcast.7.rounds, bf16[16,64,2048]{2,1,0:T(8,128)(2,1)S(1)} %copy-done.1, bf16[16,64,128]{2,1,0:T(8,128)(2,1)S(1)} %copy-done.2, ...), custom_call_target="tpu_custom_call", output_to_operand_aliasing={{}: (9, {})} | custom-call | flops 2684354560 | bytes 1048576 | tf_op jit(solution)/shard_map/pallas_call | solution.py:366
  114.3 1.4 %shard_map.91 = (bf16[32,64,128]{2,1,0:T(8,128)(2,1)S(1)}, f32[32,64,128]{2,1,0:T(8,128)S(1)}) custom-call(s32[1]{0:T(128)} %bitcast.core.refs_0_, bf16[16,64,2048]{2,1,0:T(8,128)(2,1)S(1)} %copy-done.1, bf16[16,64,1024]{2,1,0:T(8,128)(2,1)S(1)} %collective-permute-done.refs_5_.sib, bf16[128,1024]{1,0:T(8,128)(2,1)S(1)} %multiply_convert_fusion.s2, ...), custom_call_target="tpu_custom_call" | custom-call | flops 536870912 | bytes 1048576 | tf_op jit(solution)/shard_map/pallas_call | solution.py:383
  115.8 1.0 copy-done.3
  116.7 1.3 %collective-permute-start.14 = (bf16[32,64,128]{2,1,0:T(8,128)(2,1)S(1)}, bf16[32,64,128]{2,1,0:T(8,128)(2,1)S(1)}, u32[]{:S(2)}, u32[]{:S(2)}) collective-permute-start(bf16[32,64,128]{2,1,0:T(8,128)(2,1)S(1)} %get-tuple-element.85), channel_id=1, source_target_pairs={{0,2},{2,0},{4,6},{6,4},{8,10},{10,8},{12,14},{14,12},{16,18},{18,... | collective-permute-start | bytes 1572872 | tf_op jit(solution)/shard_map/ppermute | solution.py:392
  118.1 1.5 %collective-permute-done.14 = bf16[32,64,128]{2,1,0:T(8,128)(2,1)S(1)} collective-permute-done((bf16[32,64,128]{2,1,0:T(8,128)(2,1)S(1)}, bf16[32,64,128]{2,1,0:T(8,128)(2,1)S(1)}, u32[]{:S(2)}, u32[]{:S(2)}) %collective-permute-start.14) | collective-permute-done | bytes 524320 | tf_op jit(solution)/shard_map/ppermute | solution.py:392
  119.6 1.4 %convert_add_fusion = f32[32,64,128]{2,1,0:T(8,128)S(1)} fusion(f32[32,64,128]{2,1,0:T(8,128)} %copy-done.3, bf16[32,64,128]{2,1,0:T(8,128)(2,1)S(1)} %collective-permute-done.14), kind=kLoop, calls=%fused_computation.9 | loop fusion | flops 524288 | bytes 2621440 | tf_op jit(solution)/shard_map/add | solution.py:392
  121.1 1.9 %collective-permute-start.15 = (bf16[16,32,128]{2,1,0:T(8,128)(2,1)S(1)}, bf16[16,32,128]{2,1,0:T(8,128)(2,1)S(1)}, u32[]{:S(2)}, u32[]{:S(2)}) collective-permute-start(bf16[16,32,128]{2,1,0:T(8,128)(2,1)S(1)} %get-tuple-element.103), channel_id=1, source_target_pairs={{2,30},{3,31},{6,2},{7,3},{10,6},{11,7},{14,10},{15,11},{18,14},{1... | collective-permute-start | bytes 393224 | tf_op jit(solution)/shard_map/ppermute | solution.py:403
  123.2 3.1 %collective-permute-start.17 = (bf16[16,32,128]{2,1,0:T(8,128)(2,1)S(1)}, bf16[16,32,128]{2,1,0:T(8,128)(2,1)S(1)}, u32[]{:S(2)}, u32[]{:S(2)}) collective-permute-start(bf16[16,32,128]{2,1,0:T(8,128)(2,1)S(1)} %dynamic-slice_convert_fusion), channel_id=1, source_target_pairs={{2,3},{3,2},{6,7},{7,6},{10,11},{11,10},{14,15},{15,14},{18,19},{1... | collective-permute-start | bytes 393224 | tf_op jit(solution)/shard_map/ppermute | solution.py:403
  126.4 1.2 collective-permute-done.15
  127.6 2.5 %collective-permute-done.16 = bf16[16,32,128]{2,1,0:T(8,128)(2,1)S(1)} collective-permute-done((bf16[16,32,128]{2,1,0:T(8,128)(2,1)S(1)}, bf16[16,32,128]{2,1,0:T(8,128)(2,1)S(1)}, u32[]{:S(2)}, u32[]{:S(2)}) %collective-permute-start.16) | collective-permute-done | bytes 131104 | tf_op jit(solution)/shard_map/ppermute | solution.py:403
  130.1 0.2 collective-permute-done.17
  130.3 0.8 add_convert_fusion
  (86 shorter events, 4.0 us)
Async XLA Ops:
  0.0 126.3 %copy-start = (f32[16,64]{1,0:T(8,128)S(1)}, f32[16,64]{1,0:T(8,128)}, u32[]{:S(2)}) copy-start(f32[16,64]{1,0:T(8,128)} %param.10) | copy-start | bytes 12292
  2.3 6.7 %collective-permute-start.2 = (s32[16,33]{1,0:T(8,128)S(1)}, s32[16,33]{1,0:T(8,128)S(1)}, u32[]{:S(2)}, u32[]{:S(2)}) collective-permute-start(s32[16,33]{1,0:T(8,128)S(1)} %pad_add_fusion), channel_id=1, source_target_pairs={{0,2},{2,0},{4,6},{6,4},{8,10},{10,8},{12,14},{14,12},{16,18},{18,... | collective-permute-start | bytes 6344 | tf_op jit(solution)/shard_map/ppermute | solution.py:253
  2.3 16.9 %collective-permute-start.1 = (bf16[16,64,128]{2,1,0:T(8,128)(2,1)}, bf16[16,64,128]{2,1,0:T(8,128)(2,1)S(1)}, u32[]{:S(2)}, u32[]{:S(2)}) collective-permute-start(bf16[16,64,128]{2,1,0:T(8,128)(2,1)} %vec.7), channel_id=1, source_target_pairs={{0,2},{2,0},{4,6},{6,4},{8,10},{10,8},{12,14},{14,12},{16,18},{18,... | collective-permute-start | bytes 786440 | tf_op jit(solution)/shard_map/ppermute | solution.py:254
  2.8 3.1 %copy-start.5 = (s32[16]{0:T(128)S(1)}, s32[16]{0:T(128)}, u32[]{:S(2)}) copy-start(s32[16]{0:T(128)} %param.14) | copy-start | bytes 196
  2.8 3.2 %copy-start.4 = (s32[16,16]{1,0:T(8,128)S(1)}, s32[16,16]{1,0:T(8,128)}, u32[]{:S(2)}) copy-start(s32[16,16]{1,0:T(8,128)} %param.15) | copy-start | bytes 3076
  2.8 3.3 %copy-start.2 = (bf16[16,64,128]{2,1,0:T(8,128)(2,1)S(1)}, bf16[16,64,128]{2,1,0:T(8,128)(2,1)}, u32[]{:S(2)}) copy-start(bf16[16,64,128]{2,1,0:T(8,128)(2,1)} %vec.7) | copy-start | bytes 786436
  5.8 23.9 %collective-permute-start = (bf16[16,64,1024]{2,1,0:T(8,128)(2,1)}, bf16[16,64,1024]{2,1,0:T(8,128)(2,1)S(1)}, u32[]{:S(2)}, u32[]{:S(2)}) collective-permute-start(bf16[16,64,1024]{2,1,0:T(8,128)(2,1)} %shard_map.82), channel_id=1, source_target_pairs={{0,2},{2,0},{4,6},{6,4},{8,10},{10,8},{12,14},{14,12},{16,18},{18,... | collective-permute-start | bytes 6291464 | tf_op jit(solution)/shard_map/ppermute | solution.py:269
  6.1 2.1 %copy-start.6 = (f32[2048]{0:T(1024)S(1)}, f32[2048]{0:T(1024)}, u32[]{:S(2)}) copy-start(f32[2048]{0:T(1024)} %param.11) | copy-start | bytes 24580
  10.1 6.7 %collective-permute-start.4 = (s32[16,33]{1,0:T(8,128)S(1)}, s32[16,33]{1,0:T(8,128)S(1)}, u32[]{:S(2)}, u32[]{:S(2)}) collective-permute-start(s32[16,33]{1,0:T(8,128)S(1)} %get-tuple-element.106), channel_id=1, source_target_pairs={{0,4},{2,6},{4,8},{6,10},{8,12},{10,14},{12,16},{14,18},{16,20},{1... | collective-permute-start | bytes 6344 | tf_op jit(solution)/shard_map/ppermute | solution.py:256
  19.9 9.8 %collective-permute-start.3 = (bf16[16,64,128]{2,1,0:T(8,128)(2,1)}, bf16[16,64,128]{2,1,0:T(8,128)(2,1)S(1)}, u32[]{:S(2)}, u32[]{:S(2)}) collective-permute-start(bf16[16,64,128]{2,1,0:T(8,128)(2,1)} %broadcast_select_fusion), channel_id=1, source_target_pairs={{0,4},{2,6},{4,8},{6,10},{8,12},{10,14},{12,16},{14,18},{16,20},{1... | collective-permute-start | bytes 786440 | tf_op jit(solution)/shard_map/ppermute | solution.py:256
  23.6 66.7 %collective-permute-start.10 = (bf16[16,64,256]{2,1,0:T(8,128)(2,1)}, bf16[16,64,256]{2,1,0:T(8,128)(2,1)S(1)}, u32[]{:S(2)}, u32[]{:S(2)}) collective-permute-start(bf16[16,64,256]{2,1,0:T(8,128)(2,1)} %get-tuple-element.73), channel_id=1, source_target_pairs={{2,6},{6,10},{10,14},{14,18},{18,22},{22,26},{26,30},{30,2},{3,7},... | collective-permute-start | bytes 1572872 | tf_op jit(solution)/shard_map/ppermute | solution.py:271
  26.1 64.3 %collective-permute-start.9 = (bf16[16,64,256]{2,1,0:T(8,128)(2,1)}, bf16[16,64,256]{2,1,0:T(8,128)(2,1)S(1)}, u32[]{:S(2)}, u32[]{:S(2)}) collective-permute-start(bf16[16,64,256]{2,1,0:T(8,128)(2,1)} %get-tuple-element.72), channel_id=1, source_target_pairs={{2,4},{6,8},{10,12},{14,16},{18,20},{22,24},{26,28},{30,0},{3,5},{... | collective-permute-start | bytes 1572872 | tf_op jit(solution)/shard_map/ppermute | solution.py:271
  29.7 2.2 %copy-start.1 = (bf16[16,64,2048]{2,1,0:T(8,128)(2,1)S(1)}, bf16[16,64,2048]{2,1,0:T(8,128)(2,1)}, u32[]{:S(2)}) copy-start(bf16[16,64,2048]{2,1,0:T(8,128)(2,1)} %own.9) | copy-start | bytes 12582916
  30.2 14.9 %collective-permute-start.5 = (bf16[128,512]{1,0:T(8,128)(2,1)S(1)}, bf16[128,512]{1,0:T(8,128)(2,1)S(1)}, u32[]{:S(2)}, u32[]{:S(2)}) collective-permute-start(bf16[128,512]{1,0:T(8,128)(2,1)S(1)} %fusion.9), channel_id=1, source_target_pairs={{0,4},{2,6},{4,0},{6,2},{8,12},{10,14},{12,8},{14,10},{16,20},{18,... | collective-permute-start | bytes 393224 | tf_op jit(solution)/shard_map/ppermute | solution.py:218
  45.1 8.7 %collective-permute-start.6 = (bf16[128,512]{1,0:T(8,128)(2,1)S(1)}, bf16[128,512]{1,0:T(8,128)(2,1)S(1)}, u32[]{:S(2)}, u32[]{:S(2)}) collective-permute-start(bf16[128,512]{1,0:T(8,128)(2,1)S(1)} %fusion.10), channel_id=1, source_target_pairs={{0,8},{2,10},{4,12},{6,14},{8,0},{10,2},{12,4},{14,6},{16,24},{18,... | collective-permute-start | bytes 393224 | tf_op jit(solution)/shard_map/ppermute | solution.py:218
  45.2 50.2 %collective-permute-start.11 = (bf16[16,64,256]{2,1,0:T(8,128)(2,1)S(1)}, bf16[16,64,256]{2,1,0:T(8,128)(2,1)S(1)}, u32[]{:S(2)}, u32[]{:S(2)}) collective-permute-start(bf16[16,64,256]{2,1,0:T(8,128)(2,1)S(1)} %get-tuple-element.74), channel_id=1, source_target_pairs={{0,4},{2,6},{4,8},{6,10},{8,12},{10,14},{12,16},{14,18},{16,20},{1... | collective-permute-start | bytes 1572872 | tf_op jit(solution)/shard_map/ppermute | solution.py:276
  53.8 17.3 %collective-permute-start.7 = (bf16[128,512]{1,0:T(8,128)(2,1)S(1)}, bf16[128,512]{1,0:T(8,128)(2,1)S(1)}, u32[]{:S(2)}, u32[]{:S(2)}) collective-permute-start(bf16[128,512]{1,0:T(8,128)(2,1)S(1)} %fusion.8), channel_id=1, source_target_pairs={{0,16},{2,18},{4,20},{6,22},{8,24},{10,26},{12,28},{14,30},{16,0},... | collective-permute-start | bytes 393224 | tf_op jit(solution)/shard_map/ppermute | solution.py:218
  53.9 50.0 %collective-permute-start.12 = (bf16[16,64,256]{2,1,0:T(8,128)(2,1)S(1)}, bf16[16,64,256]{2,1,0:T(8,128)(2,1)S(1)}, u32[]{:S(2)}, u32[]{:S(2)}) collective-permute-start(bf16[16,64,256]{2,1,0:T(8,128)(2,1)S(1)} %get-tuple-element.79), channel_id=1, source_target_pairs={{0,4},{2,6},{4,8},{6,10},{8,12},{10,14},{12,16},{14,18},{16,20},{1... | collective-permute-start | bytes 1572872 | tf_op jit(solution)/shard_map/ppermute | solution.py:276
  71.2 37.8 %collective-permute-start.13 = (bf16[16,64,256]{2,1,0:T(8,128)(2,1)S(1)}, bf16[16,64,256]{2,1,0:T(8,128)(2,1)S(1)}, u32[]{:S(2)}, u32[]{:S(2)}) collective-permute-start(bf16[16,64,256]{2,1,0:T(8,128)(2,1)S(1)} %get-tuple-element.80), channel_id=1, source_target_pairs={{0,4},{2,6},{4,8},{6,10},{8,12},{10,14},{12,16},{14,18},{16,20},{1... | collective-permute-start | bytes 1572872 | tf_op jit(solution)/shard_map/ppermute | solution.py:276
  90.3 13.5 %collective-permute-start.8 = (bf16[128,512]{1,0:T(8,128)(2,1)S(1)}, bf16[128,512]{1,0:T(8,128)(2,1)S(1)}, u32[]{:S(2)}, u32[]{:S(2)}) collective-permute-start(bf16[128,512]{1,0:T(8,128)(2,1)S(1)} %add_convert_fusion.1), channel_id=1, source_target_pairs={{0,4},{2,6},{4,0},{6,2},{8,12},{10,14},{12,8},{14,10},{16,20},{18,... | collective-permute-start | bytes 393224 | tf_op jit(solution)/shard_map/ppermute | solution.py:218
  115.7 1.0 copy-start.3
  116.7 2.9 %collective-permute-start.14 = (bf16[32,64,128]{2,1,0:T(8,128)(2,1)S(1)}, bf16[32,64,128]{2,1,0:T(8,128)(2,1)S(1)}, u32[]{:S(2)}, u32[]{:S(2)}) collective-permute-start(bf16[32,64,128]{2,1,0:T(8,128)(2,1)S(1)} %get-tuple-element.85), channel_id=1, source_target_pairs={{0,2},{2,0},{4,6},{6,4},{8,10},{10,8},{12,14},{14,12},{16,18},{18,... | collective-permute-start | bytes 1572872 | tf_op jit(solution)/shard_map/ppermute | solution.py:392
  121.1 6.5 %collective-permute-start.15 = (bf16[16,32,128]{2,1,0:T(8,128)(2,1)S(1)}, bf16[16,32,128]{2,1,0:T(8,128)(2,1)S(1)}, u32[]{:S(2)}, u32[]{:S(2)}) collective-permute-start(bf16[16,32,128]{2,1,0:T(8,128)(2,1)S(1)} %get-tuple-element.103), channel_id=1, source_target_pairs={{2,30},{3,31},{6,2},{7,3},{10,6},{11,7},{14,10},{15,11},{18,14},{1... | collective-permute-start | bytes 393224 | tf_op jit(solution)/shard_map/ppermute | solution.py:403
  123.1 7.0 %collective-permute-start.16 = (bf16[16,32,128]{2,1,0:T(8,128)(2,1)S(1)}, bf16[16,32,128]{2,1,0:T(8,128)(2,1)S(1)}, u32[]{:S(2)}, u32[]{:S(2)}) collective-permute-start(bf16[16,32,128]{2,1,0:T(8,128)(2,1)S(1)} %get-tuple-element.104), channel_id=1, source_target_pairs={{0,1},{1,0},{4,5},{5,4},{8,9},{9,8},{12,13},{13,12},{16,17},{17,16... | collective-permute-start | bytes 393224 | tf_op jit(solution)/shard_map/ppermute | solution.py:403
  123.2 7.1 %collective-permute-start.17 = (bf16[16,32,128]{2,1,0:T(8,128)(2,1)S(1)}, bf16[16,32,128]{2,1,0:T(8,128)(2,1)S(1)}, u32[]{:S(2)}, u32[]{:S(2)}) collective-permute-start(bf16[16,32,128]{2,1,0:T(8,128)(2,1)S(1)} %dynamic-slice_convert_fusion), channel_id=1, source_target_pairs={{2,3},{3,2},{6,7},{7,6},{10,11},{11,10},{14,15},{15,14},{18,19},{1... | collective-permute-start | bytes 393224 | tf_op jit(solution)/shard_map/ppermute | solution.py:403

commit v6 on v5

--- a/solution.py
+++ b/solution.py
@@ -265,7 +265,7 @@
         )(core_id, pair_density)
 
     (give_half,) = packed(core_id, half_g, 1)
-    first_pieces = packed(lax.optimization_barrier((core_id, *edge))[0], width, 2)
+    first_pieces = packed(lax.optimization_barrier((core_id, edge[0]))[0], width, 2)
     sib = lax.ppermute(give_half, "ka", sibling)
     own_half = lax.dynamic_slice_in_dim(pair_density, core * half_g, half_g, 2)
     came = [[lax.ppermute(piece, "ka", pairs) for piece, pairs in zip(first_pieces, to_next)]]
@@ -313,8 +313,6 @@
         own_cross | (own_t[0] == 1),
         sib_cross | (sib_t[0] == 1),
     )
-    a_t, p_t = columns(pick(table, table_s)), columns(table_p)
-    far_list, far_rounds = listing(a_t, p_t, a_t[1] + local_k, p_t[1], a_t[0] == 0, p_t[0] == 2)
 
     sums = jax.ShapeDtypeStruct((2 * local_k, pair_count, trial_count), F32)
     work = [
@@ -330,9 +328,9 @@
             flops=4 * count * pairs * width * width * trial_count, transcendentals=0, bytes_accessed=1 << 20
         )
 
-    near_rounds, vec_p, far_list, far_rounds = lax.optimization_barrier(
-        (near_rounds, vec_p, far_list, far_rounds)
-    )
+    a_t, p_t = columns(pick(table, table_s)), columns(table_p)
+    far_list, far_rounds = listing(a_t, p_t, a_t[1] + local_k, p_t[1], a_t[0] == 0, p_t[0] == 2)
+    near_rounds, far_list, far_rounds = lax.optimization_barrier((near_rounds, far_list, far_rounds))
     near_rounds = density.before(near_rounds)
     near, w_half = pl.pallas_call(
         functools.partial(near_kernel, 0, 1, True),
@@ -344,9 +342,12 @@
         cost_estimate=cost(1, 160),
     )(core_id, near_list, near_rounds, pair_density, trial_vectors, sib, vec_s, screen)
     near = density.after(near)
+    near, vec_p = lax.optimization_barrier((near, vec_p))
     for start, count, going in ((1, 1, (1,)), (2, groups - 2, range(2, groups))):
         if count < 1 or start >= groups:
             continue
+        if start == 2:
+            near, *came[0] = lax.optimization_barrier((near, *came[0]))
         for g in going:
             near = send_group(g, near)
         near = pl.pallas_call(
@@ -359,7 +360,8 @@
             compiler_params=params(),
             cost_estimate=cost(count, 160),
         )(core_id, near_list, near_rounds, pair_density, trial_vectors, sib, vec_s, w_half, near)
-        near = density.after(near)
+        if start == 1:
+            near = density.after(near)
     near, far_rounds = lax.optimization_barrier((near, far_rounds))
     far = None
     for c in range(groups):
@@ -372,12 +374,12 @@
             + [VMEM((local_k, pair_count, width), BF16), pltpu.SemaphoreType.DMA],
             input_output_aliases={9: 0} if c else {},
             compiler_params=params(),
-            cost_estimate=cost(1, 80),
+            cost_estimate=cost(1, 8),
         )(
             core_id, far_list, far_rounds, pair_density, trial_vectors, sib, vec_s, w_half, vec_p,
             *([far] if c else []), *came[c],
         )
-        if c % 2 == 1:
+        if c in (1, groups - 1):
             far = density.after(far)
     screened2 = (2.0 * my_coulomb[None, :] * density.finish().astype(F32)).astype(BF16)
     give, keep = pl.pallas_call(

time: 133 us -> 116 us (0.87); the launches traced: 131 us -> 115 us
  starting transfers between devices: 34.6 us -> 25.5 us
  waiting for transfers between devices: 15.3 us -> 6.4 us
  Pallas kernels: 62.7 us -> 67.5 us
  local copies, waits for them, and re-layouts: 6.3 us -> 4.1 us
  other arithmetic: 7.98 us -> 5.91 us
  matrix products: 2.58 us -> 4.42 us
    ppermute x3, starting transfers between devices: 19.9 us -> 1.86 us  [send_group(): came.append([lax.ppermute(piece, 'ka', onward)])]
    ppermute x4, starting transfers between devices: 0.28 us -> 6.57 us  [after(): lax.ppermute(self.give, 'ka', [(i, i ^ self.bit) for i in range(self.size)])]
    pallas_call x4, Pallas kernels: 20.5 us -> 25.2 us  [on_device(): pl.pallas_call(functools.partial(far_kernel, c, 1, c == 0, len(came[c])),...]
    ppermute x2, waiting for transfers between devices: 4.65 us -> 0.01 us  [on_device(): table_p, vec_p = (lax.ppermute(value, 'ka', onward) for value in edge)]
    ppermute x4, waiting for transfers between devices: 5.19 us -> 1.14 us  [after(): lax.ppermute(self.give, 'ka', [(i, i ^ self.bit) for i in range(self.size)])]
    ppermute x2, starting transfers between devices: 4.61 us -> 6.56 us  [on_device(): lax.ppermute(piece, 'ka', pairs)]
    dot_general x2, matrix products: 2.58 us -> 4.42 us  [on_device(): lax.dot_general(v, d, (((0, 1), (0, 1)), ((), ())), preferred_element_typ...]
    unnamed x18 -> x20, local copies, waits for them, and re-layouts: 3.02 us -> 1.45 us
  transfers between devices with their start and end apart: 18 -> 18, of which waited for: 8 -> 4; matrix products, arithmetic and copies ran while one was open for 7% -> 9% of each run, Pallas kernels for 43% -> 55%
where the time goes in v6:
time: 116 us; the launch traced here: 115 us
  Pallas kernels  67.5 us (58%)
  starting transfers between devices  25.5 us (22%)
  waiting for transfers between devices  6.4 us (6%)
  other arithmetic  5.91 us (5%)
  matrix products  4.42 us (4%)
  local copies, waits for them, and re-layouts  4.1 us (4%)
  between operations  1.61 us (1%)
    pallas_call x4, Pallas kernels, on_device(): pl.pallas_call(functools.partial(far_kernel, c, 1, c == 0, len(came[c])),...  25.2 us
    pallas_call x2, Pallas kernels, on_device(): pl.pallas_call(functools.partial(near_kernel, start, count, False), out_s...  24.9 us
    pallas_call x1, Pallas kernels, on_device(): pl.pallas_call(functools.partial(near_kernel, 0, 1, True), out_shape=(sum...  10.7 us
    ppermute x4, starting transfers between devices, after(): lax.ppermute(self.give, 'ka', [(i, i ^ self.bit) for i in range(self.size)])  6.57 us
    ppermute x2, starting transfers between devices, on_device(): lax.ppermute(piece, 'ka', pairs)  6.56 us
    pallas_call x2, Pallas kernels, packed(): pl.pallas_call(pack_kernel, out_shape=[jax.ShapeDtypeStruct((local_k, pai...  5.19 us
    ppermute x3, starting transfers between devices, sent(): lax.ppermute(rows_of(value, (mine + steps) % parts).astype(BF16), ('ka',...  5.12 us
    dot_general x2, matrix products, on_device(): lax.dot_general(v, d, (((0, 1), (0, 1)), ((), ())), preferred_element_typ...  4.42 us
  transfers between devices with their start and end apart: 18, of which 4 were waited for; matrix products, arithmetic and copies ran while one was open for 9% of the time, Pallas kernels for 55%

profile of v6, /device:TPU:1, one launch (start us, length us, event | category | flops | bytes accessed | tf_op | source)
XLA Modules:
  0.0 115.4 jit_solution(7548690073768127565)
XLA Ops:
  0.0 3.0 %shard_map.82 = bf16[16,64,1024]{2,1,0:T(8,128)(2,1)} custom-call(s32[1]{0:T(128)} %bitcast.core.refs_0_, bf16[16,64,2048]{2,1,0:T(8,128)(2,1)} %own.9), custom_call_target="tpu_custom_call" | custom-call | tf_op jit(solution)/shard_map/pallas_call | solution.py:259
  3.0 0.1 collective-permute-start
  3.1 0.5 collective-permute-start.1
  3.8 0.1 collective-permute-start.2
  4.1 2.9 %fusion.2 = f32[1024,128]{0,1:T(8,128)} fusion(bf16[16,64,128]{2,1,0:T(8,128)(2,1)S(1)} %copy-done.2, bf16[16,64,2048]{2,1,0:T(8,128)(2,1)} %own.9, s32[]{:T(128)S(6)} %select_n.197), kind=kOutput, calls=%fused_computation.2 | convolution fusion | flops 268435456 | bytes 2883588 | tf_op jit(solution)/shard_map/dot_general | solution.py:280
  7.4 0.2 dynamic-update-slice.4
  7.8 0.2 slice_reduce_fusion.2
  8.1 0.2 dynamic-update-slice.5
  8.4 0.1 convert_reduce_fusion.3
  8.5 0.3 convert_reduce_fusion
  8.8 2.7 %collective-permute-start.3 = (s32[16,33]{1,0:T(8,128)S(1)}, s32[16,33]{1,0:T(8,128)S(1)}, u32[]{:S(2)}, u32[]{:S(2)}) collective-permute-start(s32[16,33]{1,0:T(8,128)S(1)} %get-tuple-element.110), channel_id=1, source_target_pairs={{0,4},{2,6},{4,8},{6,10},{8,12},{10,14},{12,16},{14,18},{16,20},{1... | collective-permute-start | bytes 6344 | tf_op jit(solution)/shard_map/ppermute | solution.py:256
  11.5 0.2 slice_reduce_fusion.1
  12.1 2.2 %shard_map.85 = (bf16[16,64,256]{2,1,0:T(8,128)(2,1)}, bf16[16,64,256]{2,1,0:T(8,128)(2,1)}) custom-call(s32[1]{0:T(128)} %bitcast.core.refs_0_, bf16[16,64,2048]{2,1,0:T(8,128)(2,1)} %own.9), custom_call_target="tpu_custom_call" | custom-call | tf_op jit(solution)/shard_map/pallas_call | solution.py:259
  14.3 3.4 %collective-permute-start.8 = (bf16[16,64,256]{2,1,0:T(8,128)(2,1)}, bf16[16,64,256]{2,1,0:T(8,128)(2,1)S(1)}, u32[]{:S(2)}, u32[]{:S(2)}) collective-permute-start(bf16[16,64,256]{2,1,0:T(8,128)(2,1)} %get-tuple-element.66), channel_id=1, source_target_pairs={{2,4},{6,8},{10,12},{14,16},{18,20},{22,24},{26,28},{30,0},{3,5},{... | collective-permute-start | bytes 1572872 | tf_op jit(solution)/shard_map/ppermute | solution.py:271
  17.7 3.1 %collective-permute-start.9 = (bf16[16,64,256]{2,1,0:T(8,128)(2,1)}, bf16[16,64,256]{2,1,0:T(8,128)(2,1)}, u32[]{:S(2)}, u32[]{:S(2)}) collective-permute-start(bf16[16,64,256]{2,1,0:T(8,128)(2,1)} %get-tuple-element.67), channel_id=1, source_target_pairs={{2,6},{6,10},{10,14},{14,18},{18,22},{22,26},{26,30},{30,2},{3,7},... | collective-permute-start | bytes 1572872 | tf_op jit(solution)/shard_map/ppermute | solution.py:271
  21.0 0.2 dynamic-update-slice.2
  21.2 0.2 slice_reduce_fusion
  21.7 0.2 dynamic-update-slice.3
  22.0 0.1 convert_reduce_fusion.2
  22.1 0.6 fusion.44
  23.0 0.3 convert_reduce_fusion.1
  23.3 0.2 select_reduce_fusion.1
  23.5 0.2 select_reduce_fusion
  25.0 1.3 %collective-permute-start.6 = (bf16[16,64,128]{2,1,0:T(8,128)(2,1)S(1)}, bf16[16,64,128]{2,1,0:T(8,128)(2,1)S(1)}, u32[]{:S(2)}, u32[]{:S(2)}) collective-permute-start(bf16[16,64,128]{2,1,0:T(8,128)(2,1)S(1)} %broadcast_select_fusion), channel_id=1, source_target_pairs={{0,4},{2,6},{4,8},{6,10},{8,12},{10,14},{12,16},{14,18},{16,20},{1... | collective-permute-start | bytes 786440 | tf_op jit(solution)/shard_map/ppermute | solution.py:256
  26.3 1.5 %fusion.5 = f32[1024,128]{0,1:T(8,128)S(1)} fusion(f32[1024,128]{0,1:T(8,128)} %fusion.2, bf16[16,64,1024]{2,1,0:T(8,128)(2,1)S(1)} %collective-permute-done.refs_5_.sib, bf16[16,64,128]{2,1,0:T(8,128)(2,1)S(1)} %collective-permute-done.1.refs_6_.vec_s), kind=kOutput, calls=%fused_computation.4 | convolution fusion | flops 268566528 | bytes 3407872 | tf_op jit(solution)/shard_map/dot_general | solution.py:280
  27.9 1.3 %collective-permute-start.4 = (bf16[128,512]{1,0:T(8,128)(2,1)S(1)}, bf16[128,512]{1,0:T(8,128)(2,1)S(1)}, u32[]{:S(2)}, u32[]{:S(2)}) collective-permute-start(bf16[128,512]{1,0:T(8,128)(2,1)S(1)} %fusion.9), channel_id=1, source_target_pairs={{0,4},{2,6},{4,0},{6,2},{8,12},{10,14},{12,8},{14,10},{16,20},{18,... | collective-permute-start | bytes 393224 | tf_op jit(solution)/shard_map/ppermute | solution.py:218
  29.1 10.7 %shard_map.83 = (f32[32,64,128]{2,1,0:T(8,128)S(1)}, bf16[32,1024,256]{2,1,0:T(8,128)(2,1)S(1)}) custom-call(s32[1]{0:T(128)} %bitcast.core.refs_0_, s32[544]{0:T(1024)S(1)} %broadcast_add_fusion.refs_1_, s32[1]{0:T(128)} %bitcast.6.refs_2_, bf16[16,64,2048]{2,1,0:T(8,128)(2,1)S(1)} %copy-done.1, bf16[16,64,128]{2,1,0:T(8,128)(2,1)S(1)} %copy-done.2, ...), custom_call_target="tpu_custom_call" | custom-call | flops 5368709120 | bytes 1048576 | tf_op jit(solution)/shard_map/pallas_call | solution.py:335
  39.9 0.6 dynamic-slice_select_fusion
  40.5 1.1 collective-permute-done.4
  41.8 8.6 %shard_map.84.refs_8_ = f32[32,64,128]{2,1,0:T(8,128)S(1)} custom-call(s32[1]{0:T(128)} %bitcast.core.refs_0_, s32[544]{0:T(1024)S(1)} %broadcast_add_fusion.refs_1_, s32[1]{0:T(128)} %bitcast.6.refs_2_, bf16[16,64,2048]{2,1,0:T(8,128)(2,1)S(1)} %copy-done.1, bf16[16,64,128]{2,1,0:T(8,128)(2,1)S(1)} %copy-done.2, ...), custom_call_target="tpu_custom_call", output_to_operand_aliasing={{}: (8, {})} | custom-call | flops 5368709120 | bytes 1048576 | tf_op jit(solution)/shard_map/pallas_call | solution.py:353
  50.5 1.7 %collective-permute-start.12 = (bf16[16,64,256]{2,1,0:T(8,128)(2,1)S(1)}, bf16[16,64,256]{2,1,0:T(8,128)(2,1)S(1)}, u32[]{:S(2)}, u32[]{:S(2)}) collective-permute-start(bf16[16,64,256]{2,1,0:T(8,128)(2,1)S(1)} %get-tuple-element.81), channel_id=1, source_target_pairs={{0,4},{2,6},{4,8},{6,10},{8,12},{10,14},{12,16},{14,18},{16,20},{1... | collective-permute-start | bytes 1572872 | tf_op jit(solution)/shard_map/ppermute | solution.py:276
  52.3 16.3 %shard_map.86.near = f32[32,64,128]{2,1,0:T(8,128)S(1)} custom-call(s32[1]{0:T(128)} %bitcast.core.refs_0_, s32[544]{0:T(1024)S(1)} %broadcast_add_fusion.refs_1_, s32[1]{0:T(128)} %bitcast.6.refs_2_, bf16[16,64,2048]{2,1,0:T(8,128)(2,1)S(1)} %copy-done.1, bf16[16,64,128]{2,1,0:T(8,128)(2,1)S(1)} %copy-done.2, ...), custom_call_target="tpu_custom_call", output_to_operand_aliasing={{}: (8, {})} | custom-call | flops 10737418240 | bytes 1048576 | tf_op jit(solution)/shard_map/pallas_call | solution.py:353
  68.7 7.0 %shard_map.87.refs_0_ = f32[32,64,128]{2,1,0:T(8,128)S(1)} custom-call(s32[1]{0:T(128)} %bitcast.core.refs_0_, s32[544]{0:T(1024)S(1)} %broadcast_add_fusion.1.listed, s32[1]{0:T(128)} %bitcast.7.rounds, bf16[16,64,2048]{2,1,0:T(8,128)(2,1)S(1)} %copy-done.1, bf16[16,64,128]{2,1,0:T(8,128)(2,1)S(1)} %copy-done.2, ...), custom_call_target="tpu_custom_call" | custom-call | flops 268435456 | bytes 1048576 | tf_op jit(solution)/shard_map/pallas_call | solution.py:368
  75.7 6.0 %shard_map.88.refs_0_ = f32[32,64,128]{2,1,0:T(8,128)S(1)} custom-call(s32[1]{0:T(128)} %bitcast.core.refs_0_, s32[544]{0:T(1024)S(1)} %broadcast_add_fusion.1.listed, s32[1]{0:T(128)} %bitcast.7.rounds, bf16[16,64,2048]{2,1,0:T(8,128)(2,1)S(1)} %copy-done.1, bf16[16,64,128]{2,1,0:T(8,128)(2,1)S(1)} %copy-done.2, ...), custom_call_target="tpu_custom_call", output_to_operand_aliasing={{}: (9, {})} | custom-call | flops 268435456 | bytes 1048576 | tf_op jit(solution)/shard_map/pallas_call | solution.py:368
  81.8 5.2 %collective-permute-start.11 = (bf16[128,512]{1,0:T(8,128)(2,1)S(1)}, bf16[128,512]{1,0:T(8,128)(2,1)S(1)}, u32[]{:S(2)}, u32[]{:S(2)}) collective-permute-start(bf16[128,512]{1,0:T(8,128)(2,1)S(1)} %add_convert_fusion.1), channel_id=1, source_target_pairs={{0,4},{2,6},{4,0},{6,2},{8,12},{10,14},{12,8},{14,10},{16,20},{18,... | collective-permute-start | bytes 393224 | tf_op jit(solution)/shard_map/ppermute | solution.py:218
  86.9 6.0 %shard_map.89.refs_0_ = f32[32,64,128]{2,1,0:T(8,128)S(1)} custom-call(s32[1]{0:T(128)} %bitcast.core.refs_0_, s32[544]{0:T(1024)S(1)} %broadcast_add_fusion.1.listed, s32[1]{0:T(128)} %bitcast.7.rounds, bf16[16,64,2048]{2,1,0:T(8,128)(2,1)S(1)} %copy-done.1, bf16[16,64,128]{2,1,0:T(8,128)(2,1)S(1)} %copy-done.2, ...), custom_call_target="tpu_custom_call", output_to_operand_aliasing={{}: (9, {})} | custom-call | flops 268435456 | bytes 1048576 | tf_op jit(solution)/shard_map/pallas_call | solution.py:368
  93.0 6.2 %shard_map.90.far = f32[32,64,128]{2,1,0:T(8,128)S(1)} custom-call(s32[1]{0:T(128)} %bitcast.core.refs_0_, s32[544]{0:T(1024)S(1)} %broadcast_add_fusion.1.listed, s32[1]{0:T(128)} %bitcast.7.rounds, bf16[16,64,2048]{2,1,0:T(8,128)(2,1)S(1)} %copy-done.1, bf16[16,64,128]{2,1,0:T(8,128)(2,1)S(1)} %copy-done.2, ...), custom_call_target="tpu_custom_call", output_to_operand_aliasing={{}: (9, {})} | custom-call | flops 268435456 | bytes 1048576 | tf_op jit(solution)/shard_map/pallas_call | solution.py:368
  99.4 1.4 %shard_map.91 = (bf16[32,64,128]{2,1,0:T(8,128)(2,1)S(1)}, f32[32,64,128]{2,1,0:T(8,128)S(1)}) custom-call(s32[1]{0:T(128)} %bitcast.core.refs_0_, bf16[16,64,2048]{2,1,0:T(8,128)(2,1)S(1)} %copy-done.1, bf16[16,64,1024]{2,1,0:T(8,128)(2,1)S(1)} %collective-permute-done.refs_5_.sib, bf16[128,1024]{1,0:T(8,128)(2,1)S(1)} %multiply_convert_fusion.s2, ...), custom_call_target="tpu_custom_call" | custom-call | flops 536870912 | bytes 1048576 | tf_op jit(solution)/shard_map/pallas_call | solution.py:385
  100.8 1.0 copy-done.3
  101.8 0.8 collective-permute-start.14
  102.5 1.5 %collective-permute-done.14 = bf16[32,64,128]{2,1,0:T(8,128)(2,1)S(1)} collective-permute-done((bf16[32,64,128]{2,1,0:T(8,128)(2,1)S(1)}, bf16[32,64,128]{2,1,0:T(8,128)(2,1)S(1)}, u32[]{:S(2)}, u32[]{:S(2)}) %collective-permute-start.14) | collective-permute-done | bytes 524320 | tf_op jit(solution)/shard_map/ppermute | solution.py:394
  104.1 1.4 %convert_add_fusion = f32[32,64,128]{2,1,0:T(8,128)S(1)} fusion(f32[32,64,128]{2,1,0:T(8,128)} %copy-done.3, bf16[32,64,128]{2,1,0:T(8,128)(2,1)S(1)} %collective-permute-done.14), kind=kLoop, calls=%fused_computation.9 | loop fusion | flops 524288 | bytes 2621440 | tf_op jit(solution)/shard_map/add | solution.py:394
  105.5 0.1 fusion.48
  105.7 3.1 %collective-permute-start.17 = (bf16[16,32,128]{2,1,0:T(8,128)(2,1)S(1)}, bf16[16,32,128]{2,1,0:T(8,128)(2,1)S(1)}, u32[]{:S(2)}, u32[]{:S(2)}) collective-permute-start(bf16[16,32,128]{2,1,0:T(8,128)(2,1)S(1)} %dynamic-slice_convert_fusion), channel_id=1, source_target_pairs={{2,3},{3,2},{6,7},{7,6},{10,11},{11,10},{14,15},{15,14},{18,19},{1... | collective-permute-start | bytes 393224 | tf_op jit(solution)/shard_map/ppermute | solution.py:405
  108.9 1.9 %collective-permute-start.15 = (bf16[16,32,128]{2,1,0:T(8,128)(2,1)S(1)}, bf16[16,32,128]{2,1,0:T(8,128)(2,1)S(1)}, u32[]{:S(2)}, u32[]{:S(2)}) collective-permute-start(bf16[16,32,128]{2,1,0:T(8,128)(2,1)S(1)} %get-tuple-element.107), channel_id=1, source_target_pairs={{2,30},{3,31},{6,2},{7,3},{10,6},{11,7},{14,10},{15,11},{18,14},{1... | collective-permute-start | bytes 393224 | tf_op jit(solution)/shard_map/ppermute | solution.py:405
  110.9 3.0 %collective-permute-done.17 = bf16[16,32,128]{2,1,0:T(8,128)(2,1)S(1)} collective-permute-done((bf16[16,32,128]{2,1,0:T(8,128)(2,1)S(1)}, bf16[16,32,128]{2,1,0:T(8,128)(2,1)S(1)}, u32[]{:S(2)}, u32[]{:S(2)}) %collective-permute-start.17) | collective-permute-done | bytes 131104 | tf_op jit(solution)/shard_map/ppermute | solution.py:405
  113.9 0.7 collective-permute-done.15
  114.6 0.8 add_convert_fusion
  (88 shorter events, 3.2 us)
Async XLA Ops:
  0.0 110.9 %copy-start = (f32[16,64]{1,0:T(8,128)S(1)}, f32[16,64]{1,0:T(8,128)}, u32[]{:S(2)}) copy-start(f32[16,64]{1,0:T(8,128)} %param.10) | copy-start | bytes 12292
  0.0 3.1 %copy-start.2 = (bf16[16,64,128]{2,1,0:T(8,128)(2,1)S(1)}, bf16[16,64,128]{2,1,0:T(8,128)(2,1)}, u32[]{:S(2)}) copy-start(bf16[16,64,128]{2,1,0:T(8,128)(2,1)} %vec.7) | copy-start | bytes 786436
  0.0 3.6 %copy-start.6 = (s32[16]{0:T(128)S(1)}, s32[16]{0:T(128)}, u32[]{:S(2)}) copy-start(s32[16]{0:T(128)} %param.14) | copy-start | bytes 196
  0.0 3.7 %copy-start.5 = (s32[16,16]{1,0:T(8,128)S(1)}, s32[16,16]{1,0:T(8,128)}, u32[]{:S(2)}) copy-start(s32[16,16]{1,0:T(8,128)} %param.13) | copy-start | bytes 3076
  0.0 3.7 %copy-start.4 = (s32[16,16]{1,0:T(8,128)S(1)}, s32[16,16]{1,0:T(8,128)}, u32[]{:S(2)}) copy-start(s32[16,16]{1,0:T(8,128)} %param.15) | copy-start | bytes 3076
  3.0 23.3 %collective-permute-start = (bf16[16,64,1024]{2,1,0:T(8,128)(2,1)}, bf16[16,64,1024]{2,1,0:T(8,128)(2,1)S(1)}, u32[]{:S(2)}, u32[]{:S(2)}) collective-permute-start(bf16[16,64,1024]{2,1,0:T(8,128)(2,1)} %shard_map.82), channel_id=1, source_target_pairs={{0,2},{2,0},{4,6},{6,4},{8,10},{10,8},{12,14},{14,12},{16,18},{18,... | collective-permute-start | bytes 6291464 | tf_op jit(solution)/shard_map/ppermute | solution.py:269
  3.1 21.8 %collective-permute-start.1 = (bf16[16,64,128]{2,1,0:T(8,128)(2,1)S(1)}, bf16[16,64,128]{2,1,0:T(8,128)(2,1)S(1)}, u32[]{:S(2)}, u32[]{:S(2)}) collective-permute-start(bf16[16,64,128]{2,1,0:T(8,128)(2,1)S(1)} %copy-done.2), channel_id=1, source_target_pairs={{0,2},{2,0},{4,6},{6,4},{8,10},{10,8},{12,14},{14,12},{16,18},{18,... | collective-permute-start | bytes 786440 | tf_op jit(solution)/shard_map/ppermute | solution.py:254
  3.8 3.8 %collective-permute-start.2 = (s32[16,33]{1,0:T(8,128)S(1)}, s32[16,33]{1,0:T(8,128)S(1)}, u32[]{:S(2)}, u32[]{:S(2)}) collective-permute-start(s32[16,33]{1,0:T(8,128)S(1)} %pad_add_fusion), channel_id=1, source_target_pairs={{0,2},{2,0},{4,6},{6,4},{8,10},{10,8},{12,14},{14,12},{16,18},{18,... | collective-permute-start | bytes 6344 | tf_op jit(solution)/shard_map/ppermute | solution.py:253
  8.8 12.3 %collective-permute-start.3 = (s32[16,33]{1,0:T(8,128)S(1)}, s32[16,33]{1,0:T(8,128)S(1)}, u32[]{:S(2)}, u32[]{:S(2)}) collective-permute-start(s32[16,33]{1,0:T(8,128)S(1)} %get-tuple-element.110), channel_id=1, source_target_pairs={{0,4},{2,6},{4,8},{6,10},{8,12},{10,14},{12,16},{14,18},{16,20},{1... | collective-permute-start | bytes 6344 | tf_op jit(solution)/shard_map/ppermute | solution.py:256
  14.3 36.2 %collective-permute-start.8 = (bf16[16,64,256]{2,1,0:T(8,128)(2,1)}, bf16[16,64,256]{2,1,0:T(8,128)(2,1)S(1)}, u32[]{:S(2)}, u32[]{:S(2)}) collective-permute-start(bf16[16,64,256]{2,1,0:T(8,128)(2,1)} %get-tuple-element.66), channel_id=1, source_target_pairs={{2,4},{6,8},{10,12},{14,16},{18,20},{22,24},{26,28},{30,0},{3,5},{... | collective-permute-start | bytes 1572872 | tf_op jit(solution)/shard_map/ppermute | solution.py:271
  17.7 32.8 %collective-permute-start.9 = (bf16[16,64,256]{2,1,0:T(8,128)(2,1)}, bf16[16,64,256]{2,1,0:T(8,128)(2,1)}, u32[]{:S(2)}, u32[]{:S(2)}) collective-permute-start(bf16[16,64,256]{2,1,0:T(8,128)(2,1)} %get-tuple-element.67), channel_id=1, source_target_pairs={{2,6},{6,10},{10,14},{14,18},{18,22},{22,26},{26,30},{30,2},{3,7},... | collective-permute-start | bytes 1572872 | tf_op jit(solution)/shard_map/ppermute | solution.py:271
  24.9 4.2 %copy-start.1 = (bf16[16,64,2048]{2,1,0:T(8,128)(2,1)S(1)}, bf16[16,64,2048]{2,1,0:T(8,128)(2,1)}, u32[]{:S(2)}) copy-start(bf16[16,64,2048]{2,1,0:T(8,128)(2,1)} %own.9) | copy-start | bytes 12582916
  25.0 16.8 %collective-permute-start.6 = (bf16[16,64,128]{2,1,0:T(8,128)(2,1)S(1)}, bf16[16,64,128]{2,1,0:T(8,128)(2,1)S(1)}, u32[]{:S(2)}, u32[]{:S(2)}) collective-permute-start(bf16[16,64,128]{2,1,0:T(8,128)(2,1)S(1)} %broadcast_select_fusion), channel_id=1, source_target_pairs={{0,4},{2,6},{4,8},{6,10},{8,12},{10,14},{12,16},{14,18},{16,20},{1... | collective-permute-start | bytes 786440 | tf_op jit(solution)/shard_map/ppermute | solution.py:256
  27.9 13.7 %collective-permute-start.4 = (bf16[128,512]{1,0:T(8,128)(2,1)S(1)}, bf16[128,512]{1,0:T(8,128)(2,1)S(1)}, u32[]{:S(2)}, u32[]{:S(2)}) collective-permute-start(bf16[128,512]{1,0:T(8,128)(2,1)S(1)} %fusion.9), channel_id=1, source_target_pairs={{0,4},{2,6},{4,0},{6,2},{8,12},{10,14},{12,8},{14,10},{16,20},{18,... | collective-permute-start | bytes 393224 | tf_op jit(solution)/shard_map/ppermute | solution.py:218
  41.6 8.7 %collective-permute-start.5 = (bf16[128,512]{1,0:T(8,128)(2,1)S(1)}, bf16[128,512]{1,0:T(8,128)(2,1)S(1)}, u32[]{:S(2)}, u32[]{:S(2)}) collective-permute-start(bf16[128,512]{1,0:T(8,128)(2,1)S(1)} %fusion.10), channel_id=1, source_target_pairs={{0,8},{2,10},{4,12},{6,14},{8,0},{10,2},{12,4},{14,6},{16,24},{18,... | collective-permute-start | bytes 393224 | tf_op jit(solution)/shard_map/ppermute | solution.py:218
  41.7 33.9 %collective-permute-start.10 = (bf16[16,64,256]{2,1,0:T(8,128)(2,1)S(1)}, bf16[16,64,256]{2,1,0:T(8,128)(2,1)S(1)}, u32[]{:S(2)}, u32[]{:S(2)}) collective-permute-start(bf16[16,64,256]{2,1,0:T(8,128)(2,1)S(1)} %get-tuple-element.76), channel_id=1, source_target_pairs={{0,4},{2,6},{4,8},{6,10},{8,12},{10,14},{12,16},{14,18},{16,20},{1... | collective-permute-start | bytes 1572872 | tf_op jit(solution)/shard_map/ppermute | solution.py:276
  50.4 31.3 %collective-permute-start.7 = (bf16[128,512]{1,0:T(8,128)(2,1)S(1)}, bf16[128,512]{1,0:T(8,128)(2,1)S(1)}, u32[]{:S(2)}, u32[]{:S(2)}) collective-permute-start(bf16[128,512]{1,0:T(8,128)(2,1)S(1)} %fusion.8), channel_id=1, source_target_pairs={{0,16},{2,18},{4,20},{6,22},{8,24},{10,26},{12,28},{14,30},{16,0},... | collective-permute-start | bytes 393224 | tf_op jit(solution)/shard_map/ppermute | solution.py:218
  50.5 36.4 %collective-permute-start.12 = (bf16[16,64,256]{2,1,0:T(8,128)(2,1)S(1)}, bf16[16,64,256]{2,1,0:T(8,128)(2,1)S(1)}, u32[]{:S(2)}, u32[]{:S(2)}) collective-permute-start(bf16[16,64,256]{2,1,0:T(8,128)(2,1)S(1)} %get-tuple-element.81), channel_id=1, source_target_pairs={{0,4},{2,6},{4,8},{6,10},{8,12},{10,14},{12,16},{14,18},{16,20},{1... | collective-permute-start | bytes 1572872 | tf_op jit(solution)/shard_map/ppermute | solution.py:276
  52.3 40.7 %collective-permute-start.13 = (bf16[16,64,256]{2,1,0:T(8,128)(2,1)S(1)}, bf16[16,64,256]{2,1,0:T(8,128)(2,1)S(1)}, u32[]{:S(2)}, u32[]{:S(2)}) collective-permute-start(bf16[16,64,256]{2,1,0:T(8,128)(2,1)S(1)} %get-tuple-element.82), channel_id=1, source_target_pairs={{0,4},{2,6},{4,8},{6,10},{8,12},{10,14},{12,16},{14,18},{16,20},{1... | collective-permute-start | bytes 1572872 | tf_op jit(solution)/shard_map/ppermute | solution.py:276
  75.6 11.3 %copy-start.7 = (f32[2048]{0:T(1024)S(1)}, f32[2048]{0:T(1024)}, u32[]{:S(2)}) copy-start(f32[2048]{0:T(1024)} %param.11) | copy-start | bytes 24580
  81.8 17.4 %collective-permute-start.11 = (bf16[128,512]{1,0:T(8,128)(2,1)S(1)}, bf16[128,512]{1,0:T(8,128)(2,1)S(1)}, u32[]{:S(2)}, u32[]{:S(2)}) collective-permute-start(bf16[128,512]{1,0:T(8,128)(2,1)S(1)} %add_convert_fusion.1), channel_id=1, source_target_pairs={{0,4},{2,6},{4,0},{6,2},{8,12},{10,14},{12,8},{14,10},{16,20},{18,... | collective-permute-start | bytes 393224 | tf_op jit(solution)/shard_map/ppermute | solution.py:218
  100.8 1.0 copy-start.3
  101.8 2.3 %collective-permute-start.14 = (bf16[32,64,128]{2,1,0:T(8,128)(2,1)S(1)}, bf16[32,64,128]{2,1,0:T(8,128)(2,1)S(1)}, u32[]{:S(2)}, u32[]{:S(2)}) collective-permute-start(bf16[32,64,128]{2,1,0:T(8,128)(2,1)S(1)} %get-tuple-element.89), channel_id=1, source_target_pairs={{0,2},{2,0},{4,6},{6,4},{8,10},{10,8},{12,14},{14,12},{16,18},{18,... | collective-permute-start | bytes 1572872 | tf_op jit(solution)/shard_map/ppermute | solution.py:394
  105.7 8.2 %collective-permute-start.17 = (bf16[16,32,128]{2,1,0:T(8,128)(2,1)S(1)}, bf16[16,32,128]{2,1,0:T(8,128)(2,1)S(1)}, u32[]{:S(2)}, u32[]{:S(2)}) collective-permute-start(bf16[16,32,128]{2,1,0:T(8,128)(2,1)S(1)} %dynamic-slice_convert_fusion), channel_id=1, source_target_pairs={{2,3},{3,2},{6,7},{7,6},{10,11},{11,10},{14,15},{15,14},{18,19},{1... | collective-permute-start | bytes 393224 | tf_op jit(solution)/shard_map/ppermute | solution.py:405
  108.9 5.0 %collective-permute-start.16 = (bf16[16,32,128]{2,1,0:T(8,128)(2,1)S(1)}, bf16[16,32,128]{2,1,0:T(8,128)(2,1)S(1)}, u32[]{:S(2)}, u32[]{:S(2)}) collective-permute-start(bf16[16,32,128]{2,1,0:T(8,128)(2,1)S(1)} %get-tuple-element.108), channel_id=1, source_target_pairs={{0,1},{1,0},{4,5},{5,4},{8,9},{9,8},{12,13},{13,12},{16,17},{17,16... | collective-permute-start | bytes 393224 | tf_op jit(solution)/shard_map/ppermute | solution.py:405
  108.9 5.7 %collective-permute-start.15 = (bf16[16,32,128]{2,1,0:T(8,128)(2,1)S(1)}, bf16[16,32,128]{2,1,0:T(8,128)(2,1)S(1)}, u32[]{:S(2)}, u32[]{:S(2)}) collective-permute-start(bf16[16,32,128]{2,1,0:T(8,128)(2,1)S(1)} %get-tuple-element.107), channel_id=1, source_target_pairs={{2,30},{3,31},{6,2},{7,3},{10,6},{11,7},{14,10},{15,11},{18,14},{1... | collective-permute-start | bytes 393224 | tf_op jit(solution)/shard_map/ppermute | solution.py:405

commit v7 on v6

--- a/solution.py
+++ b/solution.py
@@ -71,14 +71,29 @@
         starts = [pl.multiple_of((1 - core[0]) * half_g, size)]
     else:
         starts = [0, half_g]
+    part = source.shape[0] // 4
     copies = [
-        pltpu.make_async_copy(source.at[:, :, pl.ds(start, size)], out, sems.at[i])
+        pltpu.make_async_copy(
+            source.at[pl.ds(j * part, part), :, pl.ds(start, size)], out.at[pl.ds(j * part, part)], sems.at[i, j]
+        )
         for i, (start, out) in enumerate(zip(starts, outs))
+        for j in range(4)
     ]
     for copy in copies:
         copy.start()
     for copy in copies:
         copy.wait()
+
+
+def density_kernel(core, own, vec, sib, vec_s, out):
+    half_g = sib.shape[2]
+    rows = lambda value: value.reshape(value.shape[0] * value.shape[1], value.shape[2])
+
+    def over_pairs(v, d):
+        return lax.dot_general(rows(v), rows(d), (((0,), (0,)), ((), ())), preferred_element_type=F32)
+
+    mine = own[:, :, pl.ds(pl.multiple_of(core[0] * half_g, half_g), half_g)]
+    out[...] = over_pairs(vec[...], mine) + over_pairs(vec_s[...], sib[...])
 
 
 def near_kernel(start, count, load, *refs):
@@ -157,7 +172,7 @@
         one_group(listed, rounds, w, g * width, slabs, vectors, out, prod, total, fresh and g == start)
 
 
-def last_kernel(core, own, sib, s2, near, far, give, keep):
+def last_kernel(core, own, sib, s2, near, far, give, edge, inner):
     half, pairs, _ = own.shape
     trials, half_g = s2.shape
     width = 256
@@ -174,15 +189,15 @@
 
     @pl.when(core[0] == 0)
     def _():
-        keep[:half] = mine - far[:half]
-        keep[half:] = other
+        edge[...] = mine - far[:half]
+        inner[...] = other
         give[:half] = (-far[half:]).astype(BF16)
         give[half:] = other.astype(BF16)
 
     @pl.when(core[0] != 0)
     def _():
-        keep[:half] = -far[half:]
-        keep[half:] = mine
+        edge[...] = -far[half:]
+        inner[...] = mine
         give[:half] = (other - far[:half]).astype(BF16)
         give[half:] = mine.astype(BF16)
 
@@ -252,8 +267,8 @@
     table = jnp.concatenate([offset * local_k + neighbors % local_k, q_index, live_count[:, None]], axis=1)
     table_s = lax.ppermute(table, "ka", sibling)
     vec_s = lax.ppermute(trial_vectors, "ka", sibling)
-    edge = (pick(table_s, table), pick(vec_s, trial_vectors))
-    table_p, vec_p = (lax.ppermute(value, "ka", onward) for value in edge)
+    edge = pick(table_s, table)
+    table_p = lax.ppermute(edge, "ka", onward)
 
     def packed(core_id, last, count):
         return pl.pallas_call(
@@ -261,11 +276,11 @@
             out_shape=[jax.ShapeDtypeStruct((local_k, pair_count, last), BF16)] * count,
             in_specs=[IN_SMEM, ANYWHERE],
             out_specs=[IN_VMEM] * count,
-            scratch_shapes=[pltpu.SemaphoreType.DMA((count,))],
+            scratch_shapes=[pltpu.SemaphoreType.DMA((count, 4))],
         )(core_id, pair_density)
 
     (give_half,) = packed(core_id, half_g, 1)
-    first_pieces = packed(lax.optimization_barrier((core_id, edge[0]))[0], width, 2)
+    first_pieces = packed(lax.optimization_barrier((core_id, edge))[0], width, 2)
     sib = lax.ppermute(give_half, "ka", sibling)
     own_half = lax.dynamic_slice_in_dim(pair_density, core * half_g, half_g, 2)
     came = [[lax.ppermute(piece, "ka", pairs) for piece, pairs in zip(first_pieces, to_next)]]
@@ -277,8 +292,13 @@
         piece, value = lax.optimization_barrier((piece, value))
         return value
 
-    contract = lambda v, d: lax.dot_general(v, d, (((0, 1), (0, 1)), ((), ())), preferred_element_type=F32)
-    part = contract(trial_vectors, own_half) + contract(vec_s, sib)
+    part = pl.pallas_call(
+        density_kernel,
+        out_shape=jax.ShapeDtypeStruct((trial_count, half_g), F32),
+        in_specs=[IN_SMEM] + [IN_VMEM] * 4,
+        out_specs=IN_VMEM,
+        compiler_params=pltpu.CompilerParams(vmem_limit_bytes=12 << 20),
+    )(core_id, pair_density, trial_vectors, sib, vec_s)
     density = Density(density_steps(part, me, size), size)
     my_coulomb = lax.dynamic_slice_in_dim(coulomb, core * half_g, half_g, 0)
 
@@ -342,12 +362,13 @@
         cost_estimate=cost(1, 160),
     )(core_id, near_list, near_rounds, pair_density, trial_vectors, sib, vec_s, screen)
     near = density.after(near)
-    near, vec_p = lax.optimization_barrier((near, vec_p))
+    edge_vec, near = lax.optimization_barrier((pick(vec_s, trial_vectors), near))
+    vec_p = lax.ppermute(edge_vec, "ka", onward)
     for start, count, going in ((1, 1, (1,)), (2, groups - 2, range(2, groups))):
         if count < 1 or start >= groups:
             continue
         if start == 2:
-            near, *came[0] = lax.optimization_barrier((near, *came[0]))
+            near, vec_p, *came[0] = lax.optimization_barrier((near, vec_p, *came[0]))
         for g in going:
             near = send_group(g, near)
         near = pl.pallas_call(
@@ -379,20 +400,21 @@
             core_id, far_list, far_rounds, pair_density, trial_vectors, sib, vec_s, w_half, vec_p,
             *([far] if c else []), *came[c],
         )
-        if c in (1, groups - 1):
+        if c >= groups - 2:
             far = density.after(far)
     screened2 = (2.0 * my_coulomb[None, :] * density.finish().astype(F32)).astype(BF16)
-    give, keep = pl.pallas_call(
+    half_sums = jax.ShapeDtypeStruct((local_k, pair_count, trial_count), F32)
+    give, edge, inner = pl.pallas_call(
         last_kernel,
-        out_shape=(jax.ShapeDtypeStruct(sums.shape, BF16), sums),
+        out_shape=(jax.ShapeDtypeStruct(sums.shape, BF16), half_sums, half_sums),
         in_specs=[IN_SMEM] + [IN_VMEM] * 5,
-        out_specs=(IN_VMEM, IN_VMEM),
+        out_specs=(IN_VMEM,) * 3,
         compiler_params=params(),
         cost_estimate=cost(1, 16),
     )(core_id, pair_density, sib, screened2, near, far)
 
-    both = keep + lax.ppermute(give, "ka", sibling).astype(F32)
-    edge, inner = both[:local_k], both[local_k:]
+    got = lax.ppermute(give, "ka", sibling)
+    edge, inner = edge + got[:local_k].astype(F32), inner + got[local_k:].astype(F32)
     rows = pair_count // parts
     rows_of = lambda value, at: lax.dynamic_slice_in_dim(value, at * rows, rows, 1)
     stay = lambda first: [(i, i) for i in range(first, size, 2)]

time: 116 us -> 111 us (0.957)
  Pallas kernels: 67.5 us -> 57.8 us
  waiting for transfers between devices: 6.4 us -> 14.1 us
  matrix products: 4.42 us -> 0 us
    pallas_call x2, Pallas kernels: 24.9 us -> 19.2 us  [on_device(): pl.pallas_call(functools.partial(near_kernel, start, count, False), out_s...]
    ppermute x3, waiting for transfers between devices: 1.54 us -> 6.26 us  [the longest x1 4.51 us: on_device(): vec_p = lax.ppermute(edge_vec, 'ka', onward)]
    dot_general x2 -> x0, matrix products: 4.42 us -> none  [on_device(): lax.dot_general(v, d, (((0, 1), (0, 1)), ((), ())), preferred_element_typ...]
    pallas_call x4, Pallas kernels: 25.2 us -> 21.4 us  [on_device(): pl.pallas_call(functools.partial(far_kernel, c, 1, c == 0, len(came[c])),...]
    ppermute x1, waiting for transfers between devices: 0.01 us -> 2.54 us  [on_device(): table_s = lax.ppermute(table, 'ka', sibling)]
    pallas_call x1, Pallas kernels: 10.7 us -> 8.88 us  [on_device(): pl.pallas_call(functools.partial(near_kernel, 0, 1, True), out_shape=(sum...]
    ppermute x4, starting transfers between devices: 6.57 us -> 8.41 us  [after(): lax.ppermute(self.give, 'ka', [(i, i ^ self.bit) for i in range(self.size)])]
    ppermute x3, waiting for transfers between devices: 0.01 us -> 1.61 us  [send_group(): came.append([lax.ppermute(piece, 'ka', onward)])]
  transfers between devices with their start and end apart: 18 -> 18, of which waited for: 4 -> 6; matrix products, arithmetic and copies ran while one was open for 9% -> 6% of each run, Pallas kernels for 55% -> 48%
where the time goes in v7:
time: 111 us; the launch traced here: 110 us
  Pallas kernels  57.8 us (52%)
  starting transfers between devices  26.3 us (24%)
  waiting for transfers between devices  14.1 us (13%)
  local copies, waits for them, and re-layouts  5.22 us (5%)
  other arithmetic  4.79 us (4%)
  between operations  1.76 us (2%)
    pallas_call x4, Pallas kernels, on_device(): pl.pallas_call(functools.partial(far_kernel, c, 1, c == 0, len(came[c])),...  21.4 us
    pallas_call x2, Pallas kernels, on_device(): pl.pallas_call(functools.partial(near_kernel, start, count, False), out_s...  19.2 us
    pallas_call x1, Pallas kernels, on_device(): pl.pallas_call(functools.partial(near_kernel, 0, 1, True), out_shape=(sum...  8.88 us
    ppermute x4, starting transfers between devices, after(): lax.ppermute(self.give, 'ka', [(i, i ^ self.bit) for i in range(self.size)])  8.41 us
    ppermute x2, starting transfers between devices, on_device(): lax.ppermute(piece, 'ka', pairs)  6.64 us
    pallas_call x2, Pallas kernels, packed(): pl.pallas_call(pack_kernel, out_shape=[jax.ShapeDtypeStruct((local_k, pai...  5.3 us
    ppermute x3, starting transfers between devices, sent(): lax.ppermute(rows_of(value, (mine + steps) % parts).astype(BF16), ('ka',...  5.13 us
    ppermute x1, waiting for transfers between devices, on_device(): vec_p = lax.ppermute(edge_vec, 'ka', onward)  4.51 us
  transfers between devices with their start and end apart: 18, of which 6 were waited for; matrix products, arithmetic and copies ran while one was open for 6% of the time, Pallas kernels for 48%

profile of v7, /device:TPU:1, one launch (start us, length us, event | category | flops | bytes accessed | tf_op | source)
XLA Modules:
  0.0 110.0 jit_solution(8935036704077118780)
XLA Ops:
  0.0 2.9 %shard_map.82 = bf16[16,64,1024]{2,1,0:T(8,128)(2,1)} custom-call(s32[1]{0:T(128)} %bitcast.core.refs_0_, bf16[16,64,2048]{2,1,0:T(8,128)(2,1)} %own.11), custom_call_target="tpu_custom_call" | custom-call | tf_op jit(solution)/shard_map/pallas_call | solution.py:274
  3.0 0.1 collective-permute-start
  3.1 0.5 collective-permute-start.1
  4.5 0.2 dynamic-update-slice.4
  4.7 2.5 %collective-permute-done.2 = s32[16,33]{1,0:T(8,128)S(1)} collective-permute-done((s32[16,33]{1,0:T(8,128)S(1)}, s32[16,33]{1,0:T(8,128)S(1)}, u32[]{:S(2)}, u32[]{:S(2)}) %collective-permute-start.2) | collective-permute-done | bytes 2144 | tf_op jit(solution)/shard_map/ppermute | solution.py:268
  7.4 0.2 slice_reduce_fusion.2
  7.8 0.2 dynamic-update-slice.5
  8.0 0.1 convert_reduce_fusion.3
  8.1 0.3 convert_reduce_fusion
  8.5 2.5 %collective-permute-start.3 = (s32[16,33]{1,0:T(8,128)S(1)}, s32[16,33]{1,0:T(8,128)S(1)}, u32[]{:S(2)}, u32[]{:S(2)}) collective-permute-start(s32[16,33]{1,0:T(8,128)S(1)} %get-tuple-element.114), channel_id=1, source_target_pairs={{0,4},{2,6},{4,8},{6,10},{8,12},{10,14},{12,16},{14,18},{16,20},{1... | collective-permute-start | bytes 6344 | tf_op jit(solution)/shard_map/ppermute | solution.py:271
  11.0 0.2 slice_reduce_fusion.1
  11.6 2.4 %shard_map.86 = (bf16[16,64,256]{2,1,0:T(8,128)(2,1)}, bf16[16,64,256]{2,1,0:T(8,128)(2,1)}) custom-call(s32[1]{0:T(128)} %bitcast.core.refs_0_, bf16[16,64,2048]{2,1,0:T(8,128)(2,1)} %own.11), custom_call_target="tpu_custom_call" | custom-call | tf_op jit(solution)/shard_map/pallas_call | solution.py:274
  14.0 3.5 %collective-permute-start.8 = (bf16[16,64,256]{2,1,0:T(8,128)(2,1)}, bf16[16,64,256]{2,1,0:T(8,128)(2,1)S(1)}, u32[]{:S(2)}, u32[]{:S(2)}) collective-permute-start(bf16[16,64,256]{2,1,0:T(8,128)(2,1)} %get-tuple-element.69), channel_id=1, source_target_pairs={{2,4},{6,8},{10,12},{14,16},{18,20},{22,24},{26,28},{30,0},{3,5},{... | collective-permute-start | bytes 1572872 | tf_op jit(solution)/shard_map/ppermute | solution.py:286
  17.5 3.1 %collective-permute-start.9 = (bf16[16,64,256]{2,1,0:T(8,128)(2,1)}, bf16[16,64,256]{2,1,0:T(8,128)(2,1)}, u32[]{:S(2)}, u32[]{:S(2)}) collective-permute-start(bf16[16,64,256]{2,1,0:T(8,128)(2,1)} %get-tuple-element.70), channel_id=1, source_target_pairs={{2,6},{6,10},{10,14},{14,18},{18,22},{22,26},{26,30},{30,2},{3,7},... | collective-permute-start | bytes 1572872 | tf_op jit(solution)/shard_map/ppermute | solution.py:286
  20.8 0.2 dynamic-update-slice.2
  21.0 0.2 slice_reduce_fusion
  21.5 0.2 dynamic-update-slice.3
  21.7 0.1 convert_reduce_fusion.2
  21.9 0.7 fusion.36
  22.8 0.3 convert_reduce_fusion.1
  23.1 0.2 select_reduce_fusion.1
  23.4 0.2 select_reduce_fusion
  24.9 2.2 %copy-done.1 = bf16[16,64,2048]{2,1,0:T(8,128)(2,1)S(1)} copy-done((bf16[16,64,2048]{2,1,0:T(8,128)(2,1)S(1)}, bf16[16,64,2048]{2,1,0:T(8,128)(2,1)}, u32[]{:S(2)}) %copy-start.1) | copy-done | bytes 4194328
  27.1 0.7 shard_map.83
  27.9 1.3 %collective-permute-start.4 = (bf16[128,512]{1,0:T(8,128)(2,1)S(1)}, bf16[128,512]{1,0:T(8,128)(2,1)S(1)}, u32[]{:S(2)}, u32[]{:S(2)}) collective-permute-start(bf16[128,512]{1,0:T(8,128)(2,1)S(1)} %dynamic-slice_convert_fusion.3), channel_id=1, source_target_pairs={{0,4},{2,6},{4,0},{6,2},{8,12},{10,14},{12,8},{14,10},{16,20},{18,... | collective-permute-start | bytes 393224 | tf_op jit(solution)/shard_map/ppermute | solution.py:233
  29.2 8.9 %shard_map.84 = (f32[32,64,128]{2,1,0:T(8,128)S(1)}, bf16[32,1024,256]{2,1,0:T(8,128)(2,1)S(1)}) custom-call(s32[1]{0:T(128)} %bitcast.core.refs_0_, s32[544]{0:T(1024)S(1)} %broadcast_add_fusion.refs_1_, s32[1]{0:T(128)} %bitcast.2.refs_2_, bf16[16,64,2048]{2,1,0:T(8,128)(2,1)S(1)} %copy-done.1, bf16[16,64,128]{2,1,0:T(8,128)(2,1)S(1)} %copy-done.3, ...), custom_call_target="tpu_custom_call" | custom-call | flops 5368709120 | bytes 1048576 | tf_op jit(solution)/shard_map/pallas_call | solution.py:355
  38.1 0.6 dynamic-slice_select_fusion
  38.8 0.5 collective-permute-start.5
  39.3 0.6 collective-permute-start.7
  39.9 1.6 %collective-permute-start.10 = (bf16[16,64,256]{2,1,0:T(8,128)(2,1)S(1)}, bf16[16,64,256]{2,1,0:T(8,128)(2,1)S(1)}, u32[]{:S(2)}, u32[]{:S(2)}) collective-permute-start(bf16[16,64,256]{2,1,0:T(8,128)(2,1)S(1)} %get-tuple-element.79), channel_id=1, source_target_pairs={{0,4},{2,6},{4,8},{6,10},{8,12},{10,14},{12,16},{14,18},{16,20},{1... | collective-permute-start | bytes 1572872 | tf_op jit(solution)/shard_map/ppermute | solution.py:291
  41.5 6.6 %shard_map.85.refs_8_ = f32[32,64,128]{2,1,0:T(8,128)S(1)} custom-call(s32[1]{0:T(128)} %bitcast.core.refs_0_, s32[544]{0:T(1024)S(1)} %broadcast_add_fusion.refs_1_, s32[1]{0:T(128)} %bitcast.2.refs_2_, bf16[16,64,2048]{2,1,0:T(8,128)(2,1)S(1)} %copy-done.2, bf16[16,64,128]{2,1,0:T(8,128)(2,1)S(1)} %copy-done.3, ...), custom_call_target="tpu_custom_call", output_to_operand_aliasing={{}: (8, {})} | custom-call | flops 5368709120 | bytes 1048576 | tf_op jit(solution)/shard_map/pallas_call | solution.py:374
  48.4 4.5 %collective-permute-done.7.vec_p = bf16[16,64,128]{2,1,0:T(8,128)(2,1)S(1)} collective-permute-done((bf16[16,64,128]{2,1,0:T(8,128)(2,1)S(1)}, bf16[16,64,128]{2,1,0:T(8,128)(2,1)S(1)}, u32[]{:S(2)}, u32[]{:S(2)}) %collective-permute-start.7) | collective-permute-done | bytes 262176 | tf_op jit(solution)/shard_map/ppermute | solution.py:366
  52.9 12.6 %shard_map.87.near = f32[32,64,128]{2,1,0:T(8,128)S(1)} custom-call(s32[1]{0:T(128)} %bitcast.core.refs_0_, s32[544]{0:T(1024)S(1)} %broadcast_add_fusion.refs_1_, s32[1]{0:T(128)} %bitcast.2.refs_2_, bf16[16,64,2048]{2,1,0:T(8,128)(2,1)S(1)} %copy-done.2, bf16[16,64,128]{2,1,0:T(8,128)(2,1)S(1)} %copy-done.3, ...), custom_call_target="tpu_custom_call", output_to_operand_aliasing={{}: (8, {})} | custom-call | flops 10737418240 | bytes 1048576 | tf_op jit(solution)/shard_map/pallas_call | solution.py:374
  65.5 6.0 %shard_map.88.refs_0_ = f32[32,64,128]{2,1,0:T(8,128)S(1)} custom-call(s32[1]{0:T(128)} %bitcast.core.refs_0_, s32[544]{0:T(1024)S(1)} %broadcast_add_fusion.1.listed, s32[1]{0:T(128)} %bitcast.3.rounds, bf16[16,64,2048]{2,1,0:T(8,128)(2,1)S(1)} %copy-done.2, bf16[16,64,128]{2,1,0:T(8,128)(2,1)S(1)} %copy-done.3, ...), custom_call_target="tpu_custom_call" | custom-call | flops 268435456 | bytes 1048576 | tf_op jit(solution)/shard_map/pallas_call | solution.py:389
  71.5 5.1 %shard_map.89.refs_0_ = f32[32,64,128]{2,1,0:T(8,128)S(1)} custom-call(s32[1]{0:T(128)} %bitcast.core.refs_0_, s32[544]{0:T(1024)S(1)} %broadcast_add_fusion.1.listed, s32[1]{0:T(128)} %bitcast.3.rounds, bf16[16,64,2048]{2,1,0:T(8,128)(2,1)S(1)} %copy-done.2, bf16[16,64,128]{2,1,0:T(8,128)(2,1)S(1)} %copy-done.3, ...), custom_call_target="tpu_custom_call", output_to_operand_aliasing={{}: (9, {})} | custom-call | flops 268435456 | bytes 1048576 | tf_op jit(solution)/shard_map/pallas_call | solution.py:389
  76.6 1.6 %collective-permute-done.11.refs_1_ = bf16[16,64,256]{2,1,0:T(8,128)(2,1)S(1)} collective-permute-done((bf16[16,64,256]{2,1,0:T(8,128)(2,1)S(1)}, bf16[16,64,256]{2,1,0:T(8,128)(2,1)S(1)}, u32[]{:S(2)}, u32[]{:S(2)}) %collective-permute-start.11) | collective-permute-done | bytes 524320 | tf_op jit(solution)/shard_map/ppermute | solution.py:291
  78.2 5.1 %shard_map.90.refs_0_ = f32[32,64,128]{2,1,0:T(8,128)S(1)} custom-call(s32[1]{0:T(128)} %bitcast.core.refs_0_, s32[544]{0:T(1024)S(1)} %broadcast_add_fusion.1.listed, s32[1]{0:T(128)} %bitcast.3.rounds, bf16[16,64,2048]{2,1,0:T(8,128)(2,1)S(1)} %copy-done.2, bf16[16,64,128]{2,1,0:T(8,128)(2,1)S(1)} %copy-done.3, ...), custom_call_target="tpu_custom_call", output_to_operand_aliasing={{}: (9, {})} | custom-call | flops 268435456 | bytes 1048576 | tf_op jit(solution)/shard_map/pallas_call | solution.py:389
  83.4 6.5 %collective-permute-start.12 = (bf16[128,512]{1,0:T(8,128)(2,1)S(1)}, bf16[128,512]{1,0:T(8,128)(2,1)S(1)}, u32[]{:S(2)}, u32[]{:S(2)}) collective-permute-start(bf16[128,512]{1,0:T(8,128)(2,1)S(1)} %add_convert_fusion.1), channel_id=1, source_target_pairs={{0,4},{2,6},{4,0},{6,2},{8,12},{10,14},{12,8},{14,10},{16,20},{18,... | collective-permute-start | bytes 393224 | tf_op jit(solution)/shard_map/ppermute | solution.py:233
  89.9 5.3 %shard_map.91.far = f32[32,64,128]{2,1,0:T(8,128)S(1)} custom-call(s32[1]{0:T(128)} %bitcast.core.refs_0_, s32[544]{0:T(1024)S(1)} %broadcast_add_fusion.1.listed, s32[1]{0:T(128)} %bitcast.3.rounds, bf16[16,64,2048]{2,1,0:T(8,128)(2,1)S(1)} %copy-done.2, bf16[16,64,128]{2,1,0:T(8,128)(2,1)S(1)} %copy-done.3, ...), custom_call_target="tpu_custom_call", output_to_operand_aliasing={{}: (9, {})} | custom-call | flops 268435456 | bytes 1048576 | tf_op jit(solution)/shard_map/pallas_call | solution.py:389
  95.3 2.2 %shard_map.92 = (bf16[32,64,128]{2,1,0:T(8,128)(2,1)}, f32[16,64,128]{2,1,0:T(8,128)S(1)}, f32[16,64,128]{2,1,0:T(8,128)S(1)}) custom-call(s32[1]{0:T(128)} %bitcast.core.refs_0_, bf16[16,64,2048]{2,1,0:T(8,128)(2,1)S(1)} %copy-done.2, bf16[16,64,1024]{2,1,0:T(8,128)(2,1)S(1)} %collective-permute-done.sib.refs_5_, ...), custom_call_target="tpu_custom_call" | custom-call | flops 536870912 | bytes 1048576 | tf_op jit(solution)/shard_map/pallas_call | solution.py:407
  97.5 0.7 collective-permute-start.14
  98.2 1.7 %collective-permute-done.14 = bf16[32,64,128]{2,1,0:T(8,128)(2,1)S(1)} collective-permute-done((bf16[32,64,128]{2,1,0:T(8,128)(2,1)}, bf16[32,64,128]{2,1,0:T(8,128)(2,1)S(1)}, u32[]{:S(2)}, u32[]{:S(2)}) %collective-permute-start.14) | collective-permute-done | bytes 524320 | tf_op jit(solution)/shard_map/ppermute | solution.py:416
  100.0 0.2 convert_add_fusion.1
  100.2 3.2 %collective-permute-start.17 = (bf16[16,32,128]{2,1,0:T(8,128)(2,1)S(1)}, bf16[16,32,128]{2,1,0:T(8,128)(2,1)S(1)}, u32[]{:S(2)}, u32[]{:S(2)}) collective-permute-start(bf16[16,32,128]{2,1,0:T(8,128)(2,1)S(1)} %dynamic-slice_convert_fusion), channel_id=1, source_target_pairs={{2,3},{3,2},{6,7},{7,6},{10,11},{11,10},{14,15},{15,14},{18,19},{1... | collective-permute-start | bytes 393224 | tf_op jit(solution)/shard_map/ppermute | solution.py:427
  103.5 1.9 %collective-permute-start.15 = (bf16[16,32,128]{2,1,0:T(8,128)(2,1)S(1)}, bf16[16,32,128]{2,1,0:T(8,128)(2,1)S(1)}, u32[]{:S(2)}, u32[]{:S(2)}) collective-permute-start(bf16[16,32,128]{2,1,0:T(8,128)(2,1)S(1)} %get-tuple-element.109), channel_id=1, source_target_pairs={{2,30},{3,31},{6,2},{7,3},{10,6},{11,7},{14,10},{15,11},{18,14},{1... | collective-permute-start | bytes 393224 | tf_op jit(solution)/shard_map/ppermute | solution.py:427
  105.5 2.9 %collective-permute-done.17 = bf16[16,32,128]{2,1,0:T(8,128)(2,1)S(1)} collective-permute-done((bf16[16,32,128]{2,1,0:T(8,128)(2,1)S(1)}, bf16[16,32,128]{2,1,0:T(8,128)(2,1)S(1)}, u32[]{:S(2)}, u32[]{:S(2)}) %collective-permute-start.17) | collective-permute-done | bytes 131104 | tf_op jit(solution)/shard_map/ppermute | solution.py:427
  108.4 0.7 collective-permute-done.15
  109.2 0.8 add_convert_fusion
  (86 shorter events, 3.1 us)
Async XLA Ops:
  0.0 105.4 %copy-start = (f32[16,64]{1,0:T(8,128)S(1)}, f32[16,64]{1,0:T(8,128)}, u32[]{:S(2)}) copy-start(f32[16,64]{1,0:T(8,128)} %param.10) | copy-start | bytes 12292
  0.0 3.1 %copy-start.3 = (bf16[16,64,128]{2,1,0:T(8,128)(2,1)S(1)}, bf16[16,64,128]{2,1,0:T(8,128)(2,1)}, u32[]{:S(2)}) copy-start(bf16[16,64,128]{2,1,0:T(8,128)(2,1)} %vec.9) | copy-start | bytes 786436
  0.0 3.5 %copy-start.6 = (s32[16]{0:T(128)S(1)}, s32[16]{0:T(128)}, u32[]{:S(2)}) copy-start(s32[16]{0:T(128)} %param.14) | copy-start | bytes 196
  0.0 3.6 %copy-start.5 = (s32[16,16]{1,0:T(8,128)S(1)}, s32[16,16]{1,0:T(8,128)}, u32[]{:S(2)}) copy-start(s32[16,16]{1,0:T(8,128)} %param.13) | copy-start | bytes 3076
  0.0 3.7 %copy-start.4 = (s32[16,16]{1,0:T(8,128)S(1)}, s32[16,16]{1,0:T(8,128)}, u32[]{:S(2)}) copy-start(s32[16,16]{1,0:T(8,128)} %param.15) | copy-start | bytes 3076
  3.0 21.9 %collective-permute-start = (bf16[16,64,1024]{2,1,0:T(8,128)(2,1)}, bf16[16,64,1024]{2,1,0:T(8,128)(2,1)S(1)}, u32[]{:S(2)}, u32[]{:S(2)}) collective-permute-start(bf16[16,64,1024]{2,1,0:T(8,128)(2,1)} %shard_map.82), channel_id=1, source_target_pairs={{0,2},{2,0},{4,6},{6,4},{8,10},{10,8},{12,14},{14,12},{16,18},{18,... | collective-permute-start | bytes 6291464 | tf_op jit(solution)/shard_map/ppermute | solution.py:284
  3.1 21.8 %collective-permute-start.1 = (bf16[16,64,128]{2,1,0:T(8,128)(2,1)S(1)}, bf16[16,64,128]{2,1,0:T(8,128)(2,1)S(1)}, u32[]{:S(2)}, u32[]{:S(2)}) collective-permute-start(bf16[16,64,128]{2,1,0:T(8,128)(2,1)S(1)} %copy-done.3), channel_id=1, source_target_pairs={{0,2},{2,0},{4,6},{6,4},{8,10},{10,8},{12,14},{14,12},{16,18},{18,... | collective-permute-start | bytes 786440 | tf_op jit(solution)/shard_map/ppermute | solution.py:269
  3.8 3.5 %collective-permute-start.2 = (s32[16,33]{1,0:T(8,128)S(1)}, s32[16,33]{1,0:T(8,128)S(1)}, u32[]{:S(2)}, u32[]{:S(2)}) collective-permute-start(s32[16,33]{1,0:T(8,128)S(1)} %pad_add_fusion), channel_id=1, source_target_pairs={{0,2},{2,0},{4,6},{6,4},{8,10},{10,8},{12,14},{14,12},{16,18},{18,... | collective-permute-start | bytes 6344 | tf_op jit(solution)/shard_map/ppermute | solution.py:268
  8.5 12.5 %collective-permute-start.3 = (s32[16,33]{1,0:T(8,128)S(1)}, s32[16,33]{1,0:T(8,128)S(1)}, u32[]{:S(2)}, u32[]{:S(2)}) collective-permute-start(s32[16,33]{1,0:T(8,128)S(1)} %get-tuple-element.114), channel_id=1, source_target_pairs={{0,4},{2,6},{4,8},{6,10},{8,12},{10,14},{12,16},{14,18},{16,20},{1... | collective-permute-start | bytes 6344 | tf_op jit(solution)/shard_map/ppermute | solution.py:271
  14.0 34.3 %collective-permute-start.8 = (bf16[16,64,256]{2,1,0:T(8,128)(2,1)}, bf16[16,64,256]{2,1,0:T(8,128)(2,1)S(1)}, u32[]{:S(2)}, u32[]{:S(2)}) collective-permute-start(bf16[16,64,256]{2,1,0:T(8,128)(2,1)} %get-tuple-element.69), channel_id=1, source_target_pairs={{2,4},{6,8},{10,12},{14,16},{18,20},{22,24},{26,28},{30,0},{3,5},{... | collective-permute-start | bytes 1572872 | tf_op jit(solution)/shard_map/ppermute | solution.py:286
  17.5 30.8 %collective-permute-start.9 = (bf16[16,64,256]{2,1,0:T(8,128)(2,1)}, bf16[16,64,256]{2,1,0:T(8,128)(2,1)}, u32[]{:S(2)}, u32[]{:S(2)}) collective-permute-start(bf16[16,64,256]{2,1,0:T(8,128)(2,1)} %get-tuple-element.70), channel_id=1, source_target_pairs={{2,6},{6,10},{10,14},{14,18},{18,22},{22,26},{26,30},{30,2},{3,7},... | collective-permute-start | bytes 1572872 | tf_op jit(solution)/shard_map/ppermute | solution.py:286
  24.9 2.2 %copy-start.1 = (bf16[16,64,2048]{2,1,0:T(8,128)(2,1)S(1)}, bf16[16,64,2048]{2,1,0:T(8,128)(2,1)}, u32[]{:S(2)}) copy-start(bf16[16,64,2048]{2,1,0:T(8,128)(2,1)} %own.11) | copy-start | bytes 12582916
  27.9 10.2 %copy-start.2 = (bf16[16,64,2048]{2,1,0:T(8,128)(2,1)S(1)}, bf16[16,64,2048]{2,1,0:T(8,128)(2,1)}, u32[]{:S(2)}) copy-start(bf16[16,64,2048]{2,1,0:T(8,128)(2,1)} %own.11) | copy-start | bytes 12582916
  27.9 10.8 %collective-permute-start.4 = (bf16[128,512]{1,0:T(8,128)(2,1)S(1)}, bf16[128,512]{1,0:T(8,128)(2,1)S(1)}, u32[]{:S(2)}, u32[]{:S(2)}) collective-permute-start(bf16[128,512]{1,0:T(8,128)(2,1)S(1)} %dynamic-slice_convert_fusion.3), channel_id=1, source_target_pairs={{0,4},{2,6},{4,0},{6,2},{8,12},{10,14},{12,8},{14,10},{16,20},{18,... | collective-permute-start | bytes 393224 | tf_op jit(solution)/shard_map/ppermute | solution.py:233
  38.8 9.4 %collective-permute-start.5 = (bf16[128,512]{1,0:T(8,128)(2,1)S(1)}, bf16[128,512]{1,0:T(8,128)(2,1)S(1)}, u32[]{:S(2)}, u32[]{:S(2)}) collective-permute-start(bf16[128,512]{1,0:T(8,128)(2,1)S(1)} %fusion.3), channel_id=1, source_target_pairs={{0,8},{2,10},{4,12},{6,14},{8,0},{10,2},{12,4},{14,6},{16,24},{18,... | collective-permute-start | bytes 393224 | tf_op jit(solution)/shard_map/ppermute | solution.py:233
  39.3 13.5 %collective-permute-start.7 = (bf16[16,64,128]{2,1,0:T(8,128)(2,1)S(1)}, bf16[16,64,128]{2,1,0:T(8,128)(2,1)S(1)}, u32[]{:S(2)}, u32[]{:S(2)}) collective-permute-start(bf16[16,64,128]{2,1,0:T(8,128)(2,1)S(1)} %broadcast_select_fusion), channel_id=1, source_target_pairs={{0,4},{2,6},{4,8},{6,10},{8,12},{10,14},{12,16},{14,18},{16,20},{1... | collective-permute-start | bytes 786440 | tf_op jit(solution)/shard_map/ppermute | solution.py:366
  39.9 31.6 %collective-permute-start.10 = (bf16[16,64,256]{2,1,0:T(8,128)(2,1)S(1)}, bf16[16,64,256]{2,1,0:T(8,128)(2,1)S(1)}, u32[]{:S(2)}, u32[]{:S(2)}) collective-permute-start(bf16[16,64,256]{2,1,0:T(8,128)(2,1)S(1)} %get-tuple-element.79), channel_id=1, source_target_pairs={{0,4},{2,6},{4,8},{6,10},{8,12},{10,14},{12,16},{14,18},{16,20},{1... | collective-permute-start | bytes 1572872 | tf_op jit(solution)/shard_map/ppermute | solution.py:291
  48.3 35.0 %collective-permute-start.6 = (bf16[128,512]{1,0:T(8,128)(2,1)S(1)}, bf16[128,512]{1,0:T(8,128)(2,1)S(1)}, u32[]{:S(2)}, u32[]{:S(2)}) collective-permute-start(bf16[128,512]{1,0:T(8,128)(2,1)S(1)} %fusion.2), channel_id=1, source_target_pairs={{0,16},{2,18},{4,20},{6,22},{8,24},{10,26},{12,28},{14,30},{16,0},... | collective-permute-start | bytes 393224 | tf_op jit(solution)/shard_map/ppermute | solution.py:233
  52.9 25.3 %collective-permute-start.11 = (bf16[16,64,256]{2,1,0:T(8,128)(2,1)S(1)}, bf16[16,64,256]{2,1,0:T(8,128)(2,1)S(1)}, u32[]{:S(2)}, u32[]{:S(2)}) collective-permute-start(bf16[16,64,256]{2,1,0:T(8,128)(2,1)S(1)} %get-tuple-element.80), channel_id=1, source_target_pairs={{0,4},{2,6},{4,8},{6,10},{8,12},{10,14},{12,16},{14,18},{16,20},{1... | collective-permute-start | bytes 1572872 | tf_op jit(solution)/shard_map/ppermute | solution.py:291
  52.9 37.0 %collective-permute-start.13 = (bf16[16,64,256]{2,1,0:T(8,128)(2,1)S(1)}, bf16[16,64,256]{2,1,0:T(8,128)(2,1)S(1)}, u32[]{:S(2)}, u32[]{:S(2)}) collective-permute-start(bf16[16,64,256]{2,1,0:T(8,128)(2,1)S(1)} %get-tuple-element.85), channel_id=1, source_target_pairs={{0,4},{2,6},{4,8},{6,10},{8,12},{10,14},{12,16},{14,18},{16,20},{1... | collective-permute-start | bytes 1572872 | tf_op jit(solution)/shard_map/ppermute | solution.py:291
  76.6 13.3 %copy-start.7 = (f32[2048]{0:T(1024)S(1)}, f32[2048]{0:T(1024)}, u32[]{:S(2)}) copy-start(f32[2048]{0:T(1024)} %param.11) | copy-start | bytes 24580
  83.4 11.8 %collective-permute-start.12 = (bf16[128,512]{1,0:T(8,128)(2,1)S(1)}, bf16[128,512]{1,0:T(8,128)(2,1)S(1)}, u32[]{:S(2)}, u32[]{:S(2)}) collective-permute-start(bf16[128,512]{1,0:T(8,128)(2,1)S(1)} %add_convert_fusion.1), channel_id=1, source_target_pairs={{0,4},{2,6},{4,0},{6,2},{8,12},{10,14},{12,8},{14,10},{16,20},{18,... | collective-permute-start | bytes 393224 | tf_op jit(solution)/shard_map/ppermute | solution.py:233
  97.5 2.4 %collective-permute-start.14 = (bf16[32,64,128]{2,1,0:T(8,128)(2,1)}, bf16[32,64,128]{2,1,0:T(8,128)(2,1)S(1)}, u32[]{:S(2)}, u32[]{:S(2)}) collective-permute-start(bf16[32,64,128]{2,1,0:T(8,128)(2,1)} %get-tuple-element.92), channel_id=1, source_target_pairs={{0,2},{2,0},{4,6},{6,4},{8,10},{10,8},{12,14},{14,12},{16,18},{18,... | collective-permute-start | bytes 1572872 | tf_op jit(solution)/shard_map/ppermute | solution.py:416
  100.2 8.2 %collective-permute-start.17 = (bf16[16,32,128]{2,1,0:T(8,128)(2,1)S(1)}, bf16[16,32,128]{2,1,0:T(8,128)(2,1)S(1)}, u32[]{:S(2)}, u32[]{:S(2)}) collective-permute-start(bf16[16,32,128]{2,1,0:T(8,128)(2,1)S(1)} %dynamic-slice_convert_fusion), channel_id=1, source_target_pairs={{2,3},{3,2},{6,7},{7,6},{10,11},{11,10},{14,15},{15,14},{18,19},{1... | collective-permute-start | bytes 393224 | tf_op jit(solution)/shard_map/ppermute | solution.py:427
  103.4 5.0 %collective-permute-start.16 = (bf16[16,32,128]{2,1,0:T(8,128)(2,1)S(1)}, bf16[16,32,128]{2,1,0:T(8,128)(2,1)S(1)}, u32[]{:S(2)}, u32[]{:S(2)}) collective-permute-start(bf16[16,32,128]{2,1,0:T(8,128)(2,1)S(1)} %get-tuple-element.110), channel_id=1, source_target_pairs={{0,1},{1,0},{4,5},{5,4},{8,9},{9,8},{12,13},{13,12},{16,17},{17,16... | collective-permute-start | bytes 393224 | tf_op jit(solution)/shard_map/ppermute | solution.py:427
  103.5 5.7 %collective-permute-start.15 = (bf16[16,32,128]{2,1,0:T(8,128)(2,1)S(1)}, bf16[16,32,128]{2,1,0:T(8,128)(2,1)S(1)}, u32[]{:S(2)}, u32[]{:S(2)}) collective-permute-start(bf16[16,32,128]{2,1,0:T(8,128)(2,1)S(1)} %get-tuple-element.109), channel_id=1, source_target_pairs={{2,30},{3,31},{6,2},{7,3},{10,6},{11,7},{14,10},{15,11},{18,14},{1... | collective-permute-start | bytes 393224 | tf_op jit(solution)/shard_map/ppermute | solution.py:427
